TPU v7x, 32 devices: a whole 2x2x4 slice. The times are simulated.
32 devices in a mesh: section: 4 (over x, core), dp: 2 (over y), ctx: 4 (over z).
Axes of the slice: x: 2, y: 2, z: 4, core: 2. Of those that a mesh axis runs over, the one named last changes fastest.
Arguments:
- layer_input: bfloat16 [4, 2, 512, 4096], P('section', 'dp', 'ctx'), may hold values from -6 to 6
- attn_grad: bfloat16 [4, 2, 512, 4096], P('section', 'dp', 'ctx'), may hold values from -48 to 48
- queries: bfloat16 [4, 2, 512, 4096], P('section', 'dp', None, 'ctx'), may hold values from -6 to 6
- keys: bfloat16 [4, 2, 512, 512], P('section', 'dp', 'ctx'), may hold values from -6 to 6
- values: bfloat16 [4, 2, 512, 512], P('section', 'dp', 'ctx'), may hold values from -4 to 4
- kv_weight: bfloat16 [4, 4096, 1024], P('section', 'ctx'), may hold values from -0.09375 to 0.09375
- segments: int32 [2, 512], P('dp'), may hold values from 0 to 3, as said below
- positions: int32 [2, 512], P('dp'), may hold values from 0 to 16383, as said below
Outputs:
- grad_prev: bfloat16 [4, 2, 512, 4096], P('section', 'dp', 'ctx')
- query_grad: bfloat16 [4, 2, 512, 4096], P('section', 'dp', 'ctx')
- weight_grad: float32 [4, 4096, 1024], P('section', 'ctx', 'dp')
Inputs may be any that keep to these rules, and one draw needn't show every extreme that they name: `segments`: every sequence holds four documents: segment ids start at 0, never fall, and end at 3. Inside a segment positions rise by one a token.
All inputs are finite; a program needn't handle non-finite values.
Results may differ from a plain program's by a relative error of at most 0.012.
Values may be sent and summed in bfloat16 or wider, within the bound.
No kernel may reach another device: no remote copies, remote signals or barrier semaphores. Data moves between devices by JAX's collectives and lax.ppermute only.
A program may use at most 128 MiB of HBM per device.

v0:
```python
import math

import jax
import jax.numpy as jnp
import numpy as np
from jax import lax
from jax.sharding import PartitionSpec as P

QUERY_HEADS = 32
KEY_VALUE_HEADS = 4
HEAD_WIDTH = 128


def passed_along(value, axis, by):
    size = lax.axis_size(axis)
    pairs = [(i, i + by) for i in range(size) if 0 <= i + by < size]
    return lax.ppermute(value, axis, pairs)


def yarn_table(head_size):
    theta_base = 1000000.0
    factor = 4.0
    pretrain_len = 32768.0
    exponent = np.arange(0, head_size, 2) / head_size
    extrapolated = 1.0 / theta_base**exponent
    interpolated = extrapolated / factor

    def boundary(rotations):
        return (
            head_size
            * math.log(pretrain_len / (rotations * 2.0 * math.pi))
            / (2.0 * math.log(theta_base))
        )

    lower_dim = max(math.floor(boundary(32.0)), 0)
    upper_dim = min(math.ceil(boundary(1.0)), head_size - 1)
    ramp_width = max(upper_dim - lower_dim, 0.001)
    ramp_share = np.clip((np.arange(head_size // 2) - lower_dim) / ramp_width, 0.0, 1.0)
    keep_share = 1.0 - ramp_share
    frequency = interpolated * (1.0 - keep_share) + extrapolated * keep_share
    return (frequency.astype(np.float32), float(0.1 * math.log(factor) + 1.0))


def rotate_back(gradient, places, frequency, mscale):
    angles = places.astype(jnp.float32)[:, None] * frequency[None, :]
    cosine = jnp.cos(angles) * mscale
    sine_term = jnp.sin(angles) * mscale
    cosine = jnp.concatenate([cosine, cosine], -1)[:, None, :]
    sine_term = jnp.concatenate([sine_term, sine_term], -1)[:, None, :]
    half_size = gradient.shape[-1] // 2
    turned = jnp.concatenate([gradient[..., half_size:], -gradient[..., :half_size]], -1)
    return gradient * cosine + turned * sine_term


def attend_local(query_heads, key_heads, value_heads, grad_heads, seg_ids):
    sequence_length = query_heads.shape[0]
    local_heads = query_heads.shape[1] // HEAD_WIDTH
    kv_heads = key_heads.shape[1] // HEAD_WIDTH
    group_share_count = local_heads // kv_heads
    score_scale = HEAD_WIDTH ** (-0.5)
    query_complete = query_heads.reshape(sequence_length, kv_heads, group_share_count, HEAD_WIDTH)
    key_complete = key_heads.reshape(sequence_length, kv_heads, HEAD_WIDTH)
    value_complete = value_heads.reshape(sequence_length, kv_heads, HEAD_WIDTH)
    gradient_total = grad_heads.reshape(sequence_length, kv_heads, group_share_count, HEAD_WIDTH)
    block_rows = min(512, sequence_length)
    dq_parts = []
    key_gradient = jnp.zeros((sequence_length, kv_heads, HEAD_WIDTH), jnp.float32)
    value_gradient = jnp.zeros((sequence_length, kv_heads, HEAD_WIDTH), jnp.float32)
    for block_index in range(sequence_length // block_rows):
        row_start = block_index * block_rows
        row_stop = row_start + block_rows
        q_blk = query_complete[row_start:row_stop]
        k_blk = key_complete[:row_stop]
        v_blk = value_complete[:row_stop]
        g_blk = gradient_total[row_start:row_stop]
        scores = (
            jnp.einsum("qkgd,lkd->kgql", q_blk, k_blk, preferred_element_type=jnp.float32)
            * score_scale
        )
        row_ids = jnp.arange(row_start, row_stop)[:, None]
        col_ids = jnp.arange(row_stop)[None, :]
        allowed = (col_ids <= row_ids) & (
            seg_ids[row_start:row_stop][:, None] == seg_ids[:row_stop][None, :]
        )
        scores = jnp.where(allowed, scores, -1e30)
        row_max = jnp.max(scores, -1, keepdims=True)
        shifted = jnp.exp(scores - row_max)
        row_total = jnp.sum(shifted, -1, keepdims=True)
        attention = shifted / row_total
        probs_half = attention.astype(jnp.bfloat16)
        outputs = jnp.einsum(
            "kgql,lkd->qkgd", probs_half, v_blk, preferred_element_type=jnp.float32
        )
        row_delta = jnp.transpose(jnp.sum(g_blk.astype(jnp.float32) * outputs, -1), (1, 2, 0))[
            ..., None
        ]
        dprobs = jnp.einsum("qkgd,lkd->kgql", g_blk, v_blk, preferred_element_type=jnp.float32)
        dscore_half = (attention * (dprobs - row_delta)).astype(jnp.bfloat16)
        dq_parts.append(
            jnp.einsum("kgql,lkd->qkgd", dscore_half, k_blk, preferred_element_type=jnp.float32)
            * score_scale
        )
        key_gradient = key_gradient.at[:row_stop].add(
            jnp.einsum("kgql,qkgd->lkd", dscore_half, q_blk, preferred_element_type=jnp.float32)
            * score_scale
        )
        value_gradient = value_gradient.at[:row_stop].add(
            jnp.einsum("kgql,qkgd->lkd", probs_half, g_blk, preferred_element_type=jnp.float32)
        )
    query_grad = jnp.concatenate(dq_parts, 0).reshape(sequence_length, local_heads, HEAD_WIDTH)
    return (query_grad, key_gradient, value_gradient)


def on_device(layer_input, attn_grad, queries, keys, values, kv_weight, segments, positions):
    frequency, mscale = yarn_table(HEAD_WIDTH)
    inputs = layer_input[0, 0]
    output_gradient = attn_grad[0, 0]
    query_heads = queries[0, 0]
    key_row_block = keys[0, 0]
    value_row_block = values[0, 0]
    weight_rows = kv_weight[0]
    seg_ids = segments[0]
    places = positions[0]
    ctx_size = lax.axis_size("ctx")
    ctx_index = lax.axis_index("ctx")
    data_size = lax.axis_size("dp")
    sequence_length = query_heads.shape[0]
    kv_width = key_row_block.shape[1]
    kv_heads = kv_width // HEAD_WIDTH
    local_heads = query_heads.shape[1] // HEAD_WIDTH
    group_share_count = QUERY_HEADS // KEY_VALUE_HEADS
    kv_local = max(1, kv_heads // ctx_size)
    grad_heads = lax.all_to_all(output_gradient, "ctx", split_axis=1, concat_axis=0, tiled=True)
    key_complete, value_complete = (
        lax.all_gather(key_row_block, "ctx", axis=0, tiled=True),
        lax.all_gather(value_row_block, "ctx", axis=0, tiled=True),
    )
    first_col = ctx_index * local_heads // group_share_count * HEAD_WIDTH
    key_heads = lax.dynamic_slice_in_dim(key_complete, first_col, kv_local * HEAD_WIDTH, 1)
    value_heads = lax.dynamic_slice_in_dim(value_complete, first_col, kv_local * HEAD_WIDTH, 1)
    query_grad, key_gradient, value_gradient = attend_local(
        query_heads, key_heads, value_heads, grad_heads, seg_ids
    )
    query_back = (
        rotate_back(query_grad, places, frequency, mscale)
        .astype(jnp.bfloat16)
        .reshape(sequence_length, local_heads * HEAD_WIDTH)
    )
    query_out = lax.all_to_all(query_back, "ctx", split_axis=0, concat_axis=1, tiled=True)
    key_back = rotate_back(key_gradient, places, frequency, mscale).reshape(
        sequence_length, kv_local * HEAD_WIDTH
    )
    value_back = value_gradient.reshape(sequence_length, kv_local * HEAD_WIDTH)
    zeros_full = jnp.zeros((sequence_length, kv_width), jnp.float32)
    key_full = lax.dynamic_update_slice_in_dim(zeros_full, key_back, first_col, 1)
    value_full = lax.dynamic_update_slice_in_dim(zeros_full, value_back, first_col, 1)
    key_sum, value_sum = (
        lax.psum_scatter(key_full, "ctx", scatter_dimension=0, tiled=True),
        lax.psum_scatter(value_full, "ctx", scatter_dimension=0, tiled=True),
    )
    kv_grad = jnp.concatenate([key_sum, value_sum], 1).astype(jnp.bfloat16)
    input_cols = lax.all_to_all(inputs, "ctx", split_axis=1, concat_axis=0, tiled=True)
    gradient_total = lax.all_gather(kv_grad, "ctx", axis=0, tiled=True)
    rows_part = jnp.einsum(
        "td,tc->dc", input_cols, gradient_total, preferred_element_type=jnp.float32
    )
    cols_back = jnp.einsum(
        "tc,rc->tr", gradient_total, weight_rows, preferred_element_type=jnp.float32
    ).astype(jnp.bfloat16)
    back_rows = lax.all_to_all(cols_back, "ctx", split_axis=0, concat_axis=1, tiled=True)
    weight_grad = lax.psum_scatter(rows_part, "dp", scatter_dimension=1, tiled=True) / data_size
    grad_prev = passed_along(back_rows, "section", -1)
    return (grad_prev[None, None], query_out[None, None], weight_grad[None])


def solution(mesh):
    return jax.shard_map(
        on_device,
        mesh=mesh,
        in_specs=(
            P("section", "dp", "ctx", None),
            P("section", "dp", "ctx", None),
            P("section", "dp", None, "ctx"),
            P("section", "dp", "ctx", None),
            P("section", "dp", "ctx", None),
            P("section", "ctx", None),
            P("dp", None),
            P("dp", None),
        ),
        out_specs=(
            P("section", "dp", "ctx", None),
            P("section", "dp", "ctx", None),
            P("section", "ctx", "dp"),
        ),
        check_vma=False,
    )
```

profile of v0, /device:TPU:0, one launch (start us, length us, event | category | flops | bytes accessed | tf_op | source)
XLA Modules:
  0.0 270.1 jit_solution(15797264139231069279)
XLA Ops:
  7.2 2.0 all_to_all.50
  10.5 6.3 %all-to-all-start = ((bf16[128,4,1024]{2,0,1:T(8,128)(2,1)}), bf16[128,4,1024]{2,0,1:T(8,128)(2,1)S(1)}, u32[]{:S(2)}, u32[]{:S(2)}) async-start(bf16[128,4,1024]{2,0,1:T(8,128)(2,1)} %copy.78), calls=%async_computation | async-start | bytes 2097152 | tf_op jit(solution)/shard_map/all_to_all | solution.py:133
  16.8 2.3 copy.108
  19.1 34.3 %all-gather = bf16[1,1,512,512]{3,2,1,0:T(8,128)(2,1)} all-gather(bf16[1,1,128,512]{3,2,1,0:T(8,128)(2,1)S(1)} %copy-done.10), channel_id=2, replica_groups=mesh['section'=4,'dp'=2,'ctx'=4] {'ctx'}, dimensions={2}, use_global_device_ids=true | all-gather | bytes 655360 | tf_op jit(solution)/shard_map/all_gather | solution.py:135
  53.4 16.6 %all-gather.1 = bf16[1,1,512,512]{3,2,1,0:T(8,128)(2,1)} all-gather(bf16[1,1,128,512]{3,2,1,0:T(8,128)(2,1)S(1)} %copy-done.11), channel_id=3, replica_groups=mesh['section'=4,'dp'=2,'ctx'=4] {'ctx'}, dimensions={2}, use_global_device_ids=true | all-gather | bytes 655360 | tf_op jit(solution)/shard_map/all_gather | solution.py:136
  71.5 2.8 %fusion.4 = (f32[8,512]{1,0:T(8,128)S(1)}, f32[512,512,8]{1,0,2:T(8,128)S(1)}) fusion(pred[512,512]{0,1:T(8,128)(4,1)S(1)} %fusion.27, bf16[512,8,128]{0,2,1:T(8,128)(2,1)} %bitcast.156, bf16[1,1,512,512]{3,2,1,0:T(8,128)(2,1)} %all-gather, s32[]{:T(128)S(6)} %select_n.16), kind=kOutput, calls=%fused_computation.7 | convolution fusion | flops 543158272 | bytes 9846788 | tf_op jit(solution)/shard_map/qkgd,lkd->kgql/dot_general | solution.py:77
  74.4 3.3 %copy-done.1 = f32[512,512,8]{1,0,2:T(8,128)} copy-done((f32[512,512,8]{1,0,2:T(8,128)}, f32[512,512,8]{1,0,2:T(8,128)S(1)}, u32[]{:S(2)}) %copy-start.1) | copy-done | bytes 8388632
  77.6 2.4 fusion.3
  81.6 5.6 %fusion.22 = f32[512,512]{0,1:T(8,128)} fusion(f32[512,512]{0,1:T(8,128)} %broadcast_in_dim.18.clone, s32[]{:T(128)S(6)} %select_n.16, bf16[512,8,128]{2,1,0:T(8,128)(2,1)S(1)} %bitcast.163, f32[8,512]{1,0:T(8,128)} %fusion.3, f32[8,512]{1,0:T(8,128)S(1)} %get-tuple-element.69, f32[512,512,8]{1,0,2:T(8,128)} %copy-done.1, pred[512,512]{0,1:T(8,128)(4,1)S(1)} %fusion.27), kind=kOutput, calls=%fused_computation.26 | convolution fusion | flops 547356672 | bytes 9994244 | tf_op jit(solution)/shard_map/kgql,qkgd->lkd/dot_general | solution.py:108
  89.5 3.0 %copy.104 = f32[512,1,8,128]{0,3,2,1:T(8,128)} copy(f32[512,1,8,128]{3,2,0,1:T(8,128)} %bitcast.159) | data formatting | bytes 4194304 | tf_op jit(solution)/shard_map/convert_element_type | solution.py:94
  92.5 6.9 %fusion.11 = f32[512,8]{0,1:T(8,128)S(1)} fusion(f32[512,1,8,128]{0,3,2,1:T(8,128)} %copy.104, bf16[1,1,512,512]{3,2,1,0:T(8,128)(2,1)S(1)} %copy-done.7, s32[]{:T(128)S(6)} %select_n.16, f32[8,512]{1,0:T(8,128)S(1)} %copy-done.12, f32[8,512]{1,0:T(8,128)S(1)} %get-tuple-element.69, f32[512,512,8]{1,0,2:T(8,128)} %copy-done.1, pred[512,512]{0,1:T(8,128)(4,1)S(1)} %fusion.27), kind=kOutput, calls=%fused_computation.17 | convolution fusion | flops 548401152 | bytes 10928132 | tf_op jit(solution)/shard_map/kgql,lkd->qkgd/dot_general | solution.py:91
  99.4 5.5 %fusion.5 = bf16[8,512,512]{1,2,0:T(8,128)(2,1)S(1)} fusion(f32[8,512]{1,0:T(8,128)S(1)} %bitcast.168, f32[8,512]{1,0:T(8,128)S(1)} %copy-done.12, f32[8,512]{1,0:T(8,128)S(1)} %get-tuple-element.69, f32[512,512,8]{1,0,2:T(8,128)} %copy-done.1, pred[512,512]{0,1:T(8,128)(4,1)S(1)} %fusion.27, bf16[512,8,128]{2,1,0:T(8,128)(2,1)S(1)} %bitcast.164, ...), kind=kOutput, calls=%fused_computation.8 | convolution fusion | flops 551550976 | bytes 14073860 | tf_op jit(solution)/shard_map/qkgd,lkd->kgql/dot_general | solution.py:97
  107.9 2.3 copy.94
  110.2 3.8 %all-to-all-start.3 = ((bf16[128,4,1024]{0,2,1:T(8,128)(2,1)}), bf16[128,4,1024]{0,2,1:T(8,128)(2,1)S(1)}, u32[]{:S(2)}, u32[]{:S(2)}) async-start(bf16[128,4,1024]{0,2,1:T(8,128)(2,1)} %bitcast.161), calls=%async_computation.5 | async-start | bytes 2097152 | tf_op jit(solution)/shard_map/all_to_all | solution.py:162
  116.6 34.8 %reduce-scatter.4.cloned.1.call-done = f32[128,512]{0,1:T(8,128)} async-done(((f32[512,512]{0,1:T(8,128)}), f32[128,512]{0,1:T(8,128)}) %reduce-scatter.4.cloned.1.call-update) | async-done | bytes 262160 | tf_op jit(solution)/shard_map/reduce_scatter | solution.py:158
  155.4 29.2 %all-gather.4.cloned.1.call-done = bf16[512,1024]{0,1:T(8,128)(2,1)} async-done(((bf16[128,1024]{0,1:T(8,128)(2,1)}), bf16[512,1024]{0,1:T(8,128)(2,1)}) %all-gather.4.cloned.1.call-update) | async-done | bytes 1048592 | tf_op jit(solution)/shard_map/all_gather | solution.py:163
  184.5 4.7 %convolution_bitcast_fusion = f32[1024,1024]{0,1:T(8,128)} fusion(bf16[512,1024]{0,1:T(8,128)(2,1)} %all-gather.4.cloned.1.call-done, bf16[512,1024]{1,0:T(8,128)(2,1)} %bitcast.165), kind=kOutput, calls=%fused_computation.14 | convolution fusion | flops 1073741824 | bytes 6291456 | tf_op jit(solution)/shard_map/td,tc->dc/dot_general | solution.py:164
  190.5 2.3 fusion.16
  192.8 4.5 %all-to-all-start.1 = ((bf16[4,128,1024]{2,1,0:T(8,128)(2,1)}), bf16[4,128,1024]{2,1,0:T(8,128)(2,1)}, u32[]{:S(2)}, u32[]{:S(2)}) async-start(bf16[4,128,1024]{2,1,0:T(8,128)(2,1)} %bitcast.30), calls=%async_computation.3 | async-start | bytes 2097152 | tf_op jit(solution)/shard_map/all_to_all | solution.py:170
  197.3 4.4 %multiply_bitcast_fusion.2 = (f32[512,1,8,128]{0,3,2,1:T(8,128)}, f32[512,8,128]{0,2,1:T(8,128)S(1)}) fusion(bf16[8,512,512]{1,2,0:T(8,128)(2,1)} %copy-done.2, bf16[1,1,512,512]{3,2,1,0:T(8,128)(2,1)} %all-gather, s32[]{:T(128)S(6)} %select_n.16), kind=kOutput, calls=%fused_computation.23 | convolution fusion | flops 537395200 | bytes 8519684 | tf_op jit(solution)/shard_map/kgql,lkd->qkgd/dot_general | solution.py:100
  203.5 3.0 %mul.183 = f32[4,128,1024]{1,0,2:T(4,128)} reshape(f32[512,8,128]{0,2,1:T(8,128)} %maximum_multiply_fusion) | data formatting | bytes 4194304 | tf_op jit(solution)/shard_map/mul | solution.py:52
  206.5 2.9 %copy.92 = f32[4,128,1024]{2,1,0:T(8,128)} copy(f32[4,128,1024]{1,0,2:T(4,128)} %mul.183) | data formatting | bytes 4194304 | tf_op jit(solution)/shard_map/mul | solution.py:52
  209.5 3.0 %reshape.284 = f32[4,128,1024]{1,0,2:T(4,128)} reshape(f32[512,1,8,128]{0,3,2,1:T(8,128)} %get-tuple-element.58) | data formatting | bytes 4194304 | tf_op jit(solution)/shard_map/reshape | solution.py:110
  212.5 2.9 %copy.91 = f32[4,128,1024]{2,1,0:T(8,128)} copy(f32[4,128,1024]{1,0,2:T(4,128)} %reshape.284) | data formatting | bytes 4194304 | tf_op jit(solution)/shard_map/reshape | solution.py:110
  217.0 2.8 %mul.178 = f32[4,128,1024]{2,1,0:T(8,128)} reshape(f32[512,8,128]{2,1,0:T(8,128)} %mul.177) | data formatting | bytes 4194304 | tf_op jit(solution)/shard_map/mul | solution.py:52
  219.8 3.5 %add_convert_fusion = bf16[4,128,1024]{2,1,0:T(8,128)(2,1)S(1)} fusion(f32[4,128,1024]{2,1,0:T(8,128)} %copy.92, f32[4,128,1024]{2,1,0:T(8,128)} %copy.91, f32[4,128,1024]{2,1,0:T(8,128)} %mul.178), kind=kLoop, calls=%fused_computation.21 | loop fusion | flops 1572864 | bytes 7340032 | tf_op jit(solution)/shard_map/convert_element_type | solution.py:146
  224.5 4.8 %all-to-all-start.2 = ((bf16[4,128,1024]{1,2,0:T(8,128)(2,1)}), bf16[4,128,1024]{1,2,0:T(8,128)(2,1)S(1)}, u32[]{:S(2)}, u32[]{:S(2)}) async-start(bf16[4,128,1024]{1,2,0:T(8,128)(2,1)} %copy.93), calls=%async_computation.4 | async-start | bytes 2097152 | tf_op jit(solution)/shard_map/all_to_all | solution.py:149
  229.3 2.3 copy.109
  232.9 21.0 %all-to-all-done.2 = bf16[4,128,1024]{1,2,0:T(8,128)(2,1)S(1)} async-done(((bf16[4,128,1024]{1,2,0:T(8,128)(2,1)}), bf16[4,128,1024]{1,2,0:T(8,128)(2,1)S(1)}, u32[]{:S(2)}, u32[]{:S(2)}) %all-to-all-start.2) | async-done | bytes 1048608 | tf_op jit(solution)/shard_map/all_to_all | solution.py:149
  255.2 3.2 %multiply_bitcast_fusion = f32[1,1024,512]{1,2,0:T(8,128)} fusion(f32[1024,512]{0,1:T(8,128)} %reduce-scatter.8.cloned.1.call-done), kind=kLoop, calls=%fused_computation.20 | loop fusion | flops 524288 | bytes 4194304 | tf_op jit(solution)/shard_map/broadcast_in_dim | solution.py:173
  258.4 2.9 %copy.97 = f32[1,1024,512]{2,1,0:T(8,128)} copy(f32[1,1024,512]{1,2,0:T(8,128)} %multiply_bitcast_fusion) | data formatting | bytes 4194304
  261.3 2.3 copy.119
  (71 shorter events, 24.8 us)
Async XLA Ops:
  7.2 182.1 %copy-start = (bf16[1,1024,1024]{2,1,0:T(8,128)(2,1)S(1)}, bf16[1,1024,1024]{2,1,0:T(8,128)(2,1)}, u32[]{:S(2)}) copy-start(bf16[1,1024,1024]{2,1,0:T(8,128)(2,1)} %param.23) | copy-start | bytes 6291460
  7.2 11.9 %copy-start.10 = (bf16[1,1,128,512]{3,2,1,0:T(8,128)(2,1)S(1)}, bf16[1,1,128,512]{3,2,1,0:T(8,128)(2,1)}, u32[]{:S(2)}) copy-start(bf16[1,1,128,512]{3,2,1,0:T(8,128)(2,1)} %param.21) | copy-start | bytes 393220
  7.2 46.2 %copy-start.14 = (s32[1,512]{1,0:T(1,128)S(1)}, s32[1,512]{1,0:T(1,128)}, u32[]{:S(2)}) copy-start(s32[1,512]{1,0:T(1,128)} %param.25) | copy-start | bytes 6148
  7.2 46.2 %copy-start.11 = (bf16[1,1,128,512]{3,2,1,0:T(8,128)(2,1)S(1)}, bf16[1,1,128,512]{3,2,1,0:T(8,128)(2,1)}, u32[]{:S(2)}) copy-start(bf16[1,1,128,512]{3,2,1,0:T(8,128)(2,1)} %param.22) | copy-start | bytes 393220
  9.2 60.8 %copy-start.15 = (f32[64]{0:T(128)S(1)}, f32[64]{0:T(128)}, u32[]{:S(2)}) copy-start(f32[64]{0:T(128)} %constant.120) | copy-start | bytes 772
  9.2 62.1 %copy-start.13 = (s32[1,512]{1,0:T(1,128)S(1)}, s32[1,512]{1,0:T(1,128)}, u32[]{:S(2)}) copy-start(s32[1,512]{1,0:T(1,128)} %param.24) | copy-start | bytes 6148
  10.5 69.5 %all-to-all-start = ((bf16[128,4,1024]{2,0,1:T(8,128)(2,1)}), bf16[128,4,1024]{2,0,1:T(8,128)(2,1)S(1)}, u32[]{:S(2)}, u32[]{:S(2)}) async-start(bf16[128,4,1024]{2,0,1:T(8,128)(2,1)} %copy.78), calls=%async_computation | async-start | bytes 2097152 | tf_op jit(solution)/shard_map/all_to_all | solution.py:133
  16.8 98.1 %reduce-scatter.6.cloned.1.call-start = ((), (), s32[]{:S(2)}) async-start(), calls=%async_computation.8 | async-start | bytes 1310720 | tf_op jit(solution)/shard_map/reduce_scatter | solution.py:159
  74.4 3.3 %copy-start.1 = (f32[512,512,8]{1,0,2:T(8,128)}, f32[512,512,8]{1,0,2:T(8,128)S(1)}, u32[]{:S(2)}) copy-start(f32[512,512,8]{1,0,2:T(8,128)S(1)} %get-tuple-element.70) | copy-start | bytes 25165828
  80.3 1.3 copy-start.5
  87.3 64.1 %reduce-scatter.4.cloned.1.call-start = ((), (), s32[]{:S(2)}) async-start(), calls=%async_computation.7 | async-start | bytes 1310720 | tf_op jit(solution)/shard_map/reduce_scatter | solution.py:158
  87.7 4.8 %copy-start.7 = (bf16[1,1,512,512]{3,2,1,0:T(8,128)(2,1)S(1)}, bf16[1,1,512,512]{3,2,1,0:T(8,128)(2,1)}, u32[]{:S(2)}) copy-start(bf16[1,1,512,512]{3,2,1,0:T(8,128)(2,1)} %all-gather.1) | copy-start | bytes 1572868
  87.7 4.8 %copy-start.12 = (f32[8,512]{1,0:T(8,128)S(1)}, f32[8,512]{1,0:T(8,128)}, u32[]{:S(2)}) copy-start(f32[8,512]{1,0:T(8,128)} %fusion.3) | copy-start | bytes 49156
  92.5 6.9 %copy-start.6 = (bf16[64,8,8,128]{3,2,1,0:T(8,128)(2,1)S(1)}, bf16[64,8,8,128]{3,2,1,0:T(8,128)(2,1)}, u32[]{:S(2)}) copy-start(bf16[64,8,8,128]{3,2,1,0:T(8,128)(2,1)} %copy-done.5) | copy-start | bytes 3145732
  99.4 5.5 %copy-start.3 = (bf16[1,1,512,1024]{2,3,1,0:T(8,128)(2,1)S(1)}, bf16[1,1,512,1024]{2,3,1,0:T(8,128)(2,1)}, u32[]{:S(2)}) copy-start(bf16[1,1,512,1024]{2,3,1,0:T(8,128)(2,1)} %copy.108) | copy-start | bytes 3145732
  104.9 2.0 copy-start.2
  104.9 1.6 copy-start.8
  104.9 1.6 copy-start.9
  106.9 1.0 copy-start.4
  110.2 43.9 %all-to-all-start.3 = ((bf16[128,4,1024]{0,2,1:T(8,128)(2,1)}), bf16[128,4,1024]{0,2,1:T(8,128)(2,1)S(1)}, u32[]{:S(2)}, u32[]{:S(2)}) async-start(bf16[128,4,1024]{0,2,1:T(8,128)(2,1)} %bitcast.161), calls=%async_computation.5 | async-start | bytes 2097152 | tf_op jit(solution)/shard_map/all_to_all | solution.py:162
  114.0 70.5 %all-gather.4.cloned.1.call-start = ((), (), s32[]{:S(2)}) async-start(), calls=%async_computation.9 | async-start | bytes 1310720 | tf_op jit(solution)/shard_map/all_gather | solution.py:163
  154.0 101.2 %reduce-scatter.8.cloned.1.call-start = ((), (), s32[]{:S(2)}) async-start(), calls=%async_computation.10 | async-start | bytes 6291456 | tf_op jit(solution)/shard_map/reduce_scatter | solution.py:171
  189.3 1.2 copy-start.16
  192.8 31.8 %all-to-all-start.1 = ((bf16[4,128,1024]{2,1,0:T(8,128)(2,1)}), bf16[4,128,1024]{2,1,0:T(8,128)(2,1)}, u32[]{:S(2)}, u32[]{:S(2)}) async-start(bf16[4,128,1024]{2,1,0:T(8,128)(2,1)} %bitcast.30), calls=%async_computation.3 | async-start | bytes 2097152 | tf_op jit(solution)/shard_map/all_to_all | solution.py:170
  224.5 29.3 %all-to-all-start.2 = ((bf16[4,128,1024]{1,2,0:T(8,128)(2,1)}), bf16[4,128,1024]{1,2,0:T(8,128)(2,1)S(1)}, u32[]{:S(2)}, u32[]{:S(2)}) async-start(bf16[4,128,1024]{1,2,0:T(8,128)(2,1)} %copy.93), calls=%async_computation.4 | async-start | bytes 2097152 | tf_op jit(solution)/shard_map/all_to_all | solution.py:149
  231.6 23.6 %collective-permute-start = (bf16[128,4096]{1,0:T(8,128)(2,1)}, bf16[128,4096]{1,0:T(8,128)(2,1)}, u32[]{:S(2)}, u32[]{:S(2)}) collective-permute-start(bf16[128,4096]{1,0:T(8,128)(2,1)} %bitcast.56), channel_id=1, source_target_pairs={{8,0},{16,8},{24,16},{9,1},{17,9},{25,17},{10,2},{18,10},{26,18},{... | collective-permute-start | bytes 3145736 | tf_op jit(solution)/shard_map/ppermute | solution.py:17
Sparse Core Ops, SparseCore 0:
  87.4 27.5 reduce-scatter.5
  117.9 33.3 reduce-scatter.3
  154.1 30.3 all-gather.3
  189.4 52.6 reduce-scatter.7
where the time goes:
time: 271 us; the launch traced here: 270 us
  waiting for transfers between devices  85.9 us (32%)
  blocking collectives  50.9 us (19%)
  local copies, waits for them, and re-layouts  47.6 us (18%)
  matrix products  33.6 us (12%)
  starting transfers between devices  20.9 us (8%)
  other arithmetic  17 us (6%)
  between operations  14.1 us (5%)
    reduce_scatter x1, waiting for transfers between devices, on_device(): lax.psum_scatter(key_full, 'ctx', scatter_dimension=0, tiled=True)  34.8 us
    all_gather x1, blocking collectives, on_device(): lax.all_gather(key_row_block, 'ctx', axis=0, tiled=True)  34.3 us
    all_gather x1, waiting for transfers between devices, on_device(): gradient_total = lax.all_gather(kv_grad, 'ctx', axis=0, tiled=True)  29.2 us
    all_to_all x1, waiting for transfers between devices, on_device(): lax.all_to_all(query_back, 'ctx', split_axis=0, concat_axis=1, tiled=True)  21 us
    unnamed x40, local copies, waits for them, and re-layouts  16.7 us
    all_gather x1, blocking collectives, on_device(): lax.all_gather(value_row_block, 'ctx', axis=0, tiled=True)  16.6 us
    mul x4, local copies, waits for them, and re-layouts, rotate_back(): return gradient * cosine + turned * sine_term  10.2 us
    dot_general x1, matrix products, attend_local(): jnp.einsum('kgql,lkd->qkgd', probs_half, v_blk, preferred_element_type=jn...  6.9 us
  transfers between devices with their start and end apart: 9, of which 4 were waited for; matrix products, arithmetic and copies ran while one was open for 25% of the time, Pallas kernels for 0%

commit v1 on v0

v1 whole, which is shorter than its diff:
```python
import functools
import math

import jax
import jax.numpy as jnp
import numpy as np
from jax import lax
from jax.experimental import pallas as pl
from jax.experimental.pallas import tpu as pltpu
from jax.sharding import PartitionSpec as P

QUERY_HEADS = 32
KEY_VALUE_HEADS = 4
HEAD_WIDTH = 128
QUERY_BLOCK = 256
MASKED = -1e30


def yarn_table(head_size):
    theta_base = 1000000.0
    factor = 4.0
    pretrain_len = 32768.0
    exponent = np.arange(0, head_size, 2) / head_size
    extrapolated = 1.0 / theta_base**exponent
    interpolated = extrapolated / factor

    def boundary(rotations):
        return (
            head_size
            * math.log(pretrain_len / (rotations * 2.0 * math.pi))
            / (2.0 * math.log(theta_base))
        )

    lower_dim = max(math.floor(boundary(32.0)), 0)
    upper_dim = min(math.ceil(boundary(1.0)), head_size - 1)
    ramp_width = max(upper_dim - lower_dim, 0.001)
    ramp_share = np.clip((np.arange(head_size // 2) - lower_dim) / ramp_width, 0.0, 1.0)
    keep_share = 1.0 - ramp_share
    frequency = interpolated * (1.0 - keep_share) + extrapolated * keep_share
    return (frequency.astype(np.float32), float(0.1 * math.log(factor) + 1.0))


def dot(a, b, dims):
    return lax.dot_general(a, b, (dims, ((), ())), preferred_element_type=jnp.float32)


NT = ((1,), (1,))
NN = ((1,), (0,))
TN = ((0,), (0,))
VMEM_LIMIT = 48 * 1024 * 1024


def rows_at(pos_ref, piece, count):
    return pl.ds(pl.multiple_of(pos_ref[piece] * count, count), count)


def attention_kernel(n, pos_ref, *refs):
    g_refs, kv_refs, refs = refs[:n], refs[n : 2 * n], refs[2 * n :]
    q_ref, seg_ref, cos_ref, sin_ref = refs[:4]
    dq_refs, dkv_ref = refs[4 : 4 + n], refs[4 + n]
    k_s, v_s, kt_s, bias_s, g_s, dq_s, dk_s, dv_s = refs[5 + n :]
    tokens = q_ref.shape[0]
    piece_rows = tokens // n
    width = HEAD_WIDTH
    half = width // 2
    block = min(QUERY_BLOCK, tokens)
    scale = HEAD_WIDTH ** (-0.5)
    head = pl.program_id(0)

    @pl.when(head == 0)
    def _():
        for m in range(n):
            rows = rows_at(pos_ref, m, piece_rows)
            k_s[rows, :] = kv_refs[m][:, :width]
            v_s[rows, :] = kv_refs[m][:, width:]
        kt_s[...] = k_s[...].astype(jnp.float32).T.astype(jnp.bfloat16)
        seg_row = seg_ref[...].astype(jnp.float32)
        seg_col = jnp.broadcast_to(seg_row, (width, tokens)).T
        for start in range(0, tokens, width):
            q_seg = seg_row[:, start : start + width]
            key_id = lax.broadcasted_iota(jnp.int32, (tokens, width), 0)
            query_id = start + lax.broadcasted_iota(jnp.int32, (tokens, width), 1)
            allowed = (seg_col == q_seg) & (key_id <= query_id)
            bias_s[:, start : start + width] = jnp.where(allowed, 0.0, MASKED)
        dk_s[...] = jnp.zeros_like(dk_s)
        dv_s[...] = jnp.zeros_like(dv_s)

    for m in range(n):
        g_s[rows_at(pos_ref, m, piece_rows), :] = g_refs[m][...]

    for start in range(0, tokens, block):
        stop = start + block
        q = q_ref[start:stop, :]
        g = g_s[start:stop, :]
        scores = dot(k_s[:stop, :], q, NT) * scale + bias_s[:stop, start:stop]
        top = jnp.max(scores, 0, keepdims=True)
        shifted = jnp.exp(scores - top)
        total = jnp.sum(shifted, 0, keepdims=True)
        attention = shifted * (1.0 / total)
        dprobs = dot(v_s[:stop, :], g, NT)
        delta = jnp.sum(attention * dprobs, 0, keepdims=True)
        dscores = (attention * (dprobs - delta)).astype(jnp.bfloat16)
        dv_s[:stop, :] += dot(attention.astype(jnp.bfloat16), g, NN)
        dk_s[:stop, :] += dot(dscores, q, NN)
        dq = dot(kt_s[:, :stop], dscores, NN)
        c = cos_ref[:, start:stop]
        t = sin_ref[:, start:stop]
        u, w = dq[:half], dq[half:]
        turned = jnp.concatenate([u * c + w * t, w * c - u * t], 0)
        dq_s[start:stop, :] = turned.T.astype(jnp.bfloat16)
    for m in range(n):
        dq_refs[m][...] = dq_s[rows_at(pos_ref, m, piece_rows), :]

    @pl.when(head == pl.num_programs(0) - 1)
    def _():
        dk = dk_s[...].T
        c = cos_ref[...]
        t = sin_ref[...]
        u, w = dk[:half], dk[half:]
        turned = jnp.concatenate([u * c + w * t, w * c - u * t], 0)
        dkv_ref[:, :width] = turned.T.astype(jnp.bfloat16)
        dkv_ref[:, width:] = dv_s[...].astype(jnp.bfloat16)


def attention_backward(pos, pieces, queries, segments, cosine, sine):
    n = len(pieces)
    tokens, cols = queries.shape
    width = HEAD_WIDTH
    heads = cols // width
    piece_rows = tokens // n
    bf16, f32 = jnp.bfloat16, jnp.float32
    out = pl.pallas_call(
        functools.partial(attention_kernel, n),
        out_shape=[jax.ShapeDtypeStruct((piece_rows, cols), bf16)] * n
        + [jax.ShapeDtypeStruct((tokens, 2 * width), bf16)],
        grid_spec=pltpu.PrefetchScalarGridSpec(
            num_scalar_prefetch=1,
            grid=(heads,),
            in_specs=[pl.BlockSpec((piece_rows, width), lambda h, p: (0, h))] * n
            + [pl.BlockSpec((piece_rows, 2 * width), lambda h, p: (0, cols // (2 * width)))] * n
            + [
                pl.BlockSpec((tokens, width), lambda h, p: (0, h)),
                pl.BlockSpec((1, tokens), lambda h, p: (0, 0)),
                pl.BlockSpec((width // 2, tokens), lambda h, p: (0, 0)),
                pl.BlockSpec((width // 2, tokens), lambda h, p: (0, 0)),
            ],
            out_specs=[pl.BlockSpec((piece_rows, width), lambda h, p: (0, h))] * n
            + [pl.BlockSpec((tokens, 2 * width), lambda h, p: (0, 0))],
            scratch_shapes=[
                pltpu.VMEM((tokens, width), bf16),
                pltpu.VMEM((tokens, width), bf16),
                pltpu.VMEM((width, tokens), bf16),
                pltpu.VMEM((tokens, tokens), f32),
                pltpu.VMEM((tokens, width), bf16),
                pltpu.VMEM((tokens, width), bf16),
                pltpu.VMEM((tokens, width), f32),
                pltpu.VMEM((tokens, width), f32),
            ],
        ),
        compiler_params=pltpu.CompilerParams(
            dimension_semantics=("arbitrary",), vmem_limit_bytes=VMEM_LIMIT
        ),
        cost_estimate=pl.CostEstimate(
            flops=10 * heads * tokens * tokens * width,
            bytes_accessed=6 * tokens * cols,
            transcendentals=heads * tokens * tokens,
        ),
        name="attention_backward",
    )(pos, *pieces, *pieces, queries, segments, cosine, sine)
    return out[:n], out[n]


def input_kernel(n, share, pos_ref, *refs):
    part_refs, weight_ref = refs[:n], refs[n]
    out_refs, kv_ref = refs[n + 1 : 2 * n + 1], refs[2 * n + 1]
    total = refs[2 * n + 2] if share > 1 else None
    width = HEAD_WIDTH
    kv_width = kv_ref.shape[1] // 2
    piece_rows = out_refs[0].shape[0]
    if share > 1:
        total[...] = jnp.zeros_like(total)
    for m in range(n):
        head = pos_ref[m] // share
        for side in range(2):
            cols = pl.ds(pl.multiple_of(side * kv_width + head * width, width), width)
            part = part_refs[m][:, side * width : (side + 1) * width]
            if share > 1:
                total[:, cols] += part.astype(jnp.float32)
            else:
                kv_ref[:, cols] = part
    if share > 1:
        kv_ref[...] = total[...].astype(kv_ref.dtype)
    for m in range(n):
        rows = kv_ref[rows_at(pos_ref, m, piece_rows), :]
        out_refs[m][...] = dot(rows, weight_ref[...], NT).astype(jnp.bfloat16)


def input_gradient(pos, parts, weight, share):
    n = len(parts)
    tokens = parts[0].shape[0]
    rows, cols = weight.shape
    bf16 = jnp.bfloat16
    vmem = pl.BlockSpec(memory_space=pltpu.VMEM)
    out = pl.pallas_call(
        functools.partial(input_kernel, n, share),
        out_shape=[jax.ShapeDtypeStruct((tokens // n, rows), bf16)] * n
        + [jax.ShapeDtypeStruct((tokens, cols), bf16)],
        in_specs=[pl.BlockSpec(memory_space=pltpu.SMEM)] + [vmem] * (n + 1),
        out_specs=[vmem] * (n + 1),
        scratch_shapes=[pltpu.VMEM((tokens, cols), jnp.float32)] if share > 1 else [],
        compiler_params=pltpu.CompilerParams(vmem_limit_bytes=VMEM_LIMIT),
        cost_estimate=pl.CostEstimate(
            flops=2 * tokens * rows * cols,
            bytes_accessed=2 * (2 * tokens * cols + rows * cols + tokens * rows),
            transcendentals=0,
        ),
        name="input_gradient",
    )(pos, *parts, weight)
    return out[:n], out[n]


def weight_kernel(n, halves, pos_ref, *refs):
    x_refs, kv_ref = refs[:n], refs[n]
    out_refs, x_s = refs[n + 1 : -1], refs[-1]
    piece_rows = x_refs[0].shape[0]
    for m in range(n):
        x_s[rows_at(pos_ref, m, piece_rows), :] = x_refs[m][...]
    if halves:
        cols = kv_ref.shape[1] // 2
        mine = pos_ref[n]
        for out_ref, side in zip(out_refs, (1 - mine, mine)):
            picked = kv_ref[:, pl.ds(pl.multiple_of(side * cols, cols), cols)]
            out_ref[...] = dot(x_s[...], picked, TN).astype(out_ref.dtype)
    else:
        out_refs[0][...] = dot(x_s[...], kv_ref[...], TN)


def weight_gradient(pos, pieces, kv_grad, halves):
    n = len(pieces)
    rows = pieces[0].shape[1]
    tokens, cols = kv_grad.shape
    vmem = pl.BlockSpec(memory_space=pltpu.VMEM)
    if halves:
        out_shape = [
            jax.ShapeDtypeStruct((rows, cols // 2), jnp.bfloat16),
            jax.ShapeDtypeStruct((rows, cols // 2), jnp.float32),
        ]
    else:
        out_shape = [jax.ShapeDtypeStruct((rows, cols), jnp.float32)]
    return pl.pallas_call(
        functools.partial(weight_kernel, n, halves),
        out_shape=out_shape,
        in_specs=[pl.BlockSpec(memory_space=pltpu.SMEM)] + [vmem] * (n + 1),
        out_specs=[vmem] * len(out_shape),
        scratch_shapes=[pltpu.VMEM((tokens, rows), jnp.bfloat16)],
        compiler_params=pltpu.CompilerParams(vmem_limit_bytes=VMEM_LIMIT),
        cost_estimate=pl.CostEstimate(
            flops=2 * tokens * rows * cols,
            bytes_accessed=2 * tokens * (rows + cols) + 4 * rows * cols,
            transcendentals=0,
        ),
        name="weight_gradient",
    )(pos, *pieces, kv_grad)


def join_kernel(n, pos_ref, *refs):
    out_ref = refs[n]
    cols = refs[0].shape[1]
    for m in range(n):
        at = pl.ds(pl.multiple_of(pos_ref[m] * cols, cols), cols)
        out_ref[:, at] = refs[m][...]


def join_columns(pos, pieces):
    n = len(pieces)
    rows, cols = pieces[0].shape
    vmem = pl.BlockSpec(memory_space=pltpu.VMEM)
    return pl.pallas_call(
        functools.partial(join_kernel, n),
        out_shape=jax.ShapeDtypeStruct((rows, n * cols), pieces[0].dtype),
        in_specs=[pl.BlockSpec(memory_space=pltpu.SMEM)] + [vmem] * n,
        out_specs=vmem,
        compiler_params=pltpu.CompilerParams(vmem_limit_bytes=VMEM_LIMIT),
        cost_estimate=pl.CostEstimate(
            flops=0, bytes_accessed=4 * rows * n * cols, transcendentals=0
        ),
        name="join_columns",
    )(pos, *pieces)


def swapped(value, mask, axis="ctx"):
    size = lax.axis_size(axis)
    return lax.ppermute(value, axis, [(i, i ^ mask) for i in range(size)])


def to_section_before(value, mask):
    sections, size = lax.axis_size("section"), lax.axis_size("ctx")
    pairs = [
        (s * size + i, (s - 1) * size + (i ^ mask)) for s in range(1, sections) for i in range(size)
    ]
    return lax.ppermute(value, ("section", "ctx"), pairs)


def after(values, others):
    return lax.optimization_barrier((values, others))[0]


def on_device(layer_input, attn_grad, queries, keys, values, kv_weight, segments, positions):
    frequency, mscale = yarn_table(HEAD_WIDTH)
    width = HEAD_WIDTH
    inputs, grads = layer_input[0, 0], attn_grad[0, 0]
    key_rows, value_rows = keys[0, 0], values[0, 0]
    n = lax.axis_size("ctx")
    me = lax.axis_index("ctx")
    data_size = lax.axis_size("dp")
    tokens, cols = queries.shape[2:]
    kv_heads = key_rows.shape[1] // width
    share = n // kv_heads
    masks = list(range(1, n))[::-1]
    block_of = [me ^ m for m in range(n)]
    pos = jnp.stack([*block_of, lax.axis_index("dp")]).astype(jnp.int32)

    def block(array, at, size):
        return lax.dynamic_slice_in_dim(array, at * size, size, 1)

    def outgoing(m):
        head = block_of[m] // share
        return jnp.concatenate(
            [
                block(grads, block_of[m], cols),
                block(key_rows, head, width),
                block(value_rows, head, width),
            ],
            1,
        )

    sent = {m: swapped(outgoing(m), m) for m in masks}
    pieces = [outgoing(0), *(sent[m] for m in range(1, n))]

    angles = frequency[:, None] * positions.astype(jnp.float32)
    score_scale = width ** (-0.5)
    cosine = jnp.cos(angles) * (mscale * score_scale)
    sine = jnp.sin(angles) * (mscale * score_scale)

    features = inputs.shape[1] // n
    x_out = [block(inputs, block_of[m], features) for m in range(n)]
    x_held = after(x_out, pieces)
    x_sent = {m: swapped(x_held[m], m) for m in masks}
    x_pieces = [x_out[0], *(x_sent[m] for m in range(1, n))]

    dq_pieces, dkv = attention_backward(pos, pieces, queries[0, 0], segments, cosine, sine)

    parts = {0: dkv}
    bit = n // 2
    while bit:
        for m in sorted(parts):
            parts[m | bit] = swapped(parts[m], bit)
        bit //= 2
    parts = [parts[m] for m in range(n)]

    in_grads, kv_grad = input_gradient(pos, parts, kv_weight[0], share)
    in_sent = {m: to_section_before(in_grads[m], m) for m in [*masks, 0]}
    dq_held = after(dq_pieces, parts)
    dq_sent = {m: swapped(dq_held[m], m) for m in masks}

    halves = data_size == 2
    if halves:
        away, home = weight_gradient(pos, x_pieces, kv_grad, True)
        weight_grad = (home + swapped(away, 1, "dp").astype(jnp.float32)) / data_size
    else:
        (rows_part,) = weight_gradient(pos, x_pieces, kv_grad, False)
        weight_grad = lax.psum_scatter(rows_part, "dp", scatter_dimension=1, tiled=True) / data_size

    grad_prev = join_columns(pos, [in_sent[m] for m in range(n)])
    query_grad = join_columns(pos, [dq_pieces[0], *(dq_sent[m] for m in range(1, n))])
    return (grad_prev[None, None], query_grad[None, None], weight_grad[None])


def solution(mesh):
    return jax.shard_map(
        on_device,
        mesh=mesh,
        in_specs=(
            P("section", "dp", "ctx", None),
            P("section", "dp", "ctx", None),
            P("section", "dp", None, "ctx"),
            P("section", "dp", "ctx", None),
            P("section", "dp", "ctx", None),
            P("section", "ctx", None),
            P("dp", None),
            P("dp", None),
        ),
        out_specs=(
            P("section", "dp", "ctx", None),
            P("section", "dp", "ctx", None),
            P("section", "ctx", "dp"),
        ),
        check_vma=False,
    )
```

time: 271 us -> 143 us (0.53)
  the two profiles are of different devices: /device:TPU:0 before, /device:TPU:9 now
where the time goes in v1:
time: 143 us
  waiting for transfers between devices  69.1 us (48%)
  starting transfers between devices  46.1 us (32%)
  Pallas kernels  21.4 us (15%)
  other arithmetic  3.07 us (2%)
  local copies, waits for them, and re-layouts  2.22 us (2%)
    ppermute x13, waiting for transfers between devices, swapped(): return lax.ppermute(value, axis, [(i, i ^ mask) for i in range(size)])  52.6 us
    ppermute x4, starting transfers between devices, to_section_before(): return lax.ppermute(value, ('section', 'ctx'), pairs)  28.6 us
    ppermute x13, starting transfers between devices, swapped(): return lax.ppermute(value, axis, [(i, i ^ mask) for i in range(size)])  17.5 us
    ppermute x4, waiting for transfers between devices, to_section_before(): return lax.ppermute(value, ('section', 'ctx'), pairs)  16.6 us
    pallas_call x1, Pallas kernels, attention_backward(): pl.pallas_call(functools.partial(attention_kernel, n), out_shape=[jax.Sha...  12.7 us
    pallas_call x1, Pallas kernels, input_gradient(): pl.pallas_call(functools.partial(input_kernel, n, share), out_shape=[jax....  3.59 us
    pallas_call x2, Pallas kernels, join_columns(): pl.pallas_call(functools.partial(join_kernel, n), out_shape=jax.ShapeDtyp...  3.17 us
  transfers between devices with their start and end apart: 17, of which 8 were waited for; matrix products, arithmetic and copies ran while one was open for 1% of the time, Pallas kernels for 5%

profile of v1, /device:TPU:9, one launch (start us, length us, event | category | flops | bytes accessed | tf_op | source)
XLA Modules:
  0.0 142.8 jit_solution(17057632261844038362)
XLA Ops:
  0.7 1.3 dynamic-slice_bitcast_fusion.4
  2.1 0.7 dynamic-slice_bitcast_fusion.8
  2.8 2.4 %collective-permute-start.1 = (bf16[128,1280]{1,0:T(8,128)(2,1)S(1)}, bf16[128,1280]{1,0:T(8,128)(2,1)S(1)}, u32[]{:S(2)}, u32[]{:S(2)}) collective-permute-start(bf16[128,1280]{1,0:T(8,128)(2,1)S(1)} %pad_maximum_fusion.2), channel_id=1, source_target_pairs={{0,2},{1,3},{2,0},{3,1},{4,6},{5,7},{6,4},{7,5},{8,10},{9,11},{10,... | collective-permute-start | bytes 983048 | tf_op jit(solution)/shard_map/ppermute | solution.py:293
  5.2 0.2 collective-permute-start
  5.5 0.2 collective-permute-start.2
  5.7 0.5 fusion.1
  6.3 0.1 stack.23.pos_ref
  6.4 0.8 pad_maximum_fusion.refs_0_.refs_4_
  7.2 12.9 %collective-permute-done.1.refs_2_.refs_6_ = bf16[128,1280]{1,0:T(8,128)(2,1)S(1)} collective-permute-done((bf16[128,1280]{1,0:T(8,128)(2,1)S(1)}, bf16[128,1280]{1,0:T(8,128)(2,1)S(1)}, u32[]{:S(2)}, u32[]{:S(2)}) %collective-permute-start.1) | collective-permute-done | bytes 327712 | tf_op jit(solution)/shard_map/ppermute | solution.py:293
  20.0 13.5 %collective-permute-done.2.refs_3_.refs_7_ = bf16[128,1280]{1,0:T(8,128)(2,1)S(1)} collective-permute-done((bf16[128,1280]{1,0:T(8,128)(2,1)S(1)}, bf16[128,1280]{1,0:T(8,128)(2,1)S(1)}, u32[]{:S(2)}, u32[]{:S(2)}) %collective-permute-start.2) | collective-permute-done | bytes 327712 | tf_op jit(solution)/shard_map/ppermute | solution.py:293
  33.6 12.7 %attention_backward.1 = (bf16[128,1024]{1,0:T(8,128)(2,1)S(1)}, bf16[128,1024]{1,0:T(8,128)(2,1)S(1)}, bf16[128,1024]{1,0:T(8,128)(2,1)S(1)}, bf16[128,1024]{1,0:T(8,128)(2,1)S(1)}, bf16[512,256]{1,0:T(8,128)(2,1)S(1)}) custom-call(s32[5]{0:T(128)S(1)} %stack.23.pos_ref, bf16[128,1280]{1,0:T(8,128)(2,1)S(1)} %pad_maximum_fusion.refs_0_.refs_4_, ...), custom_call_target="tpu_custom_call" | custom-call | flops 2684354560 | bytes 3145728 | tf_op jit(solution)/shard_map/attention_backward/pallas_call | solution.py:132
  46.4 3.4 %collective-permute-start.3 = (bf16[512,256]{1,0:T(8,128)(2,1)S(1)}, bf16[512,256]{1,0:T(8,128)(2,1)S(1)}, u32[]{:S(2)}, u32[]{:S(2)}) collective-permute-start(bf16[512,256]{1,0:T(8,128)(2,1)S(1)} %get-tuple-element.21.refs_0_), channel_id=1, source_target_pairs={{0,1},{1,0},{2,3},{3,2},{4,5},{5,4},{6,7},{7,6},{8,9},{9,8},{10,11... | collective-permute-start | bytes 786440 | tf_op jit(solution)/shard_map/ppermute | solution.py:293
  49.8 7.7 %collective-permute-done.4.refs_2_ = bf16[512,256]{1,0:T(8,128)(2,1)S(1)} collective-permute-done((bf16[512,256]{1,0:T(8,128)(2,1)S(1)}, bf16[512,256]{1,0:T(8,128)(2,1)S(1)}, u32[]{:S(2)}, u32[]{:S(2)}) %collective-permute-start.4) | collective-permute-done | bytes 262176 | tf_op jit(solution)/shard_map/ppermute | solution.py:293
  57.5 4.5 %collective-permute-start.5 = (bf16[512,256]{1,0:T(8,128)(2,1)S(1)}, bf16[512,256]{1,0:T(8,128)(2,1)S(1)}, u32[]{:S(2)}, u32[]{:S(2)}) collective-permute-start(bf16[512,256]{1,0:T(8,128)(2,1)S(1)} %collective-permute-done.4.refs_2_), channel_id=1, source_target_pairs={{0,1},{1,0},{2,3},{3,2},{4,5},{5,4},{6,7},{7,6},{8,9},{9,8},{10,11... | collective-permute-start | bytes 786440 | tf_op jit(solution)/shard_map/ppermute | solution.py:293
  62.3 2.6 %collective-permute-start.15 = (bf16[128,1024]{1,0:T(8,128)(2,1)S(1)}, bf16[128,1024]{1,0:T(8,128)(2,1)S(1)}, u32[]{:S(2)}, u32[]{:S(2)}) collective-permute-start(bf16[128,1024]{1,0:T(8,128)(2,1)S(1)} %get-tuple-element.35), channel_id=1, source_target_pairs={{0,3},{1,2},{2,1},{3,0},{4,7},{5,6},{6,5},{7,4},{8,11},{9,10},{10,... | collective-permute-start | bytes 786440 | tf_op jit(solution)/shard_map/ppermute | solution.py:293
  64.9 7.3 %collective-permute-done.5.refs_3_ = bf16[512,256]{1,0:T(8,128)(2,1)S(1)} collective-permute-done((bf16[512,256]{1,0:T(8,128)(2,1)S(1)}, bf16[512,256]{1,0:T(8,128)(2,1)S(1)}, u32[]{:S(2)}, u32[]{:S(2)}) %collective-permute-start.5) | collective-permute-done | bytes 262176 | tf_op jit(solution)/shard_map/ppermute | solution.py:293
  72.2 3.6 %input_gradient.1 = (bf16[128,1024]{1,0:T(8,128)(2,1)S(1)}, bf16[128,1024]{1,0:T(8,128)(2,1)S(1)}, bf16[128,1024]{1,0:T(8,128)(2,1)S(1)}, bf16[128,1024]{1,0:T(8,128)(2,1)S(1)}, bf16[512,1024]{1,0:T(8,128)(2,1)S(1)}) custom-call(s32[5]{0:T(128)S(1)} %stack.23.pos_ref, bf16[512,256]{1,0:T(8,128)(2,1)S(1)} %get-tuple-element.21.refs_0_, ...), custom_call_target="tpu_custom_call" | custom-call | flops 1073741824 | bytes 5242880 | tf_op jit(solution)/shard_map/input_gradient/pallas_call | solution.py:204
  75.8 2.8 %collective-permute-done.13.refs_1_ = bf16[128,1024]{1,0:T(8,128)(2,1)S(1)} collective-permute-done((bf16[128,1024]{1,0:T(8,128)(2,1)S(1)}, bf16[128,1024]{1,0:T(8,128)(2,1)S(1)}, u32[]{:S(2)}, u32[]{:S(2)}) %collective-permute-start.13) | collective-permute-done | bytes 262176 | tf_op jit(solution)/shard_map/ppermute | solution.py:293
  78.6 8.3 %collective-permute-done.15.refs_3_ = bf16[128,1024]{1,0:T(8,128)(2,1)S(1)} collective-permute-done((bf16[128,1024]{1,0:T(8,128)(2,1)S(1)}, bf16[128,1024]{1,0:T(8,128)(2,1)S(1)}, u32[]{:S(2)}, u32[]{:S(2)}) %collective-permute-start.15) | collective-permute-done | bytes 262176 | tf_op jit(solution)/shard_map/ppermute | solution.py:293
  86.9 1.9 %weight_gradient.1 = (bf16[1024,512]{1,0:T(8,128)(2,1)S(1)}, f32[1024,512]{1,0:T(8,128)S(1)}) custom-call(s32[5]{0:T(128)S(1)} %stack.23.pos_ref, bf16[128,1024]{1,0:T(8,128)(2,1)S(1)} %get-tuple-element.41.refs_0_, bf16[128,1024]{1,0:T(8,128)(2,1)S(1)} %collective-permute-done.13.refs_1_, bf16[128,1024]{1,0:T(8,128)(2,1)S(1)} %collective-permute-done.14.refs_2_, ...), custom_call_target="tpu_custom_call" | custom-call | flops 1073741824 | bytes 6291456 | tf_op jit(solution)/shard_map/weight_gradient/pallas_call | solution.py:250
  88.8 1.3 collective-permute-start.16
  90.1 0.4 collective-permute-start.11
  90.6 2.2 %collective-permute-start.12 = (bf16[128,1024]{1,0:T(8,128)(2,1)S(1)}, bf16[128,1024]{1,0:T(8,128)(2,1)S(1)}, u32[]{:S(2)}, u32[]{:S(2)}) collective-permute-start(bf16[128,1024]{1,0:T(8,128)(2,1)S(1)} %get-tuple-element.32), channel_id=1, source_target_pairs={{0,3},{1,2},{2,1},{3,0},{4,7},{5,6},{6,5},{7,4},{8,11},{9,10},{10,... | collective-permute-start | bytes 786440 | tf_op jit(solution)/shard_map/ppermute | solution.py:293
  92.8 5.2 %collective-permute-start.6 = (bf16[128,1024]{1,0:T(8,128)(2,1)S(1)}, bf16[128,1024]{1,0:T(8,128)(2,1)S(1)}, u32[]{:S(2)}, u32[]{:S(2)}) collective-permute-start(bf16[128,1024]{1,0:T(8,128)(2,1)S(1)} %get-tuple-element.22), channel_id=1, source_target_pairs={{8,0},{9,1},{10,2},{11,3},{16,8},{17,9},{18,10},{19,11},{24,16},{2... | collective-permute-start | bytes 786440 | tf_op jit(solution)/shard_map/ppermute | solution.py:301
  97.9 6.7 %collective-permute-start.7 = (bf16[128,1024]{1,0:T(8,128)(2,1)S(1)}, bf16[128,1024]{1,0:T(8,128)(2,1)S(1)}, u32[]{:S(2)}, u32[]{:S(2)}) collective-permute-start(bf16[128,1024]{1,0:T(8,128)(2,1)S(1)} %get-tuple-element.23), channel_id=1, source_target_pairs={{8,1},{9,0},{10,3},{11,2},{16,9},{17,8},{18,11},{19,10},{24,17},{2... | collective-permute-start | bytes 786440 | tf_op jit(solution)/shard_map/ppermute | solution.py:301
  104.6 10.6 %collective-permute-start.8 = (bf16[128,1024]{1,0:T(8,128)(2,1)S(1)}, bf16[128,1024]{1,0:T(8,128)(2,1)S(1)}, u32[]{:S(2)}, u32[]{:S(2)}) collective-permute-start(bf16[128,1024]{1,0:T(8,128)(2,1)S(1)} %get-tuple-element.24), channel_id=1, source_target_pairs={{8,2},{9,3},{10,0},{11,1},{16,10},{17,11},{18,8},{19,9},{24,18},{2... | collective-permute-start | bytes 786440 | tf_op jit(solution)/shard_map/ppermute | solution.py:301
  115.3 6.2 %collective-permute-start.9 = (bf16[128,1024]{1,0:T(8,128)(2,1)S(1)}, bf16[128,1024]{1,0:T(8,128)(2,1)S(1)}, u32[]{:S(2)}, u32[]{:S(2)}) collective-permute-start(bf16[128,1024]{1,0:T(8,128)(2,1)S(1)} %get-tuple-element.25), channel_id=1, source_target_pairs={{8,3},{9,2},{10,1},{11,0},{16,11},{17,10},{18,9},{19,8},{24,19},{2... | collective-permute-start | bytes 786440 | tf_op jit(solution)/shard_map/ppermute | solution.py:301
  121.5 1.6 %join_columns.3 = bf16[128,4096]{1,0:T(8,128)(2,1)} custom-call(s32[5]{0:T(128)S(1)} %stack.23.pos_ref, bf16[128,1024]{1,0:T(8,128)(2,1)S(1)} %get-tuple-element.26.refs_0_, bf16[128,1024]{1,0:T(8,128)(2,1)S(1)} %collective-permute-done.10.refs_1_, bf16[128,1024]{1,0:T(8,128)(2,1)S(1)} %collective-permute-done.11.refs_2_, ...), custom_call_target="tpu_custom_call" | custom-call | bytes 2097152 | tf_op jit(solution)/shard_map/join_columns/pallas_call | solution.py:278
  123.0 0.9 collective-permute-done.8.refs_2_
  124.0 15.6 %collective-permute-done.9.refs_3_ = bf16[128,1024]{1,0:T(8,128)(2,1)S(1)} collective-permute-done((bf16[128,1024]{1,0:T(8,128)(2,1)S(1)}, bf16[128,1024]{1,0:T(8,128)(2,1)S(1)}, u32[]{:S(2)}, u32[]{:S(2)}) %collective-permute-start.9) | collective-permute-done | bytes 262176 | tf_op jit(solution)/shard_map/ppermute | solution.py:301
  139.6 1.6 %join_columns.2 = bf16[128,4096]{1,0:T(8,128)(2,1)} custom-call(s32[5]{0:T(128)S(1)} %stack.23.pos_ref, bf16[128,1024]{1,0:T(8,128)(2,1)S(1)} %collective-permute-done.6.refs_0_, bf16[128,1024]{1,0:T(8,128)(2,1)S(1)} %collective-permute-done.7.refs_1_, bf16[128,1024]{1,0:T(8,128)(2,1)S(1)} %collective-permute-done.8.refs_2_, ...), custom_call_target="tpu_custom_call" | custom-call | bytes 2097152 | tf_op jit(solution)/shard_map/join_columns/pallas_call | solution.py:278
  141.2 1.7 %multiply_bitcast_fusion = f32[1,1024,512]{2,1,0:T(8,128)} fusion(f32[1024,512]{1,0:T(8,128)S(1)} %get-tuple-element.37, bf16[1024,512]{1,0:T(8,128)(2,1)S(1)} %collective-permute-done.16), kind=kLoop, calls=%fused_computation | loop fusion | flops 1572864 | bytes 5242880 | tf_op jit(solution)/shard_map/broadcast_in_dim | solution.py:376
  (34 shorter events, 0.4 us)
Async XLA Ops:
  0.6 1.4 copy-start.4
  0.6 1.4 copy-start.5
  0.7 5.0 %copy-start.6 = (s32[1,512]{1,0:T(1,128)S(1)}, s32[1,512]{1,0:T(1,128)}, u32[]{:S(2)}) copy-start(s32[1,512]{1,0:T(1,128)} %param.16) | copy-start | bytes 6148
  0.7 5.0 %copy-start.7 = (f32[64]{0:T(128)S(1)}, f32[64]{0:T(128)}, u32[]{:S(2)}) copy-start(f32[64]{0:T(128)} %constant.88) | copy-start | bytes 772
  2.1 31.5 %copy-start.1 = (bf16[1,1,512,1024]{3,2,1,0:T(8,128)(2,1)S(1)}, bf16[1,1,512,1024]{3,2,1,0:T(8,128)(2,1)}, u32[]{:S(2)}) copy-start(bf16[1,1,512,1024]{3,2,1,0:T(8,128)(2,1)} %param.11) | copy-start | bytes 3145732
  2.1 31.5 %copy-start.2 = (s32[1,512]{1,0:T(1,128)S(1)}, s32[1,512]{1,0:T(1,128)}, u32[]{:S(2)}) copy-start(s32[1,512]{1,0:T(1,128)} %refs_9_.1) | copy-start | bytes 6148
  2.8 17.2 %collective-permute-start.1 = (bf16[128,1280]{1,0:T(8,128)(2,1)S(1)}, bf16[128,1280]{1,0:T(8,128)(2,1)S(1)}, u32[]{:S(2)}, u32[]{:S(2)}) collective-permute-start(bf16[128,1280]{1,0:T(8,128)(2,1)S(1)} %pad_maximum_fusion.2), channel_id=1, source_target_pairs={{0,2},{1,3},{2,0},{3,1},{4,6},{5,7},{6,4},{7,5},{8,10},{9,11},{10,... | collective-permute-start | bytes 983048 | tf_op jit(solution)/shard_map/ppermute | solution.py:293
  5.2 14.8 %collective-permute-start = (bf16[128,1280]{1,0:T(8,128)(2,1)S(1)}, bf16[128,1280]{1,0:T(8,128)(2,1)S(1)}, u32[]{:S(2)}, u32[]{:S(2)}) collective-permute-start(bf16[128,1280]{1,0:T(8,128)(2,1)S(1)} %pad_maximum_fusion.1), channel_id=1, source_target_pairs={{0,1},{1,0},{2,3},{3,2},{4,5},{5,4},{6,7},{7,6},{8,9},{9,8},{10,11... | collective-permute-start | bytes 983048 | tf_op jit(solution)/shard_map/ppermute | solution.py:293
  5.5 28.1 %collective-permute-start.2 = (bf16[128,1280]{1,0:T(8,128)(2,1)S(1)}, bf16[128,1280]{1,0:T(8,128)(2,1)S(1)}, u32[]{:S(2)}, u32[]{:S(2)}) collective-permute-start(bf16[128,1280]{1,0:T(8,128)(2,1)S(1)} %pad_maximum_fusion.3), channel_id=1, source_target_pairs={{0,3},{1,2},{2,1},{3,0},{4,7},{5,6},{6,5},{7,4},{8,11},{9,10},{10,... | collective-permute-start | bytes 983048 | tf_op jit(solution)/shard_map/ppermute | solution.py:293
  33.6 28.5 %copy-start.3 = (bf16[1,1,128,4096]{3,2,1,0:T(8,128)(2,1)S(1)}, bf16[1,1,128,4096]{3,2,1,0:T(8,128)(2,1)}, u32[]{:S(2)}) copy-start(bf16[1,1,128,4096]{3,2,1,0:T(8,128)(2,1)} %param.9) | copy-start | bytes 3145732
  46.3 25.9 %copy-start = (bf16[1,1024,1024]{2,1,0:T(8,128)(2,1)S(1)}, bf16[1,1024,1024]{2,1,0:T(8,128)(2,1)}, u32[]{:S(2)}) copy-start(bf16[1,1024,1024]{2,1,0:T(8,128)(2,1)} %param.14) | copy-start | bytes 6291460
  46.3 11.2 %collective-permute-start.4 = (bf16[512,256]{1,0:T(8,128)(2,1)S(1)}, bf16[512,256]{1,0:T(8,128)(2,1)S(1)}, u32[]{:S(2)}, u32[]{:S(2)}) collective-permute-start(bf16[512,256]{1,0:T(8,128)(2,1)S(1)} %get-tuple-element.21.refs_0_), channel_id=1, source_target_pairs={{0,2},{1,3},{2,0},{3,1},{4,6},{5,7},{6,4},{7,5},{8,10},{9,11},{10,... | collective-permute-start | bytes 786440 | tf_op jit(solution)/shard_map/ppermute | solution.py:293
  46.4 18.5 %collective-permute-start.3 = (bf16[512,256]{1,0:T(8,128)(2,1)S(1)}, bf16[512,256]{1,0:T(8,128)(2,1)S(1)}, u32[]{:S(2)}, u32[]{:S(2)}) collective-permute-start(bf16[512,256]{1,0:T(8,128)(2,1)S(1)} %get-tuple-element.21.refs_0_), channel_id=1, source_target_pairs={{0,1},{1,0},{2,3},{3,2},{4,5},{5,4},{6,7},{7,6},{8,9},{9,8},{10,11... | collective-permute-start | bytes 786440 | tf_op jit(solution)/shard_map/ppermute | solution.py:293
  57.5 14.6 %collective-permute-start.5 = (bf16[512,256]{1,0:T(8,128)(2,1)S(1)}, bf16[512,256]{1,0:T(8,128)(2,1)S(1)}, u32[]{:S(2)}, u32[]{:S(2)}) collective-permute-start(bf16[512,256]{1,0:T(8,128)(2,1)S(1)} %collective-permute-done.4.refs_2_), channel_id=1, source_target_pairs={{0,1},{1,0},{2,3},{3,2},{4,5},{5,4},{6,7},{7,6},{8,9},{9,8},{10,11... | collective-permute-start | bytes 786440 | tf_op jit(solution)/shard_map/ppermute | solution.py:293
  62.2 16.5 %collective-permute-start.13 = (bf16[128,1024]{1,0:T(8,128)(2,1)S(1)}, bf16[128,1024]{1,0:T(8,128)(2,1)S(1)}, u32[]{:S(2)}, u32[]{:S(2)}) collective-permute-start(bf16[128,1024]{1,0:T(8,128)(2,1)S(1)} %get-tuple-element.33), channel_id=1, source_target_pairs={{0,1},{1,0},{2,3},{3,2},{4,5},{5,4},{6,7},{7,6},{8,9},{9,8},{10,11... | collective-permute-start | bytes 786440 | tf_op jit(solution)/shard_map/ppermute | solution.py:293
  62.2 16.4 %collective-permute-start.14 = (bf16[128,1024]{1,0:T(8,128)(2,1)S(1)}, bf16[128,1024]{1,0:T(8,128)(2,1)S(1)}, u32[]{:S(2)}, u32[]{:S(2)}) collective-permute-start(bf16[128,1024]{1,0:T(8,128)(2,1)S(1)} %get-tuple-element.34), channel_id=1, source_target_pairs={{0,2},{1,3},{2,0},{3,1},{4,6},{5,7},{6,4},{7,5},{8,10},{9,11},{10,... | collective-permute-start | bytes 786440 | tf_op jit(solution)/shard_map/ppermute | solution.py:293
  62.3 24.6 %collective-permute-start.15 = (bf16[128,1024]{1,0:T(8,128)(2,1)S(1)}, bf16[128,1024]{1,0:T(8,128)(2,1)S(1)}, u32[]{:S(2)}, u32[]{:S(2)}) collective-permute-start(bf16[128,1024]{1,0:T(8,128)(2,1)S(1)} %get-tuple-element.35), channel_id=1, source_target_pairs={{0,3},{1,2},{2,1},{3,0},{4,7},{5,6},{6,5},{7,4},{8,11},{9,10},{10,... | collective-permute-start | bytes 786440 | tf_op jit(solution)/shard_map/ppermute | solution.py:293
  88.8 52.4 %collective-permute-start.16 = (bf16[1024,512]{1,0:T(8,128)(2,1)S(1)}, bf16[1024,512]{1,0:T(8,128)(2,1)S(1)}, u32[]{:S(2)}, u32[]{:S(2)}) collective-permute-start(bf16[1024,512]{1,0:T(8,128)(2,1)S(1)} %get-tuple-element.38), channel_id=1, source_target_pairs={{0,4},{4,0},{1,5},{5,1},{2,6},{6,2},{3,7},{7,3},{8,12},{12,8},{9,1... | collective-permute-start | bytes 3145736 | tf_op jit(solution)/shard_map/ppermute | solution.py:293
  90.1 7.8 %collective-permute-start.10 = (bf16[128,1024]{1,0:T(8,128)(2,1)S(1)}, bf16[128,1024]{1,0:T(8,128)(2,1)S(1)}, u32[]{:S(2)}, u32[]{:S(2)}) collective-permute-start(bf16[128,1024]{1,0:T(8,128)(2,1)S(1)} %get-tuple-element.30), channel_id=1, source_target_pairs={{0,1},{1,0},{2,3},{3,2},{4,5},{5,4},{6,7},{7,6},{8,9},{9,8},{10,11... | collective-permute-start | bytes 786440 | tf_op jit(solution)/shard_map/ppermute | solution.py:293
  90.1 14.5 %collective-permute-start.11 = (bf16[128,1024]{1,0:T(8,128)(2,1)S(1)}, bf16[128,1024]{1,0:T(8,128)(2,1)S(1)}, u32[]{:S(2)}, u32[]{:S(2)}) collective-permute-start(bf16[128,1024]{1,0:T(8,128)(2,1)S(1)} %get-tuple-element.31), channel_id=1, source_target_pairs={{0,2},{1,3},{2,0},{3,1},{4,6},{5,7},{6,4},{7,5},{8,10},{9,11},{10,... | collective-permute-start | bytes 786440 | tf_op jit(solution)/shard_map/ppermute | solution.py:293
  90.6 24.7 %collective-permute-start.12 = (bf16[128,1024]{1,0:T(8,128)(2,1)S(1)}, bf16[128,1024]{1,0:T(8,128)(2,1)S(1)}, u32[]{:S(2)}, u32[]{:S(2)}) collective-permute-start(bf16[128,1024]{1,0:T(8,128)(2,1)S(1)} %get-tuple-element.32), channel_id=1, source_target_pairs={{0,3},{1,2},{2,1},{3,0},{4,7},{5,6},{6,5},{7,4},{8,11},{9,10},{10,... | collective-permute-start | bytes 786440 | tf_op jit(solution)/shard_map/ppermute | solution.py:293
  92.8 30.3 %collective-permute-start.6 = (bf16[128,1024]{1,0:T(8,128)(2,1)S(1)}, bf16[128,1024]{1,0:T(8,128)(2,1)S(1)}, u32[]{:S(2)}, u32[]{:S(2)}) collective-permute-start(bf16[128,1024]{1,0:T(8,128)(2,1)S(1)} %get-tuple-element.22), channel_id=1, source_target_pairs={{8,0},{9,1},{10,2},{11,3},{16,8},{17,9},{18,10},{19,11},{24,16},{2... | collective-permute-start | bytes 786440 | tf_op jit(solution)/shard_map/ppermute | solution.py:301
  97.9 25.1 %collective-permute-start.7 = (bf16[128,1024]{1,0:T(8,128)(2,1)S(1)}, bf16[128,1024]{1,0:T(8,128)(2,1)S(1)}, u32[]{:S(2)}, u32[]{:S(2)}) collective-permute-start(bf16[128,1024]{1,0:T(8,128)(2,1)S(1)} %get-tuple-element.23), channel_id=1, source_target_pairs={{8,1},{9,0},{10,3},{11,2},{16,9},{17,8},{18,11},{19,10},{24,17},{2... | collective-permute-start | bytes 786440 | tf_op jit(solution)/shard_map/ppermute | solution.py:301
  104.6 19.4 %collective-permute-start.8 = (bf16[128,1024]{1,0:T(8,128)(2,1)S(1)}, bf16[128,1024]{1,0:T(8,128)(2,1)S(1)}, u32[]{:S(2)}, u32[]{:S(2)}) collective-permute-start(bf16[128,1024]{1,0:T(8,128)(2,1)S(1)} %get-tuple-element.24), channel_id=1, source_target_pairs={{8,2},{9,3},{10,0},{11,1},{16,10},{17,11},{18,8},{19,9},{24,18},{2... | collective-permute-start | bytes 786440 | tf_op jit(solution)/shard_map/ppermute | solution.py:301
  115.3 24.3 %collective-permute-start.9 = (bf16[128,1024]{1,0:T(8,128)(2,1)S(1)}, bf16[128,1024]{1,0:T(8,128)(2,1)S(1)}, u32[]{:S(2)}, u32[]{:S(2)}) collective-permute-start(bf16[128,1024]{1,0:T(8,128)(2,1)S(1)} %get-tuple-element.25), channel_id=1, source_target_pairs={{8,3},{9,2},{10,1},{11,0},{16,11},{17,10},{18,9},{19,8},{24,19},{2... | collective-permute-start | bytes 786440 | tf_op jit(solution)/shard_map/ppermute | solution.py:301

commit v2 on v1

--- a/solution.py
+++ b/solution.py
@@ -13,6 +13,7 @@
 KEY_VALUE_HEADS = 4
 HEAD_WIDTH = 128
 QUERY_BLOCK = 256
+FEATURE_BLOCK = 256
 MASKED = -1e30
 
 
@@ -47,7 +48,8 @@
 NT = ((1,), (1,))
 NN = ((1,), (0,))
 TN = ((0,), (0,))
-VMEM_LIMIT = 48 * 1024 * 1024
+ATTENTION_VMEM = 24 * 1024 * 1024
+VMEM_LIMIT = 24 * 1024 * 1024
 
 
 def rows_at(pos_ref, piece, count):
@@ -57,8 +59,8 @@
 def attention_kernel(n, pos_ref, *refs):
     g_refs, kv_refs, refs = refs[:n], refs[n : 2 * n], refs[2 * n :]
     q_ref, seg_ref, cos_ref, sin_ref = refs[:4]
-    dq_refs, dkv_ref = refs[4 : 4 + n], refs[4 + n]
-    k_s, v_s, kt_s, bias_s, g_s, dq_s, dk_s, dv_s = refs[5 + n :]
+    dq_ref, dkv_ref = refs[4:6]
+    k_s, v_s, kt_s, bias_s, g_s, dk_s, dv_s = refs[6:]
     tokens = q_ref.shape[0]
     piece_rows = tokens // n
     width = HEAD_WIDTH
@@ -107,9 +109,7 @@
         t = sin_ref[:, start:stop]
         u, w = dq[:half], dq[half:]
         turned = jnp.concatenate([u * c + w * t, w * c - u * t], 0)
-        dq_s[start:stop, :] = turned.T.astype(jnp.bfloat16)
-    for m in range(n):
-        dq_refs[m][...] = dq_s[rows_at(pos_ref, m, piece_rows), :]
+        dq_ref[start:stop, :] = turned.T.astype(jnp.bfloat16)
 
     @pl.when(head == pl.num_programs(0) - 1)
     def _():
@@ -129,10 +129,12 @@
     heads = cols // width
     piece_rows = tokens // n
     bf16, f32 = jnp.bfloat16, jnp.float32
-    out = pl.pallas_call(
+    return pl.pallas_call(
         functools.partial(attention_kernel, n),
-        out_shape=[jax.ShapeDtypeStruct((piece_rows, cols), bf16)] * n
-        + [jax.ShapeDtypeStruct((tokens, 2 * width), bf16)],
+        out_shape=[
+            jax.ShapeDtypeStruct((tokens, cols), bf16),
+            jax.ShapeDtypeStruct((tokens, 2 * width), bf16),
+        ],
         grid_spec=pltpu.PrefetchScalarGridSpec(
             num_scalar_prefetch=1,
             grid=(heads,),
@@ -144,21 +146,22 @@
                 pl.BlockSpec((width // 2, tokens), lambda h, p: (0, 0)),
                 pl.BlockSpec((width // 2, tokens), lambda h, p: (0, 0)),
             ],
-            out_specs=[pl.BlockSpec((piece_rows, width), lambda h, p: (0, h))] * n
-            + [pl.BlockSpec((tokens, 2 * width), lambda h, p: (0, 0))],
+            out_specs=[
+                pl.BlockSpec((tokens, width), lambda h, p: (0, h)),
+                pl.BlockSpec((tokens, 2 * width), lambda h, p: (0, 0)),
+            ],
             scratch_shapes=[
                 pltpu.VMEM((tokens, width), bf16),
                 pltpu.VMEM((tokens, width), bf16),
                 pltpu.VMEM((width, tokens), bf16),
                 pltpu.VMEM((tokens, tokens), f32),
                 pltpu.VMEM((tokens, width), bf16),
-                pltpu.VMEM((tokens, width), bf16),
                 pltpu.VMEM((tokens, width), f32),
                 pltpu.VMEM((tokens, width), f32),
             ],
         ),
         compiler_params=pltpu.CompilerParams(
-            dimension_semantics=("arbitrary",), vmem_limit_bytes=VMEM_LIMIT
+            dimension_semantics=("arbitrary",), vmem_limit_bytes=ATTENTION_VMEM
         ),
         cost_estimate=pl.CostEstimate(
             flops=10 * heads * tokens * tokens * width,
@@ -167,16 +170,25 @@
         ),
         name="attention_backward",
     )(pos, *pieces, *pieces, queries, segments, cosine, sine)
-    return out[:n], out[n]
 
 
 def input_kernel(n, share, pos_ref, *refs):
     part_refs, weight_ref = refs[:n], refs[n]
     out_refs, kv_ref = refs[n + 1 : 2 * n + 1], refs[2 * n + 1]
-    total = refs[2 * n + 2] if share > 1 else None
+    weight_s, arrived, *sums = refs[2 * n + 2 :]
+    total = sums[0] if share > 1 else kv_ref
     width = HEAD_WIDTH
     kv_width = kv_ref.shape[1] // 2
     piece_rows = out_refs[0].shape[0]
+    blocks, block = weight_s.shape[:2]
+    copies = [
+        pltpu.make_async_copy(
+            weight_ref.at[pl.ds(b * block, block), :], weight_s.at[b], arrived.at[b]
+        )
+        for b in range(blocks)
+    ]
+    for copy in copies:
+        copy.start()
     if share > 1:
         total[...] = jnp.zeros_like(total)
     for m in range(n):
@@ -187,12 +199,16 @@
             if share > 1:
                 total[:, cols] += part.astype(jnp.float32)
             else:
-                kv_ref[:, cols] = part
+                total[:, cols] = part
     if share > 1:
         kv_ref[...] = total[...].astype(kv_ref.dtype)
-    for m in range(n):
-        rows = kv_ref[rows_at(pos_ref, m, piece_rows), :]
-        out_refs[m][...] = dot(rows, weight_ref[...], NT).astype(jnp.bfloat16)
+    for b, copy in enumerate(copies):
+        copy.wait()
+        for m in range(n):
+            rows = kv_ref[rows_at(pos_ref, m, piece_rows), :]
+            out_refs[m][:, b * block : (b + 1) * block] = dot(rows, weight_s[b], NT).astype(
+                jnp.bfloat16
+            )
 
 
 def input_gradient(pos, parts, weight, share):
@@ -200,14 +216,21 @@
     tokens = parts[0].shape[0]
     rows, cols = weight.shape
     bf16 = jnp.bfloat16
+    block = min(FEATURE_BLOCK, rows)
     vmem = pl.BlockSpec(memory_space=pltpu.VMEM)
     out = pl.pallas_call(
         functools.partial(input_kernel, n, share),
         out_shape=[jax.ShapeDtypeStruct((tokens // n, rows), bf16)] * n
         + [jax.ShapeDtypeStruct((tokens, cols), bf16)],
-        in_specs=[pl.BlockSpec(memory_space=pltpu.SMEM)] + [vmem] * (n + 1),
+        in_specs=[pl.BlockSpec(memory_space=pltpu.SMEM)]
+        + [vmem] * n
+        + [pl.BlockSpec(memory_space=pltpu.HBM)],
         out_specs=[vmem] * (n + 1),
-        scratch_shapes=[pltpu.VMEM((tokens, cols), jnp.float32)] if share > 1 else [],
+        scratch_shapes=[
+            pltpu.VMEM((rows // block, block, cols), bf16),
+            pltpu.SemaphoreType.DMA((rows // block,)),
+        ]
+        + ([pltpu.VMEM((tokens, cols), jnp.float32)] if share > 1 else []),
         compiler_params=pltpu.CompilerParams(vmem_limit_bytes=VMEM_LIMIT),
         cost_estimate=pl.CostEstimate(
             flops=2 * tokens * rows * cols,
@@ -263,22 +286,34 @@
     )(pos, *pieces, kv_grad)
 
 
-def join_kernel(n, pos_ref, *refs):
-    out_ref = refs[n]
-    cols = refs[0].shape[1]
-    for m in range(n):
+def join_kernel(order, pos_ref, *refs):
+    out_ref = refs[-1]
+    n, cols = len(order), refs[0].shape[1]
+    for i, m in enumerate(order):
         at = pl.ds(pl.multiple_of(pos_ref[m] * cols, cols), cols)
-        out_ref[:, at] = refs[m][...]
-
-
-def join_columns(pos, pieces):
-    n = len(pieces)
+        if i == 0 and len(refs) > n + 1:
+            relayed = pos_ref[n + 1] == 1
+
+            @pl.when(relayed)
+            def _():
+                out_ref[:, at] = refs[n][...]
+
+            @pl.when(jnp.logical_not(relayed))
+            def _():
+                out_ref[:, at] = refs[0][...]
+
+        else:
+            out_ref[:, at] = refs[i][...]
+
+
+def join_columns(pos, order, pieces):
     rows, cols = pieces[0].shape
+    n = len(order)
     vmem = pl.BlockSpec(memory_space=pltpu.VMEM)
     return pl.pallas_call(
-        functools.partial(join_kernel, n),
+        functools.partial(join_kernel, order),
         out_shape=jax.ShapeDtypeStruct((rows, n * cols), pieces[0].dtype),
-        in_specs=[pl.BlockSpec(memory_space=pltpu.SMEM)] + [vmem] * n,
+        in_specs=[pl.BlockSpec(memory_space=pltpu.SMEM)] + [vmem] * len(pieces),
         out_specs=vmem,
         compiler_params=pltpu.CompilerParams(vmem_limit_bytes=VMEM_LIMIT),
         cost_estimate=pl.CostEstimate(
@@ -286,6 +321,28 @@
         ),
         name="join_columns",
     )(pos, *pieces)
+
+
+def lay_out_kernel(in_ref, out_ref):
+    cols = in_ref.shape[2]
+    for block in range(in_ref.shape[0]):
+        out_ref[:, block * cols : (block + 1) * cols] = in_ref[block]
+
+
+def lay_out(blocks):
+    n, rows, cols = blocks.shape
+    vmem = pl.BlockSpec(memory_space=pltpu.VMEM)
+    return pl.pallas_call(
+        lay_out_kernel,
+        out_shape=jax.ShapeDtypeStruct((rows, n * cols), blocks.dtype),
+        in_specs=[vmem],
+        out_specs=vmem,
+        compiler_params=pltpu.CompilerParams(vmem_limit_bytes=VMEM_LIMIT),
+        cost_estimate=pl.CostEstimate(
+            flops=0, bytes_accessed=4 * rows * n * cols, transcendentals=0
+        ),
+        name="lay_out",
+    )(blocks)
 
 
 def swapped(value, mask, axis="ctx"):
@@ -299,6 +356,19 @@
         (s * size + i, (s - 1) * size + (i ^ mask)) for s in range(1, sections) for i in range(size)
     ]
     return lax.ppermute(value, ("section", "ctx"), pairs)
+
+
+def relayed_section_before(value, mask):
+    sections, size = lax.axis_size("section"), lax.axis_size("ctx")
+    half = sections // 2
+    first = [
+        (s * size + i, (s - 1) * size + (i if s == half else i ^ mask))
+        for s in range(1, sections)
+        for i in range(size)
+    ]
+    second = [((half - 1) * size + i, (half - 1) * size + (i ^ mask)) for i in range(size)]
+    value = lax.ppermute(value, ("section", "ctx"), first)
+    return value, lax.ppermute(value, ("section", "ctx"), second)
 
 
 def after(values, others):
@@ -318,7 +388,10 @@
     share = n // kv_heads
     masks = list(range(1, n))[::-1]
     block_of = [me ^ m for m in range(n)]
-    pos = jnp.stack([*block_of, lax.axis_index("dp")]).astype(jnp.int32)
+    section = lax.axis_index("section")
+    relay = lax.axis_size("section") == 4 and n == 4
+    at_relay = section == lax.axis_size("section") // 2 - 1
+    pos = jnp.stack([*block_of, lax.axis_index("dp"), at_relay.astype(jnp.int32)])
 
     def block(array, at, size):
         return lax.dynamic_slice_in_dim(array, at * size, size, 1)
@@ -344,24 +417,34 @@
 
     features = inputs.shape[1] // n
     x_out = [block(inputs, block_of[m], features) for m in range(n)]
+    far, near = n // 2, 1
+    middle = [m for m in masks if m not in (far, near)]
     x_held = after(x_out, pieces)
-    x_sent = {m: swapped(x_held[m], m) for m in masks}
-    x_pieces = [x_out[0], *(x_sent[m] for m in range(1, n))]
-
-    dq_pieces, dkv = attention_backward(pos, pieces, queries[0, 0], segments, cosine, sine)
+    x_sent = {m: swapped(x_held[m], m) for m in [*middle, near]}
+
+    dq, dkv = attention_backward(pos, pieces, queries[0, 0], segments, cosine, sine)
+    dkv = after(dkv, x_sent)
 
     parts = {0: dkv}
-    bit = n // 2
+    bit = far
     while bit:
         for m in sorted(parts):
             parts[m | bit] = swapped(parts[m], bit)
         bit //= 2
+    x_sent[far] = swapped(after(x_out[far], parts[far]), far)
+    dq = after(dq, parts[far])
+    dq = lax.all_to_all(dq.reshape(n, tokens // n, cols), "ctx", 0, 0, tiled=True)
     parts = [parts[m] for m in range(n)]
+    x_pieces = [x_out[0], *(x_sent[m] for m in range(1, n))]
 
     in_grads, kv_grad = input_gradient(pos, parts, kv_weight[0], share)
-    in_sent = {m: to_section_before(in_grads[m], m) for m in [*masks, 0]}
-    dq_held = after(dq_pieces, parts)
-    dq_sent = {m: swapped(dq_held[m], m) for m in masks}
+    order = [*masks, 0]
+    in_sent = [to_section_before(in_grads[m], m) for m in order[1:]]
+    if relay:
+        direct, second = relayed_section_before(in_grads[order[0]], order[0])
+        in_sent = [direct, *in_sent, second]
+    else:
+        in_sent = [to_section_before(in_grads[order[0]], order[0]), *in_sent]
 
     halves = data_size == 2
     if halves:
@@ -371,8 +454,9 @@
         (rows_part,) = weight_gradient(pos, x_pieces, kv_grad, False)
         weight_grad = lax.psum_scatter(rows_part, "dp", scatter_dimension=1, tiled=True) / data_size
 
-    grad_prev = join_columns(pos, [in_sent[m] for m in range(n)])
-    query_grad = join_columns(pos, [dq_pieces[0], *(dq_sent[m] for m in range(1, n))])
+    query_grad = lay_out(dq)
+    last = after(pos, (query_grad, weight_grad))
+    grad_prev = join_columns(last, order, in_sent)
     return (grad_prev[None, None], query_grad[None, None], weight_grad[None])
 
 

time: 143 us -> 120 us (0.84)
  the two profiles are of different devices: /device:TPU:9 before, /device:TPU:0 now
where the time goes in v2:
time: 120 us; the launch traced here: 119 us
  waiting for transfers between devices  56.2 us (47%)
  starting transfers between devices  30.3 us (25%)
  Pallas kernels  23.1 us (19%)
  local copies, waits for them, and re-layouts  5.69 us (5%)
  other arithmetic  2.35 us (2%)
    ppermute x10, waiting for transfers between devices, swapped(): return lax.ppermute(value, axis, [(i, i ^ mask) for i in range(size)])  50.1 us
    ppermute x10, starting transfers between devices, swapped(): return lax.ppermute(value, axis, [(i, i ^ mask) for i in range(size)])  20.9 us
    pallas_call x1, Pallas kernels, attention_backward(): pl.pallas_call(functools.partial(attention_kernel, n), out_shape=[jax.Sha...  13.1 us
    pallas_call x1, Pallas kernels, input_gradient(): pl.pallas_call(functools.partial(input_kernel, n, share), out_shape=[jax....  5.45 us
    ppermute x1, waiting for transfers between devices, relayed_section_before(): value = lax.ppermute(value, ('section', 'ctx'), first)  4.49 us
    ppermute x3, starting transfers between devices, to_section_before(): return lax.ppermute(value, ('section', 'ctx'), pairs)  3.88 us
    all_to_all x1, starting transfers between devices, on_device(): lax.all_to_all(dq.reshape(n, tokens // n, cols), 'ctx', 0, 0, tiled=True)  3.52 us
    unnamed x20, local copies, waits for them, and re-layouts  3.27 us
  transfers between devices with their start and end apart: 16, of which 7 were waited for; matrix products, arithmetic and copies ran while one was open for 3% of the time, Pallas kernels for 18%

profile of v2, /device:TPU:0, one launch (start us, length us, event | category | flops | bytes accessed | tf_op | source)
XLA Modules:
  0.0 118.5 jit_solution(14437261878293740137)
XLA Ops:
  0.7 1.4 %dynamic-slice_bitcast_fusion.4 = (bf16[128,1024]{1,0:T(8,128)(2,1)S(1)}, bf16[128,1024]{1,0:T(8,128)(2,1)S(1)}, bf16[128,1024]{1,0:T(8,128)(2,1)S(1)}, bf16[128,1024]{1,0:T(8,128)(2,1)S(1)}) fusion(bf16[1,1,128,4096]{3,2,1,0:T(8,128)(2,1)} %param.10, s32[]{:T(128)S(6)} %select_n.44, s32[]{:T(128)S(6)} %select_n.40, s32[]{:T(128)S(6)} %select_n.38, ...), kind=kLoop, calls=%fused_computation.9 | loop fusion | bytes 2097168 | tf_op jit(solution)/shard_map/dynamic_slice | solution.py:397
  2.2 3.1 %collective-permute-start = (bf16[128,1280]{1,0:T(8,128)(2,1)S(1)}, bf16[128,1280]{1,0:T(8,128)(2,1)S(1)}, u32[]{:S(2)}, u32[]{:S(2)}) collective-permute-start(bf16[128,1280]{1,0:T(8,128)(2,1)S(1)} %pad_maximum_fusion.1), channel_id=1, source_target_pairs={{0,1},{1,0},{2,3},{3,2},{4,5},{5,4},{6,7},{7,6},{8,9},{9,8},{10,11... | collective-permute-start | bytes 983048 | tf_op jit(solution)/shard_map/ppermute | solution.py:350
  5.4 2.7 %collective-permute-start.1 = (bf16[128,1280]{1,0:T(8,128)(2,1)S(1)}, bf16[128,1280]{1,0:T(8,128)(2,1)S(1)}, u32[]{:S(2)}, u32[]{:S(2)}) collective-permute-start(bf16[128,1280]{1,0:T(8,128)(2,1)S(1)} %pad_maximum_fusion.2), channel_id=1, source_target_pairs={{0,2},{1,3},{2,0},{3,1},{4,6},{5,7},{6,4},{7,5},{8,10},{9,11},{10,... | collective-permute-start | bytes 983048 | tf_op jit(solution)/shard_map/ppermute | solution.py:350
  8.2 0.9 dynamic-slice_bitcast_fusion
  9.1 10.2 %collective-permute-done.refs_1_.refs_5_ = bf16[128,1280]{1,0:T(8,128)(2,1)S(1)} collective-permute-done((bf16[128,1280]{1,0:T(8,128)(2,1)S(1)}, bf16[128,1280]{1,0:T(8,128)(2,1)S(1)}, u32[]{:S(2)}, u32[]{:S(2)}) %collective-permute-start) | collective-permute-done | bytes 327712 | tf_op jit(solution)/shard_map/ppermute | solution.py:350
  19.2 11.8 %collective-permute-done.1.refs_2_.refs_6_ = bf16[128,1280]{1,0:T(8,128)(2,1)S(1)} collective-permute-done((bf16[128,1280]{1,0:T(8,128)(2,1)S(1)}, bf16[128,1280]{1,0:T(8,128)(2,1)S(1)}, u32[]{:S(2)}, u32[]{:S(2)}) %collective-permute-start.1) | collective-permute-done | bytes 327712 | tf_op jit(solution)/shard_map/ppermute | solution.py:350
  31.0 6.2 %collective-permute-start.3 = (bf16[128,1024]{1,0:T(8,128)(2,1)}, bf16[128,1024]{1,0:T(8,128)(2,1)S(1)}, u32[]{:S(2)}, u32[]{:S(2)}) collective-permute-start(bf16[128,1024]{1,0:T(8,128)(2,1)} %get-tuple-element.20), channel_id=1, source_target_pairs={{0,1},{1,0},{2,3},{3,2},{4,5},{5,4},{6,7},{7,6},{8,9},{9,8},{10,11... | collective-permute-start | bytes 786440 | tf_op jit(solution)/shard_map/ppermute | solution.py:350
  37.2 2.5 %collective-permute-start.4 = (bf16[128,1024]{1,0:T(8,128)(2,1)}, bf16[128,1024]{1,0:T(8,128)(2,1)S(1)}, u32[]{:S(2)}, u32[]{:S(2)}) collective-permute-start(bf16[128,1024]{1,0:T(8,128)(2,1)} %get-tuple-element.21), channel_id=1, source_target_pairs={{0,3},{1,2},{2,1},{3,0},{4,7},{5,6},{6,5},{7,4},{8,11},{9,10},{10,... | collective-permute-start | bytes 786440 | tf_op jit(solution)/shard_map/ppermute | solution.py:350
  39.6 0.5 fusion.1
  40.3 13.1 %attention_backward.1 = (bf16[512,1024]{1,0:T(8,128)(2,1)}, bf16[512,256]{1,0:T(8,128)(2,1)}) custom-call(s32[6]{0:T(128)S(1)} %stack.31.pos_ref, bf16[128,1280]{1,0:T(8,128)(2,1)S(1)} %pad_maximum_fusion.refs_0_.refs_4_, bf16[128,1280]{1,0:T(8,128)(2,1)S(1)} %collective-permute-done.refs_1_.refs_5_, ...), custom_call_target="tpu_custom_call" | custom-call | flops 2684354560 | bytes 3145728 | tf_op jit(solution)/shard_map/attention_backward/pallas_call | solution.py:132
  53.4 1.9 %collective-permute-start.7 = (bf16[512,256]{1,0:T(8,128)(2,1)}, bf16[512,256]{1,0:T(8,128)(2,1)S(1)}, u32[]{:S(2)}, u32[]{:S(2)}) collective-permute-start(bf16[512,256]{1,0:T(8,128)(2,1)} %get-tuple-element.22.refs_0_), channel_id=1, source_target_pairs={{0,1},{1,0},{2,3},{3,2},{4,5},{5,4},{6,7},{7,6},{8,9},{9,8},{10,11... | collective-permute-start | bytes 786440 | tf_op jit(solution)/shard_map/ppermute | solution.py:350
  55.3 10.1 %collective-permute-done.5.refs_2_ = bf16[512,256]{1,0:T(8,128)(2,1)S(1)} collective-permute-done((bf16[512,256]{1,0:T(8,128)(2,1)}, bf16[512,256]{1,0:T(8,128)(2,1)S(1)}, u32[]{:S(2)}, u32[]{:S(2)}) %collective-permute-start.5) | collective-permute-done | bytes 262176 | tf_op jit(solution)/shard_map/ppermute | solution.py:350
  65.4 2.9 %collective-permute-start.6 = (bf16[128,1024]{1,0:T(8,128)(2,1)}, bf16[128,1024]{1,0:T(8,128)(2,1)S(1)}, u32[]{:S(2)}, u32[]{:S(2)}) collective-permute-start(bf16[128,1024]{1,0:T(8,128)(2,1)} %get-tuple-element.24), channel_id=1, source_target_pairs={{0,2},{1,3},{2,0},{3,1},{4,6},{5,7},{6,4},{7,5},{8,10},{9,11},{10,... | collective-permute-start | bytes 786440 | tf_op jit(solution)/shard_map/ppermute | solution.py:350
  68.3 3.5 %all-to-all-start = ((bf16[4,128,1024]{2,1,0:T(8,128)(2,1)}), bf16[4,128,1024]{2,1,0:T(8,128)(2,1)S(1)}, u32[]{:S(2)}, u32[]{:S(2)}) async-start(bf16[4,128,1024]{2,1,0:T(8,128)(2,1)} %bitcast.24), calls=%async_computation | async-start | bytes 2097152 | tf_op jit(solution)/shard_map/all_to_all | solution.py:436
  71.9 8.5 %collective-permute-done.8.refs_3_ = bf16[512,256]{1,0:T(8,128)(2,1)S(1)} collective-permute-done((bf16[512,256]{1,0:T(8,128)(2,1)S(1)}, bf16[512,256]{1,0:T(8,128)(2,1)S(1)}, u32[]{:S(2)}, u32[]{:S(2)}) %collective-permute-start.8) | collective-permute-done | bytes 262176 | tf_op jit(solution)/shard_map/ppermute | solution.py:350
  80.4 0.7 copy-done.2
  81.1 1.6 %copy-done = bf16[1,1024,1024]{2,1,0:T(8,128)(2,1)S(1)} copy-done((bf16[1,1024,1024]{2,1,0:T(8,128)(2,1)S(1)}, bf16[1,1024,1024]{2,1,0:T(8,128)(2,1)}, u32[]{:S(2)}) %copy-start) | copy-done | bytes 2097176
  82.7 0.9 copy-done.3
  83.7 5.5 %input_gradient.1 = (bf16[128,1024]{1,0:T(8,128)(2,1)S(1)}, bf16[128,1024]{1,0:T(8,128)(2,1)S(1)}, bf16[128,1024]{1,0:T(8,128)(2,1)}, bf16[128,1024]{1,0:T(8,128)(2,1)S(1)}, bf16[512,1024]{1,0:T(8,128)(2,1)S(1)}) custom-call(s32[6]{0:T(128)S(1)} %stack.31.pos_ref, bf16[512,256]{1,0:T(8,128)(2,1)} %get-tuple-element.22.refs_0_, ...), custom_call_target="tpu_custom_call" | custom-call | flops 1073741824 | bytes 5242880 | tf_op jit(solution)/shard_map/input_gradient/pallas_call | solution.py:221
  89.1 1.9 %weight_gradient.1 = (bf16[1024,512]{1,0:T(8,128)(2,1)S(1)}, f32[1024,512]{1,0:T(8,128)S(1)}) custom-call(s32[6]{0:T(128)S(1)} %stack.31.pos_ref, bf16[128,1024]{1,0:T(8,128)(2,1)S(1)} %get-tuple-element.35.refs_0_, bf16[128,1024]{1,0:T(8,128)(2,1)S(1)} %collective-permute-done.3.refs_1_, bf16[128,1024]{1,0:T(8,128)(2,1)S(1)} %collective-permute-done.6.refs_2_, ...), custom_call_target="tpu_custom_call" | custom-call | flops 1073741824 | bytes 6291456 | tf_op jit(solution)/shard_map/weight_gradient/pallas_call | solution.py:273
  91.0 1.6 %collective-permute-start.9 = (bf16[1024,512]{1,0:T(8,128)(2,1)S(1)}, bf16[1024,512]{1,0:T(8,128)(2,1)S(1)}, u32[]{:S(2)}, u32[]{:S(2)}) collective-permute-start(bf16[1024,512]{1,0:T(8,128)(2,1)S(1)} %get-tuple-element.27), channel_id=1, source_target_pairs={{0,4},{4,0},{1,5},{5,1},{2,6},{6,2},{3,7},{7,3},{8,12},{12,8},{9,1... | collective-permute-start | bytes 3145736 | tf_op jit(solution)/shard_map/ppermute | solution.py:350
  92.6 1.3 %collective-permute-start.10 = (bf16[128,1024]{1,0:T(8,128)(2,1)S(1)}, bf16[128,1024]{1,0:T(8,128)(2,1)S(1)}, u32[]{:S(2)}, u32[]{:S(2)}) collective-permute-start(bf16[128,1024]{1,0:T(8,128)(2,1)S(1)} %get-tuple-element.29), channel_id=1, source_target_pairs={{8,3},{9,2},{10,1},{11,0},{16,8},{17,9},{18,10},{19,11},{24,19},{2... | collective-permute-start | bytes 786440 | tf_op jit(solution)/shard_map/ppermute | solution.py:370
  93.9 1.3 %collective-permute-start.11 = (bf16[128,1024]{1,0:T(8,128)(2,1)}, bf16[128,1024]{1,0:T(8,128)(2,1)S(1)}, u32[]{:S(2)}, u32[]{:S(2)}) collective-permute-start(bf16[128,1024]{1,0:T(8,128)(2,1)} %get-tuple-element.30), channel_id=1, source_target_pairs={{8,2},{9,3},{10,0},{11,1},{16,10},{17,11},{18,8},{19,9},{24,18},{2... | collective-permute-start | bytes 786440 | tf_op jit(solution)/shard_map/ppermute | solution.py:358
  95.2 1.3 %collective-permute-start.12 = (bf16[128,1024]{1,0:T(8,128)(2,1)S(1)}, bf16[128,1024]{1,0:T(8,128)(2,1)S(1)}, u32[]{:S(2)}, u32[]{:S(2)}) collective-permute-start(bf16[128,1024]{1,0:T(8,128)(2,1)S(1)} %get-tuple-element.31), channel_id=1, source_target_pairs={{8,1},{9,0},{10,3},{11,2},{16,9},{17,8},{18,11},{19,10},{24,17},{2... | collective-permute-start | bytes 786440 | tf_op jit(solution)/shard_map/ppermute | solution.py:358
  96.5 1.3 %collective-permute-start.13 = (bf16[128,1024]{1,0:T(8,128)(2,1)S(1)}, bf16[128,1024]{1,0:T(8,128)(2,1)S(1)}, u32[]{:S(2)}, u32[]{:S(2)}) collective-permute-start(bf16[128,1024]{1,0:T(8,128)(2,1)S(1)} %get-tuple-element.32), channel_id=1, source_target_pairs={{8,0},{9,1},{10,2},{11,3},{16,8},{17,9},{18,10},{19,11},{24,16},{2... | collective-permute-start | bytes 786440 | tf_op jit(solution)/shard_map/ppermute | solution.py:358
  97.8 4.5 %collective-permute-done.10.refs_0_ = bf16[128,1024]{1,0:T(8,128)(2,1)S(1)} collective-permute-done((bf16[128,1024]{1,0:T(8,128)(2,1)S(1)}, bf16[128,1024]{1,0:T(8,128)(2,1)S(1)}, u32[]{:S(2)}, u32[]{:S(2)}) %collective-permute-start.10) | collective-permute-done | bytes 262176 | tf_op jit(solution)/shard_map/ppermute | solution.py:370
  102.3 0.7 collective-permute-start.14
  103.0 9.5 %collective-permute-done.9 = bf16[1024,512]{1,0:T(8,128)(2,1)S(1)} collective-permute-done((bf16[1024,512]{1,0:T(8,128)(2,1)S(1)}, bf16[1024,512]{1,0:T(8,128)(2,1)S(1)}, u32[]{:S(2)}, u32[]{:S(2)}) %collective-permute-start.9) | collective-permute-done | bytes 1048608 | tf_op jit(solution)/shard_map/ppermute | solution.py:350
  112.5 1.7 %add_multiply_fusion = f32[1024,512]{1,0:T(8,128)} fusion(f32[1024,512]{1,0:T(8,128)S(1)} %get-tuple-element.26, bf16[1024,512]{1,0:T(8,128)(2,1)S(1)} %collective-permute-done.9), kind=kLoop, calls=%fused_computation | loop fusion | flops 1572864 | bytes 5242880 | tf_op jit(solution)/shard_map/div | solution.py:452
  114.2 1.0 lay_out.1
  115.3 1.7 %collective-permute-done.11.refs_1_ = bf16[128,1024]{1,0:T(8,128)(2,1)S(1)} collective-permute-done((bf16[128,1024]{1,0:T(8,128)(2,1)}, bf16[128,1024]{1,0:T(8,128)(2,1)S(1)}, u32[]{:S(2)}, u32[]{:S(2)}) %collective-permute-start.11) | collective-permute-done | bytes 262176 | tf_op jit(solution)/shard_map/ppermute | solution.py:358
  116.9 1.6 %join_columns.1 = bf16[128,4096]{1,0:T(8,128)(2,1)} custom-call(s32[6]{0:T(128)S(1)} %stack.31.pos_ref, bf16[128,1024]{1,0:T(8,128)(2,1)S(1)} %collective-permute-done.10.refs_0_, bf16[128,1024]{1,0:T(8,128)(2,1)S(1)} %collective-permute-done.11.refs_1_, bf16[128,1024]{1,0:T(8,128)(2,1)S(1)} %collective-permute-done.12.refs_2_, ...), custom_call_target="tpu_custom_call" | custom-call | bytes 2097152 | tf_op jit(solution)/shard_map/join_columns/pallas_call | solution.py:313
  (36 shorter events, 0.5 us)
Async XLA Ops:
  0.6 1.5 %copy-start.6 = (bf16[1,1,128,512]{3,2,1,0:T(8,128)(2,1)S(1)}, bf16[1,1,128,512]{3,2,1,0:T(8,128)(2,1)}, u32[]{:S(2)}) copy-start(bf16[1,1,128,512]{3,2,1,0:T(8,128)(2,1)} %param.13) | copy-start | bytes 393220
  0.6 1.5 %copy-start.7 = (bf16[1,1,128,512]{3,2,1,0:T(8,128)(2,1)S(1)}, bf16[1,1,128,512]{3,2,1,0:T(8,128)(2,1)}, u32[]{:S(2)}) copy-start(bf16[1,1,128,512]{3,2,1,0:T(8,128)(2,1)} %param.12) | copy-start | bytes 393220
  0.7 7.4 %copy-start.8 = (s32[1,512]{1,0:T(1,128)S(1)}, s32[1,512]{1,0:T(1,128)}, u32[]{:S(2)}) copy-start(s32[1,512]{1,0:T(1,128)} %param.16) | copy-start | bytes 6148
  0.7 7.4 %copy-start.5 = (bf16[1,1,128,4096]{3,2,1,0:T(8,128)(2,1)S(1)}, bf16[1,1,128,4096]{3,2,1,0:T(8,128)(2,1)}, u32[]{:S(2)}) copy-start(bf16[1,1,128,4096]{3,2,1,0:T(8,128)(2,1)} %param.9) | copy-start | bytes 3145732
  2.2 37.4 %copy-start.9 = (f32[64]{0:T(128)S(1)}, f32[64]{0:T(128)}, u32[]{:S(2)}) copy-start(f32[64]{0:T(128)} %constant.91) | copy-start | bytes 772
  2.2 17.0 %collective-permute-start = (bf16[128,1280]{1,0:T(8,128)(2,1)S(1)}, bf16[128,1280]{1,0:T(8,128)(2,1)S(1)}, u32[]{:S(2)}, u32[]{:S(2)}) collective-permute-start(bf16[128,1280]{1,0:T(8,128)(2,1)S(1)} %pad_maximum_fusion.1), channel_id=1, source_target_pairs={{0,1},{1,0},{2,3},{3,2},{4,5},{5,4},{6,7},{7,6},{8,9},{9,8},{10,11... | collective-permute-start | bytes 983048 | tf_op jit(solution)/shard_map/ppermute | solution.py:350
  5.3 35.0 %copy-start.1 = (bf16[1,1,512,1024]{3,2,1,0:T(8,128)(2,1)S(1)}, bf16[1,1,512,1024]{3,2,1,0:T(8,128)(2,1)}, u32[]{:S(2)}) copy-start(bf16[1,1,512,1024]{3,2,1,0:T(8,128)(2,1)} %param.11) | copy-start | bytes 3145732
  5.3 35.0 %copy-start.4 = (s32[1,512]{1,0:T(1,128)S(1)}, s32[1,512]{1,0:T(1,128)}, u32[]{:S(2)}) copy-start(s32[1,512]{1,0:T(1,128)} %refs_9_.1) | copy-start | bytes 6148
  5.4 25.6 %collective-permute-start.1 = (bf16[128,1280]{1,0:T(8,128)(2,1)S(1)}, bf16[128,1280]{1,0:T(8,128)(2,1)S(1)}, u32[]{:S(2)}, u32[]{:S(2)}) collective-permute-start(bf16[128,1280]{1,0:T(8,128)(2,1)S(1)} %pad_maximum_fusion.2), channel_id=1, source_target_pairs={{0,2},{1,3},{2,0},{3,1},{4,6},{5,7},{6,4},{7,5},{8,10},{9,11},{10,... | collective-permute-start | bytes 983048 | tf_op jit(solution)/shard_map/ppermute | solution.py:350
  8.0 23.0 %collective-permute-start.2 = (bf16[128,1280]{1,0:T(8,128)(2,1)S(1)}, bf16[128,1280]{1,0:T(8,128)(2,1)S(1)}, u32[]{:S(2)}, u32[]{:S(2)}) collective-permute-start(bf16[128,1280]{1,0:T(8,128)(2,1)S(1)} %pad_maximum_fusion.3), channel_id=1, source_target_pairs={{0,3},{1,2},{2,1},{3,0},{4,7},{5,6},{6,5},{7,4},{8,11},{9,10},{10,... | collective-permute-start | bytes 983048 | tf_op jit(solution)/shard_map/ppermute | solution.py:350
  31.0 22.3 %collective-permute-start.3 = (bf16[128,1024]{1,0:T(8,128)(2,1)}, bf16[128,1024]{1,0:T(8,128)(2,1)S(1)}, u32[]{:S(2)}, u32[]{:S(2)}) collective-permute-start(bf16[128,1024]{1,0:T(8,128)(2,1)} %get-tuple-element.20), channel_id=1, source_target_pairs={{0,1},{1,0},{2,3},{3,2},{4,5},{5,4},{6,7},{7,6},{8,9},{9,8},{10,11... | collective-permute-start | bytes 786440 | tf_op jit(solution)/shard_map/ppermute | solution.py:350
  37.2 16.2 %collective-permute-start.4 = (bf16[128,1024]{1,0:T(8,128)(2,1)}, bf16[128,1024]{1,0:T(8,128)(2,1)S(1)}, u32[]{:S(2)}, u32[]{:S(2)}) collective-permute-start(bf16[128,1024]{1,0:T(8,128)(2,1)} %get-tuple-element.21), channel_id=1, source_target_pairs={{0,3},{1,2},{2,1},{3,0},{4,7},{5,6},{6,5},{7,4},{8,11},{9,10},{10,... | collective-permute-start | bytes 786440 | tf_op jit(solution)/shard_map/ppermute | solution.py:350
  53.4 12.1 %collective-permute-start.5 = (bf16[512,256]{1,0:T(8,128)(2,1)}, bf16[512,256]{1,0:T(8,128)(2,1)S(1)}, u32[]{:S(2)}, u32[]{:S(2)}) collective-permute-start(bf16[512,256]{1,0:T(8,128)(2,1)} %get-tuple-element.22.refs_0_), channel_id=1, source_target_pairs={{0,2},{1,3},{2,0},{3,1},{4,6},{5,7},{6,4},{7,5},{8,10},{9,11},{10,... | collective-permute-start | bytes 786440 | tf_op jit(solution)/shard_map/ppermute | solution.py:350
  53.4 18.4 %collective-permute-start.7 = (bf16[512,256]{1,0:T(8,128)(2,1)}, bf16[512,256]{1,0:T(8,128)(2,1)S(1)}, u32[]{:S(2)}, u32[]{:S(2)}) collective-permute-start(bf16[512,256]{1,0:T(8,128)(2,1)} %get-tuple-element.22.refs_0_), channel_id=1, source_target_pairs={{0,1},{1,0},{2,3},{3,2},{4,5},{5,4},{6,7},{7,6},{8,9},{9,8},{10,11... | collective-permute-start | bytes 786440 | tf_op jit(solution)/shard_map/ppermute | solution.py:350
  65.4 15.0 %collective-permute-start.8 = (bf16[512,256]{1,0:T(8,128)(2,1)S(1)}, bf16[512,256]{1,0:T(8,128)(2,1)S(1)}, u32[]{:S(2)}, u32[]{:S(2)}) collective-permute-start(bf16[512,256]{1,0:T(8,128)(2,1)S(1)} %collective-permute-done.5.refs_2_), channel_id=1, source_target_pairs={{0,1},{1,0},{2,3},{3,2},{4,5},{5,4},{6,7},{7,6},{8,9},{9,8},{10,11... | collective-permute-start | bytes 786440 | tf_op jit(solution)/shard_map/ppermute | solution.py:350
  65.4 23.7 %collective-permute-start.6 = (bf16[128,1024]{1,0:T(8,128)(2,1)}, bf16[128,1024]{1,0:T(8,128)(2,1)S(1)}, u32[]{:S(2)}, u32[]{:S(2)}) collective-permute-start(bf16[128,1024]{1,0:T(8,128)(2,1)} %get-tuple-element.24), channel_id=1, source_target_pairs={{0,2},{1,3},{2,0},{3,1},{4,6},{5,7},{6,4},{7,5},{8,10},{9,11},{10,... | collective-permute-start | bytes 786440 | tf_op jit(solution)/shard_map/ppermute | solution.py:350
  68.3 45.9 %all-to-all-start = ((bf16[4,128,1024]{2,1,0:T(8,128)(2,1)}), bf16[4,128,1024]{2,1,0:T(8,128)(2,1)S(1)}, u32[]{:S(2)}, u32[]{:S(2)}) async-start(bf16[4,128,1024]{2,1,0:T(8,128)(2,1)} %bitcast.24), calls=%async_computation | async-start | bytes 2097152 | tf_op jit(solution)/shard_map/all_to_all | solution.py:436
  80.4 0.7 copy-start.2
  81.1 1.6 %copy-start = (bf16[1,1024,1024]{2,1,0:T(8,128)(2,1)S(1)}, bf16[1,1024,1024]{2,1,0:T(8,128)(2,1)}, u32[]{:S(2)}) copy-start(bf16[1,1024,1024]{2,1,0:T(8,128)(2,1)} %param.14) | copy-start | bytes 6291460
  82.7 0.9 copy-start.3
  91.0 21.5 %collective-permute-start.9 = (bf16[1024,512]{1,0:T(8,128)(2,1)S(1)}, bf16[1024,512]{1,0:T(8,128)(2,1)S(1)}, u32[]{:S(2)}, u32[]{:S(2)}) collective-permute-start(bf16[1024,512]{1,0:T(8,128)(2,1)S(1)} %get-tuple-element.27), channel_id=1, source_target_pairs={{0,4},{4,0},{1,5},{5,1},{2,6},{6,2},{3,7},{7,3},{8,12},{12,8},{9,1... | collective-permute-start | bytes 3145736 | tf_op jit(solution)/shard_map/ppermute | solution.py:350
  92.6 9.7 %collective-permute-start.10 = (bf16[128,1024]{1,0:T(8,128)(2,1)S(1)}, bf16[128,1024]{1,0:T(8,128)(2,1)S(1)}, u32[]{:S(2)}, u32[]{:S(2)}) collective-permute-start(bf16[128,1024]{1,0:T(8,128)(2,1)S(1)} %get-tuple-element.29), channel_id=1, source_target_pairs={{8,3},{9,2},{10,1},{11,0},{16,8},{17,9},{18,10},{19,11},{24,19},{2... | collective-permute-start | bytes 786440 | tf_op jit(solution)/shard_map/ppermute | solution.py:370
  93.9 23.0 %collective-permute-start.11 = (bf16[128,1024]{1,0:T(8,128)(2,1)}, bf16[128,1024]{1,0:T(8,128)(2,1)S(1)}, u32[]{:S(2)}, u32[]{:S(2)}) collective-permute-start(bf16[128,1024]{1,0:T(8,128)(2,1)} %get-tuple-element.30), channel_id=1, source_target_pairs={{8,2},{9,3},{10,0},{11,1},{16,10},{17,11},{18,8},{19,9},{24,18},{2... | collective-permute-start | bytes 786440 | tf_op jit(solution)/shard_map/ppermute | solution.py:358
  95.2 21.7 %collective-permute-start.12 = (bf16[128,1024]{1,0:T(8,128)(2,1)S(1)}, bf16[128,1024]{1,0:T(8,128)(2,1)S(1)}, u32[]{:S(2)}, u32[]{:S(2)}) collective-permute-start(bf16[128,1024]{1,0:T(8,128)(2,1)S(1)} %get-tuple-element.31), channel_id=1, source_target_pairs={{8,1},{9,0},{10,3},{11,2},{16,9},{17,8},{18,11},{19,10},{24,17},{2... | collective-permute-start | bytes 786440 | tf_op jit(solution)/shard_map/ppermute | solution.py:358
  96.5 20.4 %collective-permute-start.13 = (bf16[128,1024]{1,0:T(8,128)(2,1)S(1)}, bf16[128,1024]{1,0:T(8,128)(2,1)S(1)}, u32[]{:S(2)}, u32[]{:S(2)}) collective-permute-start(bf16[128,1024]{1,0:T(8,128)(2,1)S(1)} %get-tuple-element.32), channel_id=1, source_target_pairs={{8,0},{9,1},{10,2},{11,3},{16,8},{17,9},{18,10},{19,11},{24,16},{2... | collective-permute-start | bytes 786440 | tf_op jit(solution)/shard_map/ppermute | solution.py:358
  102.3 14.6 %collective-permute-start.14 = (bf16[128,1024]{1,0:T(8,128)(2,1)S(1)}, bf16[128,1024]{1,0:T(8,128)(2,1)S(1)}, u32[]{:S(2)}, u32[]{:S(2)}) collective-permute-start(bf16[128,1024]{1,0:T(8,128)(2,1)S(1)} %collective-permute-done.10.refs_0_), channel_id=1, source_target_pairs={{8,11},{9,10},{10,9},{11,8},{12,15},{13,14},{14,13},{15,12}} | collective-permute-start | bytes 786440 | tf_op jit(solution)/shard_map/ppermute | solution.py:371

commit v3 on v2

--- a/solution.py
+++ b/solution.py
@@ -13,6 +13,7 @@
 KEY_VALUE_HEADS = 4
 HEAD_WIDTH = 128
 QUERY_BLOCK = 256
+HEADS_AT_ONCE = 2
 FEATURE_BLOCK = 256
 MASKED = -1e30
 
@@ -66,7 +67,7 @@
     width = HEAD_WIDTH
     half = width // 2
     block = min(QUERY_BLOCK, tokens)
-    scale = HEAD_WIDTH ** (-0.5)
+    to_exponent = HEAD_WIDTH ** (-0.5) * math.log2(math.e)
     head = pl.program_id(0)
 
     @pl.when(head == 0)
@@ -92,24 +93,28 @@
 
     for start in range(0, tokens, block):
         stop = start + block
-        q = q_ref[start:stop, :]
-        g = g_s[start:stop, :]
-        scores = dot(k_s[:stop, :], q, NT) * scale + bias_s[:stop, start:stop]
-        top = jnp.max(scores, 0, keepdims=True)
-        shifted = jnp.exp(scores - top)
-        total = jnp.sum(shifted, 0, keepdims=True)
-        attention = shifted * (1.0 / total)
-        dprobs = dot(v_s[:stop, :], g, NT)
-        delta = jnp.sum(attention * dprobs, 0, keepdims=True)
-        dscores = (attention * (dprobs - delta)).astype(jnp.bfloat16)
-        dv_s[:stop, :] += dot(attention.astype(jnp.bfloat16), g, NN)
-        dk_s[:stop, :] += dot(dscores, q, NN)
-        dq = dot(kt_s[:, :stop], dscores, NN)
         c = cos_ref[:, start:stop]
         t = sin_ref[:, start:stop]
-        u, w = dq[:half], dq[half:]
-        turned = jnp.concatenate([u * c + w * t, w * c - u * t], 0)
-        dq_ref[start:stop, :] = turned.T.astype(jnp.bfloat16)
+        grad_k, grad_v = [], []
+        for lane in range(0, g_s.shape[1], width):
+            q = q_ref[start:stop, lane : lane + width]
+            g = g_s[start:stop, lane : lane + width]
+            scores = dot(k_s[:stop, :], q, NT) * to_exponent + bias_s[:stop, start:stop]
+            top = jnp.max(scores, 0, keepdims=True)
+            shifted = jnp.exp2(scores - top)
+            total = jnp.sum(shifted, 0, keepdims=True)
+            attention = shifted * (1.0 / total)
+            dprobs = dot(v_s[:stop, :], g, NT)
+            delta = jnp.sum(attention * dprobs, 0, keepdims=True)
+            dscores = (attention * (dprobs - delta)).astype(jnp.bfloat16)
+            grad_v.append(dot(attention.astype(jnp.bfloat16), g, NN))
+            grad_k.append(dot(dscores, q, NN))
+            dq = dot(kt_s[:, :stop], dscores, NN)
+            u, w = dq[:half], dq[half:]
+            turned = jnp.concatenate([u * c + w * t, w * c - u * t], 0)
+            dq_ref[start:stop, lane : lane + width] = turned.T.astype(jnp.bfloat16)
+        dv_s[:stop, :] += sum(grad_v[1:], grad_v[0])
+        dk_s[:stop, :] += sum(grad_k[1:], grad_k[0])
 
     @pl.when(head == pl.num_programs(0) - 1)
     def _():
@@ -127,6 +132,7 @@
     tokens, cols = queries.shape
     width = HEAD_WIDTH
     heads = cols // width
+    step = min(HEADS_AT_ONCE, heads) * width
     piece_rows = tokens // n
     bf16, f32 = jnp.bfloat16, jnp.float32
     return pl.pallas_call(
@@ -137,17 +143,17 @@
         ],
         grid_spec=pltpu.PrefetchScalarGridSpec(
             num_scalar_prefetch=1,
-            grid=(heads,),
-            in_specs=[pl.BlockSpec((piece_rows, width), lambda h, p: (0, h))] * n
+            grid=(cols // step,),
+            in_specs=[pl.BlockSpec((piece_rows, step), lambda h, p: (0, h))] * n
             + [pl.BlockSpec((piece_rows, 2 * width), lambda h, p: (0, cols // (2 * width)))] * n
             + [
-                pl.BlockSpec((tokens, width), lambda h, p: (0, h)),
+                pl.BlockSpec((tokens, step), lambda h, p: (0, h)),
                 pl.BlockSpec((1, tokens), lambda h, p: (0, 0)),
                 pl.BlockSpec((width // 2, tokens), lambda h, p: (0, 0)),
                 pl.BlockSpec((width // 2, tokens), lambda h, p: (0, 0)),
             ],
             out_specs=[
-                pl.BlockSpec((tokens, width), lambda h, p: (0, h)),
+                pl.BlockSpec((tokens, step), lambda h, p: (0, h)),
                 pl.BlockSpec((tokens, 2 * width), lambda h, p: (0, 0)),
             ],
             scratch_shapes=[
@@ -155,7 +161,7 @@
                 pltpu.VMEM((tokens, width), bf16),
                 pltpu.VMEM((width, tokens), bf16),
                 pltpu.VMEM((tokens, tokens), f32),
-                pltpu.VMEM((tokens, width), bf16),
+                pltpu.VMEM((tokens, step), bf16),
                 pltpu.VMEM((tokens, width), f32),
                 pltpu.VMEM((tokens, width), f32),
             ],
@@ -191,24 +197,26 @@
         copy.start()
     if share > 1:
         total[...] = jnp.zeros_like(total)
-    for m in range(n):
-        head = pos_ref[m] // share
-        for side in range(2):
-            cols = pl.ds(pl.multiple_of(side * kv_width + head * width, width), width)
-            part = part_refs[m][:, side * width : (side + 1) * width]
-            if share > 1:
-                total[:, cols] += part.astype(jnp.float32)
-            else:
-                total[:, cols] = part
+    for source in range(n):
+        head = pos_ref[source] // share
+        for m in range(n):
+            rows = slice(m * piece_rows, (m + 1) * piece_rows)
+            part = part_refs[source][rows_at(pos_ref, m, piece_rows), :]
+            for side in range(2):
+                cols = pl.ds(pl.multiple_of(side * kv_width + head * width, width), width)
+                own = part[:, side * width : (side + 1) * width]
+                if share > 1:
+                    total[rows, cols] += own.astype(jnp.float32)
+                else:
+                    total[rows, cols] = own
     if share > 1:
         kv_ref[...] = total[...].astype(kv_ref.dtype)
     for b, copy in enumerate(copies):
         copy.wait()
+        cols = slice(b * block, (b + 1) * block)
+        product = dot(kv_ref[...], weight_s[b], NT).astype(jnp.bfloat16)
         for m in range(n):
-            rows = kv_ref[rows_at(pos_ref, m, piece_rows), :]
-            out_refs[m][:, b * block : (b + 1) * block] = dot(rows, weight_s[b], NT).astype(
-                jnp.bfloat16
-            )
+            out_refs[m][:, cols] = product[m * piece_rows : (m + 1) * piece_rows]
 
 
 def input_gradient(pos, parts, weight, share):
@@ -238,7 +246,7 @@
             transcendentals=0,
         ),
         name="input_gradient",
-    )(pos, *parts, weight)
+    )(pos, *parts, pltpu.with_memory_space_constraint(weight, pltpu.HBM))
     return out[:n], out[n]
 
 
@@ -247,7 +255,7 @@
     out_refs, x_s = refs[n + 1 : -1], refs[-1]
     piece_rows = x_refs[0].shape[0]
     for m in range(n):
-        x_s[rows_at(pos_ref, m, piece_rows), :] = x_refs[m][...]
+        x_s[m * piece_rows : (m + 1) * piece_rows, :] = x_refs[m][...]
     if halves:
         cols = kv_ref.shape[1] // 2
         mine = pos_ref[n]
@@ -420,18 +428,19 @@
     far, near = n // 2, 1
     middle = [m for m in masks if m not in (far, near)]
     x_held = after(x_out, pieces)
-    x_sent = {m: swapped(x_held[m], m) for m in [*middle, near]}
+    x_sent = {m: swapped(x_held[m], m) for m in [*middle, far]}
+    x_sent[near] = swapped(x_out[near], near)
 
     dq, dkv = attention_backward(pos, pieces, queries[0, 0], segments, cosine, sine)
-    dkv = after(dkv, x_sent)
+    dkv = after(dkv, [x_sent[m] for m in [near, *middle]])
 
     parts = {0: dkv}
     bit = far
     while bit:
         for m in sorted(parts):
-            parts[m | bit] = swapped(parts[m], bit)
+            held = after(parts[m], x_sent) if m else parts[m]
+            parts[m | bit] = swapped(held, bit)
         bit //= 2
-    x_sent[far] = swapped(after(x_out[far], parts[far]), far)
     dq = after(dq, parts[far])
     dq = lax.all_to_all(dq.reshape(n, tokens // n, cols), "ctx", 0, 0, tiled=True)
     parts = [parts[m] for m in range(n)]

time: 120 us -> 118 us (0.983)
  starting transfers between devices: 30.3 us -> 34.7 us
  waiting for transfers between devices: 56.2 us -> 53.5 us
  local copies, waits for them, and re-layouts: 5.69 us -> 3.17 us
  Pallas kernels: 23.1 us -> 21.1 us
    ppermute x10, waiting for transfers between devices: 50.1 us -> 45.4 us  [swapped(): return lax.ppermute(value, axis, [(i, i ^ mask) for i in range(size)])]
    ppermute x10, starting transfers between devices: 20.9 us -> 24.7 us  [swapped(): return lax.ppermute(value, axis, [(i, i ^ mask) for i in range(size)])]
    unnamed x20 -> x18, local copies, waits for them, and re-layouts: 3.27 us -> 0.74 us
    pallas_call x1, Pallas kernels: 13.1 us -> 10.8 us  [attention_backward(): pl.pallas_call(functools.partial(attention_kernel, n), out_shape=[jax.Sha...]
    ppermute x3, waiting for transfers between devices: 1.66 us -> 3.68 us  [to_section_before(): return lax.ppermute(value, ('section', 'ctx'), pairs)]
  transfers between devices with their start and end apart: 16 -> 16, of which waited for: 7 -> 8; matrix products, arithmetic and copies ran while one was open for 3% -> 3% of each run, Pallas kernels for 18% -> 17%
where the time goes in v3:
time: 118 us; the launch traced here: 116 us
  waiting for transfers between devices  53.5 us (45%)
  starting transfers between devices  34.7 us (29%)
  Pallas kernels  21.1 us (18%)
  local copies, waits for them, and re-layouts  3.17 us (3%)
  other arithmetic  2.3 us (2%)
    ppermute x10, waiting for transfers between devices, swapped(): return lax.ppermute(value, axis, [(i, i ^ mask) for i in range(size)])  45.4 us
    ppermute x10, starting transfers between devices, swapped(): return lax.ppermute(value, axis, [(i, i ^ mask) for i in range(size)])  24.7 us
    pallas_call x1, Pallas kernels, attention_backward(): pl.pallas_call(functools.partial(attention_kernel, n), out_shape=[jax.Sha...  10.8 us
    pallas_call x1, Pallas kernels, input_gradient(): pl.pallas_call(functools.partial(input_kernel, n, share), out_shape=[jax....  5.85 us
    ppermute x1, waiting for transfers between devices, relayed_section_before(): value = lax.ppermute(value, ('section', 'ctx'), first)  4.5 us
    all_to_all x1, starting transfers between devices, on_device(): lax.all_to_all(dq.reshape(n, tokens // n, cols), 'ctx', 0, 0, tiled=True)  4.17 us
    ppermute x3, starting transfers between devices, to_section_before(): return lax.ppermute(value, ('section', 'ctx'), pairs)  3.88 us
    ppermute x3, waiting for transfers between devices, to_section_before(): return lax.ppermute(value, ('section', 'ctx'), pairs)  3.68 us
  transfers between devices with their start and end apart: 16, of which 8 were waited for; matrix products, arithmetic and copies ran while one was open for 3% of the time, Pallas kernels for 17%

profile of v3, /device:TPU:0, one launch (start us, length us, event | category | flops | bytes accessed | tf_op | source)
XLA Modules:
  0.0 115.7 jit_solution(15067361443791049153)
XLA Ops:
  0.7 1.4 %dynamic-slice_bitcast_fusion.4 = (bf16[128,1024]{1,0:T(8,128)(2,1)S(1)}, bf16[128,1024]{1,0:T(8,128)(2,1)S(1)}, bf16[128,1024]{1,0:T(8,128)(2,1)S(1)}, bf16[128,1024]{1,0:T(8,128)(2,1)S(1)}) fusion(bf16[1,1,128,4096]{3,2,1,0:T(8,128)(2,1)} %param.10, s32[]{:T(128)S(6)} %select_n.44, s32[]{:T(128)S(6)} %select_n.40, s32[]{:T(128)S(6)} %select_n.38, ...), kind=kLoop, calls=%fused_computation.9 | loop fusion | bytes 2097168 | tf_op jit(solution)/shard_map/dynamic_slice | solution.py:405
  2.2 3.1 %collective-permute-start = (bf16[128,1280]{1,0:T(8,128)(2,1)S(1)}, bf16[128,1280]{1,0:T(8,128)(2,1)S(1)}, u32[]{:S(2)}, u32[]{:S(2)}) collective-permute-start(bf16[128,1280]{1,0:T(8,128)(2,1)S(1)} %pad_maximum_fusion.1), channel_id=1, source_target_pairs={{0,1},{1,0},{2,3},{3,2},{4,5},{5,4},{6,7},{7,6},{8,9},{9,8},{10,11... | collective-permute-start | bytes 983048 | tf_op jit(solution)/shard_map/ppermute | solution.py:358
  5.3 2.7 %collective-permute-start.1 = (bf16[128,1280]{1,0:T(8,128)(2,1)S(1)}, bf16[128,1280]{1,0:T(8,128)(2,1)S(1)}, u32[]{:S(2)}, u32[]{:S(2)}) collective-permute-start(bf16[128,1280]{1,0:T(8,128)(2,1)S(1)} %pad_maximum_fusion.2), channel_id=1, source_target_pairs={{0,2},{1,3},{2,0},{3,1},{4,6},{5,7},{6,4},{7,5},{8,10},{9,11},{10,... | collective-permute-start | bytes 983048 | tf_op jit(solution)/shard_map/ppermute | solution.py:358
  8.1 0.9 dynamic-slice_bitcast_fusion
  9.0 0.9 collective-permute-start.3
  9.9 10.1 %collective-permute-done.refs_1_.refs_5_ = bf16[128,1280]{1,0:T(8,128)(2,1)S(1)} collective-permute-done((bf16[128,1280]{1,0:T(8,128)(2,1)S(1)}, bf16[128,1280]{1,0:T(8,128)(2,1)S(1)}, u32[]{:S(2)}, u32[]{:S(2)}) %collective-permute-start) | collective-permute-done | bytes 327712 | tf_op jit(solution)/shard_map/ppermute | solution.py:358
  20.1 11.0 %collective-permute-done.1.refs_2_.refs_6_ = bf16[128,1280]{1,0:T(8,128)(2,1)S(1)} collective-permute-done((bf16[128,1280]{1,0:T(8,128)(2,1)S(1)}, bf16[128,1280]{1,0:T(8,128)(2,1)S(1)}, u32[]{:S(2)}, u32[]{:S(2)}) %collective-permute-start.1) | collective-permute-done | bytes 327712 | tf_op jit(solution)/shard_map/ppermute | solution.py:358
  31.0 2.5 %collective-permute-start.4 = (bf16[128,1024]{1,0:T(8,128)(2,1)}, bf16[128,1024]{1,0:T(8,128)(2,1)S(1)}, u32[]{:S(2)}, u32[]{:S(2)}) collective-permute-start(bf16[128,1024]{1,0:T(8,128)(2,1)} %get-tuple-element.20), channel_id=1, source_target_pairs={{0,3},{1,2},{2,1},{3,0},{4,7},{5,6},{6,5},{7,4},{8,11},{9,10},{10,... | collective-permute-start | bytes 786440 | tf_op jit(solution)/shard_map/ppermute | solution.py:358
  33.5 0.5 fusion.1
  34.2 10.8 %collective-permute-start.6 = (bf16[128,1024]{1,0:T(8,128)(2,1)}, bf16[128,1024]{1,0:T(8,128)(2,1)S(1)}, u32[]{:S(2)}, u32[]{:S(2)}) collective-permute-start(bf16[128,1024]{1,0:T(8,128)(2,1)} %get-tuple-element.23), channel_id=1, source_target_pairs={{0,2},{1,3},{2,0},{3,1},{4,6},{5,7},{6,4},{7,5},{8,10},{9,11},{10,... | collective-permute-start | bytes 786440 | tf_op jit(solution)/shard_map/ppermute | solution.py:358
  44.9 10.8 %attention_backward.1 = (bf16[512,1024]{1,0:T(8,128)(2,1)}, bf16[512,256]{1,0:T(8,128)(2,1)}) custom-call(s32[6]{0:T(128)S(1)} %stack.31.pos_ref, bf16[128,1280]{1,0:T(8,128)(2,1)S(1)} %pad_maximum_fusion.refs_0_.refs_4_, bf16[128,1280]{1,0:T(8,128)(2,1)S(1)} %collective-permute-done.refs_1_.refs_5_, ...), custom_call_target="tpu_custom_call" | custom-call | flops 2684354560 | bytes 3145728 | tf_op jit(solution)/shard_map/attention_backward/pallas_call | solution.py:138
  55.8 2.6 %collective-permute-start.5 = (bf16[512,256]{1,0:T(8,128)(2,1)}, bf16[512,256]{1,0:T(8,128)(2,1)S(1)}, u32[]{:S(2)}, u32[]{:S(2)}) collective-permute-start(bf16[512,256]{1,0:T(8,128)(2,1)} %get-tuple-element.21.refs_0_), channel_id=1, source_target_pairs={{0,2},{1,3},{2,0},{3,1},{4,6},{5,7},{6,4},{7,5},{8,10},{9,11},{10,... | collective-permute-start | bytes 786440 | tf_op jit(solution)/shard_map/ppermute | solution.py:358
  58.4 0.5 collective-permute-start.7
  58.9 9.8 %collective-permute-done.6.refs_2_ = bf16[128,1024]{1,0:T(8,128)(2,1)S(1)} collective-permute-done((bf16[128,1024]{1,0:T(8,128)(2,1)}, bf16[128,1024]{1,0:T(8,128)(2,1)S(1)}, u32[]{:S(2)}, u32[]{:S(2)}) %collective-permute-start.6) | collective-permute-done | bytes 262176 | tf_op jit(solution)/shard_map/ppermute | solution.py:358
  68.7 0.7 copy-done.1
  69.4 2.6 %collective-permute-done.5.refs_2_ = bf16[512,256]{1,0:T(8,128)(2,1)S(1)} collective-permute-done((bf16[512,256]{1,0:T(8,128)(2,1)}, bf16[512,256]{1,0:T(8,128)(2,1)S(1)}, u32[]{:S(2)}, u32[]{:S(2)}) %collective-permute-start.5) | collective-permute-done | bytes 262176 | tf_op jit(solution)/shard_map/ppermute | solution.py:358
  72.0 4.2 %all-to-all-start = ((bf16[4,128,1024]{2,1,0:T(8,128)(2,1)}), bf16[4,128,1024]{2,1,0:T(8,128)(2,1)S(1)}, u32[]{:S(2)}, u32[]{:S(2)}) async-start(bf16[4,128,1024]{2,1,0:T(8,128)(2,1)} %bitcast.24), calls=%async_computation | async-start | bytes 2097152 | tf_op jit(solution)/shard_map/all_to_all | solution.py:445
  76.2 7.8 %collective-permute-done.8.refs_3_ = bf16[512,256]{1,0:T(8,128)(2,1)S(1)} collective-permute-done((bf16[512,256]{1,0:T(8,128)(2,1)S(1)}, bf16[512,256]{1,0:T(8,128)(2,1)S(1)}, u32[]{:S(2)}, u32[]{:S(2)}) %collective-permute-start.8) | collective-permute-done | bytes 262176 | tf_op jit(solution)/shard_map/ppermute | solution.py:358
  83.9 5.8 %input_gradient.1 = (bf16[128,1024]{1,0:T(8,128)(2,1)S(1)}, bf16[128,1024]{1,0:T(8,128)(2,1)}, bf16[128,1024]{1,0:T(8,128)(2,1)}, bf16[128,1024]{1,0:T(8,128)(2,1)S(1)}, bf16[512,1024]{1,0:T(8,128)(2,1)S(1)}) custom-call(s32[6]{0:T(128)S(1)} %stack.31.pos_ref, bf16[512,256]{1,0:T(8,128)(2,1)} %get-tuple-element.21.refs_0_, ...), custom_call_target="tpu_custom_call" | custom-call | flops 1073741824 | bytes 5242880 | tf_op jit(solution)/shard_map/input_gradient/pallas_call | solution.py:229
  89.8 1.8 %weight_gradient.1 = (bf16[1024,512]{1,0:T(8,128)(2,1)S(1)}, f32[1024,512]{1,0:T(8,128)S(1)}) custom-call(s32[6]{0:T(128)S(1)} %stack.31.pos_ref, bf16[128,1024]{1,0:T(8,128)(2,1)S(1)} %get-tuple-element.34.refs_0_, bf16[128,1024]{1,0:T(8,128)(2,1)S(1)} %collective-permute-done.3.refs_1_, bf16[128,1024]{1,0:T(8,128)(2,1)S(1)} %copy-done.2, ...), custom_call_target="tpu_custom_call" | custom-call | flops 1073741824 | bytes 6291456 | tf_op jit(solution)/shard_map/weight_gradient/pallas_call | solution.py:281
  91.6 1.6 %collective-permute-start.9 = (bf16[1024,512]{1,0:T(8,128)(2,1)S(1)}, bf16[1024,512]{1,0:T(8,128)(2,1)S(1)}, u32[]{:S(2)}, u32[]{:S(2)}) collective-permute-start(bf16[1024,512]{1,0:T(8,128)(2,1)S(1)} %get-tuple-element.27), channel_id=1, source_target_pairs={{0,4},{4,0},{1,5},{5,1},{2,6},{6,2},{3,7},{7,3},{8,12},{12,8},{9,1... | collective-permute-start | bytes 3145736 | tf_op jit(solution)/shard_map/ppermute | solution.py:358
  93.3 1.3 %collective-permute-start.10 = (bf16[128,1024]{1,0:T(8,128)(2,1)S(1)}, bf16[128,1024]{1,0:T(8,128)(2,1)S(1)}, u32[]{:S(2)}, u32[]{:S(2)}) collective-permute-start(bf16[128,1024]{1,0:T(8,128)(2,1)S(1)} %get-tuple-element.29), channel_id=1, source_target_pairs={{8,3},{9,2},{10,1},{11,0},{16,8},{17,9},{18,10},{19,11},{24,19},{2... | collective-permute-start | bytes 786440 | tf_op jit(solution)/shard_map/ppermute | solution.py:378
  94.5 1.3 %collective-permute-start.11 = (bf16[128,1024]{1,0:T(8,128)(2,1)}, bf16[128,1024]{1,0:T(8,128)(2,1)S(1)}, u32[]{:S(2)}, u32[]{:S(2)}) collective-permute-start(bf16[128,1024]{1,0:T(8,128)(2,1)} %get-tuple-element.30), channel_id=1, source_target_pairs={{8,2},{9,3},{10,0},{11,1},{16,10},{17,11},{18,8},{19,9},{24,18},{2... | collective-permute-start | bytes 786440 | tf_op jit(solution)/shard_map/ppermute | solution.py:366
  95.8 1.3 %collective-permute-start.12 = (bf16[128,1024]{1,0:T(8,128)(2,1)}, bf16[128,1024]{1,0:T(8,128)(2,1)S(1)}, u32[]{:S(2)}, u32[]{:S(2)}) collective-permute-start(bf16[128,1024]{1,0:T(8,128)(2,1)} %get-tuple-element.31), channel_id=1, source_target_pairs={{8,1},{9,0},{10,3},{11,2},{16,9},{17,8},{18,11},{19,10},{24,17},{2... | collective-permute-start | bytes 786440 | tf_op jit(solution)/shard_map/ppermute | solution.py:366
  97.1 1.3 %collective-permute-start.13 = (bf16[128,1024]{1,0:T(8,128)(2,1)S(1)}, bf16[128,1024]{1,0:T(8,128)(2,1)S(1)}, u32[]{:S(2)}, u32[]{:S(2)}) collective-permute-start(bf16[128,1024]{1,0:T(8,128)(2,1)S(1)} %get-tuple-element.32), channel_id=1, source_target_pairs={{8,0},{9,1},{10,2},{11,3},{16,8},{17,9},{18,10},{19,11},{24,16},{2... | collective-permute-start | bytes 786440 | tf_op jit(solution)/shard_map/ppermute | solution.py:366
  98.4 4.5 %collective-permute-done.10.refs_0_ = bf16[128,1024]{1,0:T(8,128)(2,1)S(1)} collective-permute-done((bf16[128,1024]{1,0:T(8,128)(2,1)S(1)}, bf16[128,1024]{1,0:T(8,128)(2,1)S(1)}, u32[]{:S(2)}, u32[]{:S(2)}) %collective-permute-start.10) | collective-permute-done | bytes 262176 | tf_op jit(solution)/shard_map/ppermute | solution.py:378
  102.9 0.7 collective-permute-start.14
  103.6 4.1 %collective-permute-done.9 = bf16[1024,512]{1,0:T(8,128)(2,1)S(1)} collective-permute-done((bf16[1024,512]{1,0:T(8,128)(2,1)S(1)}, bf16[1024,512]{1,0:T(8,128)(2,1)S(1)}, u32[]{:S(2)}, u32[]{:S(2)}) %collective-permute-start.9) | collective-permute-done | bytes 1048608 | tf_op jit(solution)/shard_map/ppermute | solution.py:358
  107.7 1.7 %add_multiply_fusion = f32[1024,512]{1,0:T(8,128)} fusion(f32[1024,512]{1,0:T(8,128)S(1)} %get-tuple-element.26, bf16[1024,512]{1,0:T(8,128)(2,1)S(1)} %collective-permute-done.9), kind=kLoop, calls=%fused_computation | loop fusion | flops 1572864 | bytes 5242880 | tf_op jit(solution)/shard_map/div | solution.py:461
  109.4 1.0 lay_out.1
  110.4 3.7 %collective-permute-done.11.refs_1_ = bf16[128,1024]{1,0:T(8,128)(2,1)S(1)} collective-permute-done((bf16[128,1024]{1,0:T(8,128)(2,1)}, bf16[128,1024]{1,0:T(8,128)(2,1)S(1)}, u32[]{:S(2)}, u32[]{:S(2)}) %collective-permute-start.11) | collective-permute-done | bytes 262176 | tf_op jit(solution)/shard_map/ppermute | solution.py:366
  114.1 1.6 %join_columns.1 = bf16[128,4096]{1,0:T(8,128)(2,1)} custom-call(s32[6]{0:T(128)S(1)} %stack.31.pos_ref, bf16[128,1024]{1,0:T(8,128)(2,1)S(1)} %collective-permute-done.10.refs_0_, bf16[128,1024]{1,0:T(8,128)(2,1)S(1)} %collective-permute-done.11.refs_1_, bf16[128,1024]{1,0:T(8,128)(2,1)S(1)} %collective-permute-done.12.refs_2_, ...), custom_call_target="tpu_custom_call" | custom-call | bytes 2097152 | tf_op jit(solution)/shard_map/join_columns/pallas_call | solution.py:321
  (34 shorter events, 0.4 us)
Async XLA Ops:
  0.6 1.4 %copy-start.5 = (bf16[1,1,128,512]{3,2,1,0:T(8,128)(2,1)S(1)}, bf16[1,1,128,512]{3,2,1,0:T(8,128)(2,1)}, u32[]{:S(2)}) copy-start(bf16[1,1,128,512]{3,2,1,0:T(8,128)(2,1)} %param.13) | copy-start | bytes 393220
  0.6 1.4 %copy-start.6 = (bf16[1,1,128,512]{3,2,1,0:T(8,128)(2,1)S(1)}, bf16[1,1,128,512]{3,2,1,0:T(8,128)(2,1)}, u32[]{:S(2)}) copy-start(bf16[1,1,128,512]{3,2,1,0:T(8,128)(2,1)} %param.12) | copy-start | bytes 393220
  0.7 7.4 %copy-start.4 = (bf16[1,1,128,4096]{3,2,1,0:T(8,128)(2,1)S(1)}, bf16[1,1,128,4096]{3,2,1,0:T(8,128)(2,1)}, u32[]{:S(2)}) copy-start(bf16[1,1,128,4096]{3,2,1,0:T(8,128)(2,1)} %param.9) | copy-start | bytes 3145732
  2.2 7.7 %copy-start.7 = (s32[1,512]{1,0:T(1,128)S(1)}, s32[1,512]{1,0:T(1,128)}, u32[]{:S(2)}) copy-start(s32[1,512]{1,0:T(1,128)} %param.16) | copy-start | bytes 6148
  2.2 31.3 %copy-start.8 = (f32[64]{0:T(128)S(1)}, f32[64]{0:T(128)}, u32[]{:S(2)}) copy-start(f32[64]{0:T(128)} %constant.91) | copy-start | bytes 772
  2.2 17.8 %collective-permute-start = (bf16[128,1280]{1,0:T(8,128)(2,1)S(1)}, bf16[128,1280]{1,0:T(8,128)(2,1)S(1)}, u32[]{:S(2)}, u32[]{:S(2)}) collective-permute-start(bf16[128,1280]{1,0:T(8,128)(2,1)S(1)} %pad_maximum_fusion.1), channel_id=1, source_target_pairs={{0,1},{1,0},{2,3},{3,2},{4,5},{5,4},{6,7},{7,6},{8,9},{9,8},{10,11... | collective-permute-start | bytes 983048 | tf_op jit(solution)/shard_map/ppermute | solution.py:358
  5.3 39.6 %copy-start = (bf16[1,1,512,1024]{3,2,1,0:T(8,128)(2,1)S(1)}, bf16[1,1,512,1024]{3,2,1,0:T(8,128)(2,1)}, u32[]{:S(2)}) copy-start(bf16[1,1,512,1024]{3,2,1,0:T(8,128)(2,1)} %param.11) | copy-start | bytes 3145732
  5.3 39.6 %copy-start.3 = (s32[1,512]{1,0:T(1,128)S(1)}, s32[1,512]{1,0:T(1,128)}, u32[]{:S(2)}) copy-start(s32[1,512]{1,0:T(1,128)} %refs_9_.1) | copy-start | bytes 6148
  5.3 25.7 %collective-permute-start.1 = (bf16[128,1280]{1,0:T(8,128)(2,1)S(1)}, bf16[128,1280]{1,0:T(8,128)(2,1)S(1)}, u32[]{:S(2)}, u32[]{:S(2)}) collective-permute-start(bf16[128,1280]{1,0:T(8,128)(2,1)S(1)} %pad_maximum_fusion.2), channel_id=1, source_target_pairs={{0,2},{1,3},{2,0},{3,1},{4,6},{5,7},{6,4},{7,5},{8,10},{9,11},{10,... | collective-permute-start | bytes 983048 | tf_op jit(solution)/shard_map/ppermute | solution.py:358
  8.0 23.0 %collective-permute-start.2 = (bf16[128,1280]{1,0:T(8,128)(2,1)S(1)}, bf16[128,1280]{1,0:T(8,128)(2,1)S(1)}, u32[]{:S(2)}, u32[]{:S(2)}) collective-permute-start(bf16[128,1280]{1,0:T(8,128)(2,1)S(1)} %pad_maximum_fusion.3), channel_id=1, source_target_pairs={{0,3},{1,2},{2,1},{3,0},{4,7},{5,6},{6,5},{7,4},{8,11},{9,10},{10,... | collective-permute-start | bytes 983048 | tf_op jit(solution)/shard_map/ppermute | solution.py:358
  9.0 46.7 %collective-permute-start.3 = (bf16[128,1024]{1,0:T(8,128)(2,1)}, bf16[128,1024]{1,0:T(8,128)(2,1)S(1)}, u32[]{:S(2)}, u32[]{:S(2)}) collective-permute-start(bf16[128,1024]{1,0:T(8,128)(2,1)} %get-tuple-element.35), channel_id=1, source_target_pairs={{0,1},{1,0},{2,3},{3,2},{4,5},{5,4},{6,7},{7,6},{8,9},{9,8},{10,11... | collective-permute-start | bytes 786440 | tf_op jit(solution)/shard_map/ppermute | solution.py:358
  31.0 24.7 %collective-permute-start.4 = (bf16[128,1024]{1,0:T(8,128)(2,1)}, bf16[128,1024]{1,0:T(8,128)(2,1)S(1)}, u32[]{:S(2)}, u32[]{:S(2)}) collective-permute-start(bf16[128,1024]{1,0:T(8,128)(2,1)} %get-tuple-element.20), channel_id=1, source_target_pairs={{0,3},{1,2},{2,1},{3,0},{4,7},{5,6},{6,5},{7,4},{8,11},{9,10},{10,... | collective-permute-start | bytes 786440 | tf_op jit(solution)/shard_map/ppermute | solution.py:358
  34.2 34.5 %collective-permute-start.6 = (bf16[128,1024]{1,0:T(8,128)(2,1)}, bf16[128,1024]{1,0:T(8,128)(2,1)S(1)}, u32[]{:S(2)}, u32[]{:S(2)}) collective-permute-start(bf16[128,1024]{1,0:T(8,128)(2,1)} %get-tuple-element.23), channel_id=1, source_target_pairs={{0,2},{1,3},{2,0},{3,1},{4,6},{5,7},{6,4},{7,5},{8,10},{9,11},{10,... | collective-permute-start | bytes 786440 | tf_op jit(solution)/shard_map/ppermute | solution.py:358
  55.8 16.2 %collective-permute-start.5 = (bf16[512,256]{1,0:T(8,128)(2,1)}, bf16[512,256]{1,0:T(8,128)(2,1)S(1)}, u32[]{:S(2)}, u32[]{:S(2)}) collective-permute-start(bf16[512,256]{1,0:T(8,128)(2,1)} %get-tuple-element.21.refs_0_), channel_id=1, source_target_pairs={{0,2},{1,3},{2,0},{3,1},{4,6},{5,7},{6,4},{7,5},{8,10},{9,11},{10,... | collective-permute-start | bytes 786440 | tf_op jit(solution)/shard_map/ppermute | solution.py:358
  58.4 17.7 %collective-permute-start.7 = (bf16[512,256]{1,0:T(8,128)(2,1)}, bf16[512,256]{1,0:T(8,128)(2,1)S(1)}, u32[]{:S(2)}, u32[]{:S(2)}) collective-permute-start(bf16[512,256]{1,0:T(8,128)(2,1)} %get-tuple-element.21.refs_0_), channel_id=1, source_target_pairs={{0,1},{1,0},{2,3},{3,2},{4,5},{5,4},{6,7},{7,6},{8,9},{9,8},{10,11... | collective-permute-start | bytes 786440 | tf_op jit(solution)/shard_map/ppermute | solution.py:358
  68.7 0.7 copy-start.1
  72.0 11.9 %collective-permute-start.8 = (bf16[512,256]{1,0:T(8,128)(2,1)S(1)}, bf16[512,256]{1,0:T(8,128)(2,1)S(1)}, u32[]{:S(2)}, u32[]{:S(2)}) collective-permute-start(bf16[512,256]{1,0:T(8,128)(2,1)S(1)} %collective-permute-done.5.refs_2_), channel_id=1, source_target_pairs={{0,1},{1,0},{2,3},{3,2},{4,5},{5,4},{6,7},{7,6},{8,9},{9,8},{10,11... | collective-permute-start | bytes 786440 | tf_op jit(solution)/shard_map/ppermute | solution.py:358
  72.0 37.4 %all-to-all-start = ((bf16[4,128,1024]{2,1,0:T(8,128)(2,1)}), bf16[4,128,1024]{2,1,0:T(8,128)(2,1)S(1)}, u32[]{:S(2)}, u32[]{:S(2)}) async-start(bf16[4,128,1024]{2,1,0:T(8,128)(2,1)} %bitcast.24), calls=%async_computation | async-start | bytes 2097152 | tf_op jit(solution)/shard_map/all_to_all | solution.py:445
  76.1 13.6 %copy-start.2 = (bf16[128,1024]{1,0:T(8,128)(2,1)S(1)}, bf16[128,1024]{1,0:T(8,128)(2,1)}, u32[]{:S(2)}) copy-start(bf16[128,1024]{1,0:T(8,128)(2,1)} %copy-done.1) | copy-start | bytes 786436
  91.6 16.1 %collective-permute-start.9 = (bf16[1024,512]{1,0:T(8,128)(2,1)S(1)}, bf16[1024,512]{1,0:T(8,128)(2,1)S(1)}, u32[]{:S(2)}, u32[]{:S(2)}) collective-permute-start(bf16[1024,512]{1,0:T(8,128)(2,1)S(1)} %get-tuple-element.27), channel_id=1, source_target_pairs={{0,4},{4,0},{1,5},{5,1},{2,6},{6,2},{3,7},{7,3},{8,12},{12,8},{9,1... | collective-permute-start | bytes 3145736 | tf_op jit(solution)/shard_map/ppermute | solution.py:358
  93.3 9.7 %collective-permute-start.10 = (bf16[128,1024]{1,0:T(8,128)(2,1)S(1)}, bf16[128,1024]{1,0:T(8,128)(2,1)S(1)}, u32[]{:S(2)}, u32[]{:S(2)}) collective-permute-start(bf16[128,1024]{1,0:T(8,128)(2,1)S(1)} %get-tuple-element.29), channel_id=1, source_target_pairs={{8,3},{9,2},{10,1},{11,0},{16,8},{17,9},{18,10},{19,11},{24,19},{2... | collective-permute-start | bytes 786440 | tf_op jit(solution)/shard_map/ppermute | solution.py:378
  94.5 19.5 %collective-permute-start.11 = (bf16[128,1024]{1,0:T(8,128)(2,1)}, bf16[128,1024]{1,0:T(8,128)(2,1)S(1)}, u32[]{:S(2)}, u32[]{:S(2)}) collective-permute-start(bf16[128,1024]{1,0:T(8,128)(2,1)} %get-tuple-element.30), channel_id=1, source_target_pairs={{8,2},{9,3},{10,0},{11,1},{16,10},{17,11},{18,8},{19,9},{24,18},{2... | collective-permute-start | bytes 786440 | tf_op jit(solution)/shard_map/ppermute | solution.py:366
  95.8 18.2 %collective-permute-start.12 = (bf16[128,1024]{1,0:T(8,128)(2,1)}, bf16[128,1024]{1,0:T(8,128)(2,1)S(1)}, u32[]{:S(2)}, u32[]{:S(2)}) collective-permute-start(bf16[128,1024]{1,0:T(8,128)(2,1)} %get-tuple-element.31), channel_id=1, source_target_pairs={{8,1},{9,0},{10,3},{11,2},{16,9},{17,8},{18,11},{19,10},{24,17},{2... | collective-permute-start | bytes 786440 | tf_op jit(solution)/shard_map/ppermute | solution.py:366
  97.1 16.9 %collective-permute-start.13 = (bf16[128,1024]{1,0:T(8,128)(2,1)S(1)}, bf16[128,1024]{1,0:T(8,128)(2,1)S(1)}, u32[]{:S(2)}, u32[]{:S(2)}) collective-permute-start(bf16[128,1024]{1,0:T(8,128)(2,1)S(1)} %get-tuple-element.32), channel_id=1, source_target_pairs={{8,0},{9,1},{10,2},{11,3},{16,8},{17,9},{18,10},{19,11},{24,16},{2... | collective-permute-start | bytes 786440 | tf_op jit(solution)/shard_map/ppermute | solution.py:366
  102.9 11.2 %collective-permute-start.14 = (bf16[128,1024]{1,0:T(8,128)(2,1)S(1)}, bf16[128,1024]{1,0:T(8,128)(2,1)S(1)}, u32[]{:S(2)}, u32[]{:S(2)}) collective-permute-start(bf16[128,1024]{1,0:T(8,128)(2,1)S(1)} %collective-permute-done.10.refs_0_), channel_id=1, source_target_pairs={{8,11},{9,10},{10,9},{11,8},{12,15},{13,14},{14,13},{15,12}} | collective-permute-start | bytes 786440 | tf_op jit(solution)/shard_map/ppermute | solution.py:379

commit v4 on v3

--- a/solution.py
+++ b/solution.py
@@ -178,14 +178,7 @@
     )(pos, *pieces, *pieces, queries, segments, cosine, sine)
 
 
-def input_kernel(n, share, pos_ref, *refs):
-    part_refs, weight_ref = refs[:n], refs[n]
-    out_refs, kv_ref = refs[n + 1 : 2 * n + 1], refs[2 * n + 1]
-    weight_s, arrived, *sums = refs[2 * n + 2 :]
-    total = sums[0] if share > 1 else kv_ref
-    width = HEAD_WIDTH
-    kv_width = kv_ref.shape[1] // 2
-    piece_rows = out_refs[0].shape[0]
+def weight_copies(weight_ref, weight_s, arrived):
     blocks, block = weight_s.shape[:2]
     copies = [
         pltpu.make_async_copy(
@@ -195,15 +188,66 @@
     ]
     for copy in copies:
         copy.start()
+    return copies
+
+
+def head_columns(pos_ref, source, share, kv_width):
+    head = pos_ref[source] // share
+    return [
+        pl.ds(pl.multiple_of(side * kv_width + head * HEAD_WIDTH, HEAD_WIDTH), HEAD_WIDTH)
+        for side in range(2)
+    ]
+
+
+def product_with(pos_ref, sources, share, parts_s, block_ref):
+    kv_width = block_ref.shape[1] // 2
+    picked = [
+        block_ref[:, cols]
+        for source in sources
+        for cols in head_columns(pos_ref, source, share, kv_width)
+    ]
+    return dot(parts_s[...], jnp.concatenate(picked, 1), NT)
+
+
+def first_kernel(n, share, sources, pos_ref, *refs):
+    part_refs, weight_ref = refs[: len(sources)], refs[len(sources)]
+    out_ref, parts_s, weight_s, arrived = refs[len(sources) + 1 :]
+    copies = weight_copies(weight_ref, weight_s, arrived)
+    piece_rows = parts_s.shape[0] // n
+    wide = part_refs[0].shape[1]
+    block = weight_s.shape[1]
+    for i, part_ref in enumerate(part_refs):
+        for m in range(n):
+            rows = slice(m * piece_rows, (m + 1) * piece_rows)
+            parts_s[rows, i * wide : (i + 1) * wide] = part_ref[rows_at(pos_ref, m, piece_rows), :]
+    for b, copy in enumerate(copies):
+        copy.wait()
+        out_ref[:, b * block : (b + 1) * block] = product_with(
+            pos_ref, sources, share, parts_s, weight_s.at[b]
+        )
+
+
+def input_kernel(n, share, sources, pos_ref, *refs):
+    part_refs, weight_ref, first_ref = refs[:n], refs[n], refs[n + 1]
+    out_refs, kv_ref = refs[n + 2 : 2 * n + 2], refs[2 * n + 2]
+    parts_s, weight_s, arrived, *sums = refs[2 * n + 3 :]
+    copies = weight_copies(weight_ref, weight_s, arrived)
+    total = sums[0] if share > 1 else kv_ref
+    width = HEAD_WIDTH
+    kv_width = kv_ref.shape[1] // 2
+    piece_rows = out_refs[0].shape[0]
+    block = weight_s.shape[1]
     if share > 1:
         total[...] = jnp.zeros_like(total)
     for source in range(n):
-        head = pos_ref[source] // share
+        columns = head_columns(pos_ref, source, share, kv_width)
         for m in range(n):
             rows = slice(m * piece_rows, (m + 1) * piece_rows)
             part = part_refs[source][rows_at(pos_ref, m, piece_rows), :]
-            for side in range(2):
-                cols = pl.ds(pl.multiple_of(side * kv_width + head * width, width), width)
+            if source in sources:
+                at = sources.index(source) * 2 * width
+                parts_s[rows, at : at + 2 * width] = part
+            for side, cols in enumerate(columns):
                 own = part[:, side * width : (side + 1) * width]
                 if share > 1:
                     total[rows, cols] += own.astype(jnp.float32)
@@ -214,39 +258,68 @@
     for b, copy in enumerate(copies):
         copy.wait()
         cols = slice(b * block, (b + 1) * block)
-        product = dot(kv_ref[...], weight_s[b], NT).astype(jnp.bfloat16)
+        product = product_with(pos_ref, sources, share, parts_s, weight_s.at[b])
+        product = (product + first_ref[:, cols]).astype(jnp.bfloat16)
         for m in range(n):
             out_refs[m][:, cols] = product[m * piece_rows : (m + 1) * piece_rows]
 
 
-def input_gradient(pos, parts, weight, share):
+def first_products(pos, sources, parts, weight, n, share):
+    tokens, wide = parts[0].shape
+    rows, cols = weight.shape
+    block = min(FEATURE_BLOCK, rows)
+    vmem = pl.BlockSpec(memory_space=pltpu.VMEM)
+    return pl.pallas_call(
+        functools.partial(first_kernel, n, share, sources),
+        out_shape=jax.ShapeDtypeStruct((tokens, rows), jnp.float32),
+        in_specs=[pl.BlockSpec(memory_space=pltpu.SMEM)]
+        + [vmem] * len(parts)
+        + [pl.BlockSpec(memory_space=pltpu.HBM)],
+        out_specs=vmem,
+        scratch_shapes=[
+            pltpu.VMEM((tokens, len(parts) * wide), jnp.bfloat16),
+            pltpu.VMEM((rows // block, block, cols), jnp.bfloat16),
+            pltpu.SemaphoreType.DMA((rows // block,)),
+        ],
+        compiler_params=pltpu.CompilerParams(vmem_limit_bytes=VMEM_LIMIT),
+        cost_estimate=pl.CostEstimate(
+            flops=2 * tokens * rows * wide * len(parts),
+            bytes_accessed=2 * rows * cols + 4 * tokens * rows,
+            transcendentals=0,
+        ),
+        name="first_products",
+    )(pos, *parts, pltpu.with_memory_space_constraint(weight, pltpu.HBM))
+
+
+def input_gradient(pos, sources, parts, weight, first, share):
     n = len(parts)
-    tokens = parts[0].shape[0]
+    tokens, wide = parts[0].shape
     rows, cols = weight.shape
     bf16 = jnp.bfloat16
     block = min(FEATURE_BLOCK, rows)
     vmem = pl.BlockSpec(memory_space=pltpu.VMEM)
     out = pl.pallas_call(
-        functools.partial(input_kernel, n, share),
+        functools.partial(input_kernel, n, share, sources),
         out_shape=[jax.ShapeDtypeStruct((tokens // n, rows), bf16)] * n
         + [jax.ShapeDtypeStruct((tokens, cols), bf16)],
         in_specs=[pl.BlockSpec(memory_space=pltpu.SMEM)]
         + [vmem] * n
-        + [pl.BlockSpec(memory_space=pltpu.HBM)],
+        + [pl.BlockSpec(memory_space=pltpu.HBM), vmem],
         out_specs=[vmem] * (n + 1),
         scratch_shapes=[
+            pltpu.VMEM((tokens, len(sources) * wide), bf16),
             pltpu.VMEM((rows // block, block, cols), bf16),
             pltpu.SemaphoreType.DMA((rows // block,)),
         ]
         + ([pltpu.VMEM((tokens, cols), jnp.float32)] if share > 1 else []),
         compiler_params=pltpu.CompilerParams(vmem_limit_bytes=VMEM_LIMIT),
         cost_estimate=pl.CostEstimate(
-            flops=2 * tokens * rows * cols,
-            bytes_accessed=2 * (2 * tokens * cols + rows * cols + tokens * rows),
+            flops=2 * tokens * rows * wide * len(sources),
+            bytes_accessed=2 * (2 * tokens * cols + rows * cols + 3 * tokens * rows),
             transcendentals=0,
         ),
         name="input_gradient",
-    )(pos, *parts, pltpu.with_memory_space_constraint(weight, pltpu.HBM))
+    )(pos, *parts, pltpu.with_memory_space_constraint(weight, pltpu.HBM), first)
     return out[:n], out[n]
 
 
@@ -294,41 +367,49 @@
     )(pos, *pieces, kv_grad)
 
 
-def join_kernel(order, pos_ref, *refs):
-    out_ref = refs[-1]
-    n, cols = len(order), refs[0].shape[1]
-    for i, m in enumerate(order):
-        at = pl.ds(pl.multiple_of(pos_ref[m] * cols, cols), cols)
-        if i == 0 and len(refs) > n + 1:
-            relayed = pos_ref[n + 1] == 1
-
-            @pl.when(relayed)
+def join_kernel(order, relayed, begun, pos_ref, *refs):
+    count = len(order)
+    cols = refs[0].shape[1]
+    out_ref, done = refs[-2:]
+    at = [pl.ds(pl.multiple_of(pos_ref[m] * cols, cols), cols) for m in order]
+    for i in range(count):
+        if i == 0 and relayed:
+            taken = pos_ref[pos_ref.shape[0] - 1] == 1
+
+            @pl.when(taken)
             def _():
-                out_ref[:, at] = refs[n][...]
-
-            @pl.when(jnp.logical_not(relayed))
+                pltpu.make_async_copy(refs[count], out_ref.at[:, at[0]], done.at[0]).start()
+
+            @pl.when(jnp.logical_not(taken))
             def _():
-                out_ref[:, at] = refs[0][...]
+                pltpu.make_async_copy(refs[0], out_ref.at[:, at[0]], done.at[0]).start()
 
         else:
-            out_ref[:, at] = refs[i][...]
-
-
-def join_columns(pos, order, pieces):
+            pltpu.make_async_copy(refs[i], out_ref.at[:, at[i]], done.at[i]).start()
+    for i in range(count):
+        pltpu.make_async_copy(refs[i], out_ref.at[:, at[i]], done.at[i]).wait()
+
+
+def join_columns(pos, order, pieces, n, begun=None):
     rows, cols = pieces[0].shape
-    n = len(order)
     vmem = pl.BlockSpec(memory_space=pltpu.VMEM)
+    hbm = pl.BlockSpec(memory_space=pltpu.HBM)
+    started = begun is not None
     return pl.pallas_call(
-        functools.partial(join_kernel, order),
+        functools.partial(join_kernel, order, len(pieces) > len(order), started),
         out_shape=jax.ShapeDtypeStruct((rows, n * cols), pieces[0].dtype),
-        in_specs=[pl.BlockSpec(memory_space=pltpu.SMEM)] + [vmem] * len(pieces),
-        out_specs=vmem,
+        in_specs=[pl.BlockSpec(memory_space=pltpu.SMEM)]
+        + [vmem] * len(pieces)
+        + ([hbm] if started else []),
+        out_specs=hbm,
+        scratch_shapes=[pltpu.SemaphoreType.DMA((len(order),))],
+        input_output_aliases={1 + len(pieces): 0} if started else {},
         compiler_params=pltpu.CompilerParams(vmem_limit_bytes=VMEM_LIMIT),
         cost_estimate=pl.CostEstimate(
-            flops=0, bytes_accessed=4 * rows * n * cols, transcendentals=0
+            flops=0, bytes_accessed=4 * rows * len(order) * cols, transcendentals=0
         ),
         name="join_columns",
-    )(pos, *pieces)
+    )(pos, *pieces, *([begun] if started else []))
 
 
 def lay_out_kernel(in_ref, out_ref):
@@ -432,7 +513,7 @@
     x_sent[near] = swapped(x_out[near], near)
 
     dq, dkv = attention_backward(pos, pieces, queries[0, 0], segments, cosine, sine)
-    dkv = after(dkv, [x_sent[m] for m in [near, *middle]])
+    dkv = after(dkv, [x_sent[m] for m in [near, far]])
 
     parts = {0: dkv}
     bit = far
@@ -441,12 +522,15 @@
             held = after(parts[m], x_sent) if m else parts[m]
             parts[m | bit] = swapped(held, bit)
         bit //= 2
+    early = [0, far]
+    first = first_products(pos, early, [parts[m] for m in early], kv_weight[0], n, share)
     dq = after(dq, parts[far])
     dq = lax.all_to_all(dq.reshape(n, tokens // n, cols), "ctx", 0, 0, tiled=True)
     parts = [parts[m] for m in range(n)]
     x_pieces = [x_out[0], *(x_sent[m] for m in range(1, n))]
 
-    in_grads, kv_grad = input_gradient(pos, parts, kv_weight[0], share)
+    others = [m for m in range(n) if m not in early]
+    in_grads, kv_grad = input_gradient(pos, others, parts, kv_weight[0], first, share)
     order = [*masks, 0]
     in_sent = [to_section_before(in_grads[m], m) for m in order[1:]]
     if relay:
@@ -465,7 +549,9 @@
 
     query_grad = lay_out(dq)
     last = after(pos, (query_grad, weight_grad))
-    grad_prev = join_columns(last, order, in_sent)
+    split = n - 2
+    begun = join_columns(last, order[split:], in_sent[split:n], n)
+    grad_prev = join_columns(last, order[:split], in_sent[:split] + in_sent[n:], n, begun)
     return (grad_prev[None, None], query_grad[None, None], weight_grad[None])
 
 

time: 118 us -> 118 us (level)
  starting transfers between devices: 34.7 us -> 26.1 us
  waiting for transfers between devices: 53.5 us -> 59.4 us
  Pallas kernels: 21.1 us -> 23.8 us
    ppermute x10, starting transfers between devices: 24.7 us -> 16.8 us  [swapped(): return lax.ppermute(value, axis, [(i, i ^ mask) for i in range(size)])]
    ppermute x10, waiting for transfers between devices: 45.4 us -> 53.3 us  [swapped(): return lax.ppermute(value, axis, [(i, i ^ mask) for i in range(size)])]
    pallas_call x2 -> x4, Pallas kernels: 7.44 us -> 9.7 us  [the longest x1 3.54 us: input_gradient(): pl.pallas_call(functools.partial(input_kernel, n, share, sources), out_sh...]
    ppermute x3, waiting for transfers between devices: 3.68 us -> 1.65 us  [to_section_before(): return lax.ppermute(value, ('section', 'ctx'), pairs)]
  transfers between devices with their start and end apart: 16 -> 16, of which waited for: 8 -> 8; matrix products, arithmetic and copies ran while one was open for 3% -> 3% of each run, Pallas kernels for 17% -> 19%
where the time goes in v4:
time: 118 us; the launch traced here: 116 us
  waiting for transfers between devices  59.4 us (50%)
  starting transfers between devices  26.1 us (22%)
  Pallas kernels  23.8 us (20%)
  local copies, waits for them, and re-layouts  3.12 us (3%)
  other arithmetic  2.3 us (2%)
    ppermute x10, waiting for transfers between devices, swapped(): return lax.ppermute(value, axis, [(i, i ^ mask) for i in range(size)])  53.3 us
    ppermute x10, starting transfers between devices, swapped(): return lax.ppermute(value, axis, [(i, i ^ mask) for i in range(size)])  16.8 us
    pallas_call x1, Pallas kernels, attention_backward(): pl.pallas_call(functools.partial(attention_kernel, n), out_shape=[jax.Sha...  10.7 us
    ppermute x1, waiting for transfers between devices, relayed_section_before(): value = lax.ppermute(value, ('section', 'ctx'), first)  4.49 us
    ppermute x3, starting transfers between devices, to_section_before(): return lax.ppermute(value, ('section', 'ctx'), pairs)  3.88 us
    pallas_call x1, Pallas kernels, input_gradient(): pl.pallas_call(functools.partial(input_kernel, n, share, sources), out_sh...  3.54 us
    all_to_all x1, starting transfers between devices, on_device(): lax.all_to_all(dq.reshape(n, tokens // n, cols), 'ctx', 0, 0, tiled=True)  3.52 us
    pallas_call x1, Pallas kernels, first_products(): pl.pallas_call(functools.partial(first_kernel, n, share, sources), out_sh...  3.45 us
  transfers between devices with their start and end apart: 16, of which 8 were waited for; matrix products, arithmetic and copies ran while one was open for 3% of the time, Pallas kernels for 19%

profile of v4, /device:TPU:0, one launch (start us, length us, event | category | flops | bytes accessed | tf_op | source)
XLA Modules:
  0.0 115.7 jit_solution(162781052505398345)
XLA Ops:
  0.7 1.4 %dynamic-slice_bitcast_fusion.4 = (bf16[128,1024]{1,0:T(8,128)(2,1)S(1)}, bf16[128,1024]{1,0:T(8,128)(2,1)S(1)}, bf16[128,1024]{1,0:T(8,128)(2,1)S(1)}, bf16[128,1024]{1,0:T(8,128)(2,1)S(1)}) fusion(bf16[1,1,128,4096]{3,2,1,0:T(8,128)(2,1)} %param.10, s32[]{:T(128)S(6)} %select_n.44, s32[]{:T(128)S(6)} %select_n.40, s32[]{:T(128)S(6)} %select_n.38, ...), kind=kLoop, calls=%fused_computation.9 | loop fusion | bytes 2097168 | tf_op jit(solution)/shard_map/dynamic_slice | solution.py:486
  2.2 3.1 %collective-permute-start = (bf16[128,1280]{1,0:T(8,128)(2,1)S(1)}, bf16[128,1280]{1,0:T(8,128)(2,1)S(1)}, u32[]{:S(2)}, u32[]{:S(2)}) collective-permute-start(bf16[128,1280]{1,0:T(8,128)(2,1)S(1)} %pad_maximum_fusion.1), channel_id=1, source_target_pairs={{0,1},{1,0},{2,3},{3,2},{4,5},{5,4},{6,7},{7,6},{8,9},{9,8},{10,11... | collective-permute-start | bytes 983048 | tf_op jit(solution)/shard_map/ppermute | solution.py:439
  5.3 2.7 %collective-permute-start.1 = (bf16[128,1280]{1,0:T(8,128)(2,1)S(1)}, bf16[128,1280]{1,0:T(8,128)(2,1)S(1)}, u32[]{:S(2)}, u32[]{:S(2)}) collective-permute-start(bf16[128,1280]{1,0:T(8,128)(2,1)S(1)} %pad_maximum_fusion.2), channel_id=1, source_target_pairs={{0,2},{1,3},{2,0},{3,1},{4,6},{5,7},{6,4},{7,5},{8,10},{9,11},{10,... | collective-permute-start | bytes 983048 | tf_op jit(solution)/shard_map/ppermute | solution.py:439
  8.1 0.9 dynamic-slice_bitcast_fusion
  9.0 0.9 collective-permute-start.3
  9.9 10.2 %collective-permute-done.refs_1_.refs_5_ = bf16[128,1280]{1,0:T(8,128)(2,1)S(1)} collective-permute-done((bf16[128,1280]{1,0:T(8,128)(2,1)S(1)}, bf16[128,1280]{1,0:T(8,128)(2,1)S(1)}, u32[]{:S(2)}, u32[]{:S(2)}) %collective-permute-start) | collective-permute-done | bytes 327712 | tf_op jit(solution)/shard_map/ppermute | solution.py:439
  20.1 11.0 %collective-permute-done.1.refs_2_.refs_6_ = bf16[128,1280]{1,0:T(8,128)(2,1)S(1)} collective-permute-done((bf16[128,1280]{1,0:T(8,128)(2,1)S(1)}, bf16[128,1280]{1,0:T(8,128)(2,1)S(1)}, u32[]{:S(2)}, u32[]{:S(2)}) %collective-permute-start.1) | collective-permute-done | bytes 327712 | tf_op jit(solution)/shard_map/ppermute | solution.py:439
  31.0 7.2 %collective-permute-start.4 = (bf16[128,1024]{1,0:T(8,128)(2,1)}, bf16[128,1024]{1,0:T(8,128)(2,1)}, u32[]{:S(2)}, u32[]{:S(2)}) collective-permute-start(bf16[128,1024]{1,0:T(8,128)(2,1)} %get-tuple-element.20), channel_id=1, source_target_pairs={{0,2},{1,3},{2,0},{3,1},{4,6},{5,7},{6,4},{7,5},{8,10},{9,11},{10,... | collective-permute-start | bytes 786440 | tf_op jit(solution)/shard_map/ppermute | solution.py:439
  38.2 0.5 fusion.1
  38.9 1.3 %collective-permute-start.6 = (bf16[128,1024]{1,0:T(8,128)(2,1)S(1)}, bf16[128,1024]{1,0:T(8,128)(2,1)S(1)}, u32[]{:S(2)}, u32[]{:S(2)}) collective-permute-start(bf16[128,1024]{1,0:T(8,128)(2,1)S(1)} %get-tuple-element.23), channel_id=1, source_target_pairs={{0,3},{1,2},{2,1},{3,0},{4,7},{5,6},{6,5},{7,4},{8,11},{9,10},{10,... | collective-permute-start | bytes 786440 | tf_op jit(solution)/shard_map/ppermute | solution.py:439
  40.2 10.7 %attention_backward.1 = (bf16[512,1024]{1,0:T(8,128)(2,1)}, bf16[512,256]{1,0:T(8,128)(2,1)S(1)}) custom-call(s32[6]{0:T(128)S(1)} %stack.31.pos_ref, bf16[128,1280]{1,0:T(8,128)(2,1)S(1)} %pad_maximum_fusion.refs_0_.refs_4_, bf16[128,1280]{1,0:T(8,128)(2,1)S(1)} %collective-permute-done.refs_1_.refs_5_, ...), custom_call_target="tpu_custom_call" | custom-call | flops 2684354560 | bytes 3145728 | tf_op jit(solution)/shard_map/attention_backward/pallas_call | solution.py:138
  51.0 8.0 %collective-permute-done.4.refs_2_ = bf16[128,1024]{1,0:T(8,128)(2,1)} collective-permute-done((bf16[128,1024]{1,0:T(8,128)(2,1)}, bf16[128,1024]{1,0:T(8,128)(2,1)}, u32[]{:S(2)}, u32[]{:S(2)}) %collective-permute-start.4) | collective-permute-done | bytes 262176 | tf_op jit(solution)/shard_map/ppermute | solution.py:439
  59.0 0.7 copy-done.1
  59.7 12.0 %collective-permute-done.5.refs_1_.refs_2_ = bf16[512,256]{1,0:T(8,128)(2,1)S(1)} collective-permute-done((bf16[512,256]{1,0:T(8,128)(2,1)S(1)}, bf16[512,256]{1,0:T(8,128)(2,1)S(1)}, u32[]{:S(2)}, u32[]{:S(2)}) %collective-permute-start.5) | collective-permute-done | bytes 262176 | tf_op jit(solution)/shard_map/ppermute | solution.py:439
  71.7 3.5 %all-to-all-start = ((bf16[4,128,1024]{2,1,0:T(8,128)(2,1)}), bf16[4,128,1024]{2,1,0:T(8,128)(2,1)S(1)}, u32[]{:S(2)}, u32[]{:S(2)}) async-start(bf16[4,128,1024]{2,1,0:T(8,128)(2,1)} %bitcast.24), calls=%async_computation | async-start | bytes 2097152 | tf_op jit(solution)/shard_map/all_to_all | solution.py:528
  75.2 3.5 %first_products.1.refs_5_ = f32[512,1024]{1,0:T(8,128)S(1)} custom-call(s32[6]{0:T(128)S(1)} %stack.31.pos_ref, bf16[512,256]{1,0:T(8,128)(2,1)S(1)} %get-tuple-element.21.refs_0_, bf16[512,256]{1,0:T(8,128)(2,1)S(1)} %collective-permute-done.5.refs_1_.refs_2_, bf16[1024,1024]{1,0:T(8,128)(2,1)} %bitcast.46), custom_call_target="tpu_custom_call" | custom-call | flops 536870912 | bytes 4194304 | tf_op jit(solution)/shard_map/first_products/pallas_call | solution.py:272
  78.7 7.4 %collective-permute-done.8.refs_3_ = bf16[512,256]{1,0:T(8,128)(2,1)S(1)} collective-permute-done((bf16[512,256]{1,0:T(8,128)(2,1)S(1)}, bf16[512,256]{1,0:T(8,128)(2,1)S(1)}, u32[]{:S(2)}, u32[]{:S(2)}) %collective-permute-start.8) | collective-permute-done | bytes 262176 | tf_op jit(solution)/shard_map/ppermute | solution.py:439
  86.0 3.5 %input_gradient.1 = (bf16[128,1024]{1,0:T(8,128)(2,1)S(1)}, bf16[128,1024]{1,0:T(8,128)(2,1)S(1)}, bf16[128,1024]{1,0:T(8,128)(2,1)S(1)}, bf16[128,1024]{1,0:T(8,128)(2,1)S(1)}, bf16[512,1024]{1,0:T(8,128)(2,1)S(1)}) custom-call(s32[6]{0:T(128)S(1)} %stack.31.pos_ref, bf16[512,256]{1,0:T(8,128)(2,1)S(1)} %get-tuple-element.21.refs_0_, ...), custom_call_target="tpu_custom_call" | custom-call | flops 536870912 | bytes 7340032 | tf_op jit(solution)/shard_map/input_gradient/pallas_call | solution.py:301
  89.6 2.3 %weight_gradient.1 = (bf16[1024,512]{1,0:T(8,128)(2,1)S(1)}, f32[1024,512]{1,0:T(8,128)S(1)}) custom-call(s32[6]{0:T(128)S(1)} %stack.31.pos_ref, bf16[128,1024]{1,0:T(8,128)(2,1)S(1)} %get-tuple-element.34.refs_0_, bf16[128,1024]{1,0:T(8,128)(2,1)} %collective-permute-done.3.refs_1_, bf16[128,1024]{1,0:T(8,128)(2,1)} %collective-permute-done.4.refs_2_, ...), custom_call_target="tpu_custom_call" | custom-call | flops 1073741824 | bytes 6291456 | tf_op jit(solution)/shard_map/weight_gradient/pallas_call | solution.py:354
  91.9 1.6 %collective-permute-start.9 = (bf16[1024,512]{1,0:T(8,128)(2,1)S(1)}, bf16[1024,512]{1,0:T(8,128)(2,1)S(1)}, u32[]{:S(2)}, u32[]{:S(2)}) collective-permute-start(bf16[1024,512]{1,0:T(8,128)(2,1)S(1)} %get-tuple-element.27), channel_id=1, source_target_pairs={{0,4},{4,0},{1,5},{5,1},{2,6},{6,2},{3,7},{7,3},{8,12},{12,8},{9,1... | collective-permute-start | bytes 3145736 | tf_op jit(solution)/shard_map/ppermute | solution.py:439
  93.5 1.3 %collective-permute-start.10 = (bf16[128,1024]{1,0:T(8,128)(2,1)S(1)}, bf16[128,1024]{1,0:T(8,128)(2,1)S(1)}, u32[]{:S(2)}, u32[]{:S(2)}) collective-permute-start(bf16[128,1024]{1,0:T(8,128)(2,1)S(1)} %get-tuple-element.29), channel_id=1, source_target_pairs={{8,3},{9,2},{10,1},{11,0},{16,8},{17,9},{18,10},{19,11},{24,19},{2... | collective-permute-start | bytes 786440 | tf_op jit(solution)/shard_map/ppermute | solution.py:459
  94.8 1.3 %collective-permute-start.11 = (bf16[128,1024]{1,0:T(8,128)(2,1)S(1)}, bf16[128,1024]{1,0:T(8,128)(2,1)S(1)}, u32[]{:S(2)}, u32[]{:S(2)}) collective-permute-start(bf16[128,1024]{1,0:T(8,128)(2,1)S(1)} %get-tuple-element.30), channel_id=1, source_target_pairs={{8,2},{9,3},{10,0},{11,1},{16,10},{17,11},{18,8},{19,9},{24,18},{2... | collective-permute-start | bytes 786440 | tf_op jit(solution)/shard_map/ppermute | solution.py:447
  96.1 1.3 %collective-permute-start.13 = (bf16[128,1024]{1,0:T(8,128)(2,1)S(1)}, bf16[128,1024]{1,0:T(8,128)(2,1)S(1)}, u32[]{:S(2)}, u32[]{:S(2)}) collective-permute-start(bf16[128,1024]{1,0:T(8,128)(2,1)S(1)} %get-tuple-element.31), channel_id=1, source_target_pairs={{8,1},{9,0},{10,3},{11,2},{16,9},{17,8},{18,11},{19,10},{24,17},{2... | collective-permute-start | bytes 786440 | tf_op jit(solution)/shard_map/ppermute | solution.py:447
  97.4 1.3 %collective-permute-start.14 = (bf16[128,1024]{1,0:T(8,128)(2,1)S(1)}, bf16[128,1024]{1,0:T(8,128)(2,1)S(1)}, u32[]{:S(2)}, u32[]{:S(2)}) collective-permute-start(bf16[128,1024]{1,0:T(8,128)(2,1)S(1)} %get-tuple-element.32), channel_id=1, source_target_pairs={{8,0},{9,1},{10,2},{11,3},{16,8},{17,9},{18,10},{19,11},{24,16},{2... | collective-permute-start | bytes 786440 | tf_op jit(solution)/shard_map/ppermute | solution.py:447
  98.7 4.5 %collective-permute-done.10.refs_0_ = bf16[128,1024]{1,0:T(8,128)(2,1)S(1)} collective-permute-done((bf16[128,1024]{1,0:T(8,128)(2,1)S(1)}, bf16[128,1024]{1,0:T(8,128)(2,1)S(1)}, u32[]{:S(2)}, u32[]{:S(2)}) %collective-permute-start.10) | collective-permute-done | bytes 262176 | tf_op jit(solution)/shard_map/ppermute | solution.py:459
  103.2 0.7 collective-permute-start.12
  103.8 4.8 %collective-permute-done.9 = bf16[1024,512]{1,0:T(8,128)(2,1)S(1)} collective-permute-done((bf16[1024,512]{1,0:T(8,128)(2,1)S(1)}, bf16[1024,512]{1,0:T(8,128)(2,1)S(1)}, u32[]{:S(2)}, u32[]{:S(2)}) %collective-permute-start.9) | collective-permute-done | bytes 1048608 | tf_op jit(solution)/shard_map/ppermute | solution.py:439
  108.6 1.7 %add_multiply_fusion = f32[1024,512]{1,0:T(8,128)} fusion(f32[1024,512]{1,0:T(8,128)S(1)} %get-tuple-element.26, bf16[1024,512]{1,0:T(8,128)(2,1)S(1)} %collective-permute-done.9), kind=kLoop, calls=%fused_computation | loop fusion | flops 1572864 | bytes 5242880 | tf_op jit(solution)/shard_map/div | solution.py:545
  110.3 1.0 lay_out.1
  111.3 1.4 %join_columns.2.refs_3_ = bf16[128,4096]{1,0:T(8,128)(2,1)} custom-call(s32[6]{0:T(128)S(1)} %stack.31.pos_ref, bf16[128,1024]{1,0:T(8,128)(2,1)S(1)} %collective-permute-done.13.refs_0_, bf16[128,1024]{1,0:T(8,128)(2,1)S(1)} %collective-permute-done.14.refs_1_), custom_call_target="tpu_custom_call" | custom-call | bytes 1048576 | tf_op jit(solution)/shard_map/join_columns/pallas_call | solution.py:398
  112.7 1.6 %collective-permute-done.11.refs_1_ = bf16[128,1024]{1,0:T(8,128)(2,1)S(1)} collective-permute-done((bf16[128,1024]{1,0:T(8,128)(2,1)S(1)}, bf16[128,1024]{1,0:T(8,128)(2,1)S(1)}, u32[]{:S(2)}, u32[]{:S(2)}) %collective-permute-start.11) | collective-permute-done | bytes 262176 | tf_op jit(solution)/shard_map/ppermute | solution.py:447
  114.3 1.4 %join_columns.3 = bf16[128,4096]{1,0:T(8,128)(2,1)} custom-call(s32[6]{0:T(128)S(1)} %stack.31.pos_ref, bf16[128,1024]{1,0:T(8,128)(2,1)S(1)} %collective-permute-done.10.refs_0_, bf16[128,1024]{1,0:T(8,128)(2,1)S(1)} %collective-permute-done.11.refs_1_, bf16[128,1024]{1,0:T(8,128)(2,1)S(1)} %collective-permute-done.12.refs_2_, ...), custom_call_target="tpu_custom_call", output_to_operand_aliasing={{}: (4, {})} | custom-call | bytes 1048576 | tf_op jit(solution)/shard_map/join_columns/pallas_call | solution.py:398
  (36 shorter events, 0.4 us)
Async XLA Ops:
  0.6 1.4 %copy-start.5 = (bf16[1,1,128,512]{3,2,1,0:T(8,128)(2,1)S(1)}, bf16[1,1,128,512]{3,2,1,0:T(8,128)(2,1)}, u32[]{:S(2)}) copy-start(bf16[1,1,128,512]{3,2,1,0:T(8,128)(2,1)} %param.13) | copy-start | bytes 393220
  0.6 1.4 %copy-start.6 = (bf16[1,1,128,512]{3,2,1,0:T(8,128)(2,1)S(1)}, bf16[1,1,128,512]{3,2,1,0:T(8,128)(2,1)}, u32[]{:S(2)}) copy-start(bf16[1,1,128,512]{3,2,1,0:T(8,128)(2,1)} %param.12) | copy-start | bytes 393220
  0.7 7.4 %copy-start.4 = (bf16[1,1,128,4096]{3,2,1,0:T(8,128)(2,1)S(1)}, bf16[1,1,128,4096]{3,2,1,0:T(8,128)(2,1)}, u32[]{:S(2)}) copy-start(bf16[1,1,128,4096]{3,2,1,0:T(8,128)(2,1)} %param.9) | copy-start | bytes 3145732
  2.2 7.7 %copy-start.7 = (s32[1,512]{1,0:T(1,128)S(1)}, s32[1,512]{1,0:T(1,128)}, u32[]{:S(2)}) copy-start(s32[1,512]{1,0:T(1,128)} %param.16) | copy-start | bytes 6148
  2.2 36.0 %copy-start.8 = (f32[64]{0:T(128)S(1)}, f32[64]{0:T(128)}, u32[]{:S(2)}) copy-start(f32[64]{0:T(128)} %constant.91) | copy-start | bytes 772
  2.2 17.8 %collective-permute-start = (bf16[128,1280]{1,0:T(8,128)(2,1)S(1)}, bf16[128,1280]{1,0:T(8,128)(2,1)S(1)}, u32[]{:S(2)}, u32[]{:S(2)}) collective-permute-start(bf16[128,1280]{1,0:T(8,128)(2,1)S(1)} %pad_maximum_fusion.1), channel_id=1, source_target_pairs={{0,1},{1,0},{2,3},{3,2},{4,5},{5,4},{6,7},{7,6},{8,9},{9,8},{10,11... | collective-permute-start | bytes 983048 | tf_op jit(solution)/shard_map/ppermute | solution.py:439
  5.3 34.9 %copy-start = (bf16[1,1,512,1024]{3,2,1,0:T(8,128)(2,1)S(1)}, bf16[1,1,512,1024]{3,2,1,0:T(8,128)(2,1)}, u32[]{:S(2)}) copy-start(bf16[1,1,512,1024]{3,2,1,0:T(8,128)(2,1)} %param.11) | copy-start | bytes 3145732
  5.3 34.9 %copy-start.3 = (s32[1,512]{1,0:T(1,128)S(1)}, s32[1,512]{1,0:T(1,128)}, u32[]{:S(2)}) copy-start(s32[1,512]{1,0:T(1,128)} %refs_9_.1) | copy-start | bytes 6148
  5.3 25.7 %collective-permute-start.1 = (bf16[128,1280]{1,0:T(8,128)(2,1)S(1)}, bf16[128,1280]{1,0:T(8,128)(2,1)S(1)}, u32[]{:S(2)}, u32[]{:S(2)}) collective-permute-start(bf16[128,1280]{1,0:T(8,128)(2,1)S(1)} %pad_maximum_fusion.2), channel_id=1, source_target_pairs={{0,2},{1,3},{2,0},{3,1},{4,6},{5,7},{6,4},{7,5},{8,10},{9,11},{10,... | collective-permute-start | bytes 983048 | tf_op jit(solution)/shard_map/ppermute | solution.py:439
  8.0 23.0 %collective-permute-start.2 = (bf16[128,1280]{1,0:T(8,128)(2,1)S(1)}, bf16[128,1280]{1,0:T(8,128)(2,1)S(1)}, u32[]{:S(2)}, u32[]{:S(2)}) collective-permute-start(bf16[128,1280]{1,0:T(8,128)(2,1)S(1)} %pad_maximum_fusion.3), channel_id=1, source_target_pairs={{0,3},{1,2},{2,1},{3,0},{4,7},{5,6},{6,5},{7,4},{8,11},{9,10},{10,... | collective-permute-start | bytes 983048 | tf_op jit(solution)/shard_map/ppermute | solution.py:439
  9.0 42.0 %collective-permute-start.3 = (bf16[128,1024]{1,0:T(8,128)(2,1)}, bf16[128,1024]{1,0:T(8,128)(2,1)}, u32[]{:S(2)}, u32[]{:S(2)}) collective-permute-start(bf16[128,1024]{1,0:T(8,128)(2,1)} %get-tuple-element.35), channel_id=1, source_target_pairs={{0,1},{1,0},{2,3},{3,2},{4,5},{5,4},{6,7},{7,6},{8,9},{9,8},{10,11... | collective-permute-start | bytes 786440 | tf_op jit(solution)/shard_map/ppermute | solution.py:439
  31.0 27.9 %collective-permute-start.4 = (bf16[128,1024]{1,0:T(8,128)(2,1)}, bf16[128,1024]{1,0:T(8,128)(2,1)}, u32[]{:S(2)}, u32[]{:S(2)}) collective-permute-start(bf16[128,1024]{1,0:T(8,128)(2,1)} %get-tuple-element.20), channel_id=1, source_target_pairs={{0,2},{1,3},{2,0},{3,1},{4,6},{5,7},{6,4},{7,5},{8,10},{9,11},{10,... | collective-permute-start | bytes 786440 | tf_op jit(solution)/shard_map/ppermute | solution.py:439
  38.9 20.1 %collective-permute-start.6 = (bf16[128,1024]{1,0:T(8,128)(2,1)S(1)}, bf16[128,1024]{1,0:T(8,128)(2,1)S(1)}, u32[]{:S(2)}, u32[]{:S(2)}) collective-permute-start(bf16[128,1024]{1,0:T(8,128)(2,1)S(1)} %get-tuple-element.23), channel_id=1, source_target_pairs={{0,3},{1,2},{2,1},{3,0},{4,7},{5,6},{6,5},{7,4},{8,11},{9,10},{10,... | collective-permute-start | bytes 786440 | tf_op jit(solution)/shard_map/ppermute | solution.py:439
  59.0 12.7 %collective-permute-start.5 = (bf16[512,256]{1,0:T(8,128)(2,1)S(1)}, bf16[512,256]{1,0:T(8,128)(2,1)S(1)}, u32[]{:S(2)}, u32[]{:S(2)}) collective-permute-start(bf16[512,256]{1,0:T(8,128)(2,1)S(1)} %get-tuple-element.21.refs_0_), channel_id=1, source_target_pairs={{0,2},{1,3},{2,0},{3,1},{4,6},{5,7},{6,4},{7,5},{8,10},{9,11},{10,... | collective-permute-start | bytes 786440 | tf_op jit(solution)/shard_map/ppermute | solution.py:439
  59.0 19.7 %collective-permute-start.7 = (bf16[512,256]{1,0:T(8,128)(2,1)S(1)}, bf16[512,256]{1,0:T(8,128)(2,1)S(1)}, u32[]{:S(2)}, u32[]{:S(2)}) collective-permute-start(bf16[512,256]{1,0:T(8,128)(2,1)S(1)} %get-tuple-element.21.refs_0_), channel_id=1, source_target_pairs={{0,1},{1,0},{2,3},{3,2},{4,5},{5,4},{6,7},{7,6},{8,9},{9,8},{10,11... | collective-permute-start | bytes 786440 | tf_op jit(solution)/shard_map/ppermute | solution.py:439
  59.0 0.7 copy-start.1
  71.7 14.4 %collective-permute-start.8 = (bf16[512,256]{1,0:T(8,128)(2,1)S(1)}, bf16[512,256]{1,0:T(8,128)(2,1)S(1)}, u32[]{:S(2)}, u32[]{:S(2)}) collective-permute-start(bf16[512,256]{1,0:T(8,128)(2,1)S(1)} %collective-permute-done.5.refs_1_.refs_2_), channel_id=1, source_target_pairs={{0,1},{1,0},{2,3},{3,2},{4,5},{5,4},{6,7},{7,6},{8,9},{9,8},{10,11... | collective-permute-start | bytes 786440 | tf_op jit(solution)/shard_map/ppermute | solution.py:439
  71.7 38.6 %all-to-all-start = ((bf16[4,128,1024]{2,1,0:T(8,128)(2,1)}), bf16[4,128,1024]{2,1,0:T(8,128)(2,1)S(1)}, u32[]{:S(2)}, u32[]{:S(2)}) async-start(bf16[4,128,1024]{2,1,0:T(8,128)(2,1)} %bitcast.24), calls=%async_computation | async-start | bytes 2097152 | tf_op jit(solution)/shard_map/all_to_all | solution.py:528
  78.7 10.9 %copy-start.2 = (bf16[128,1024]{1,0:T(8,128)(2,1)S(1)}, bf16[128,1024]{1,0:T(8,128)(2,1)}, u32[]{:S(2)}) copy-start(bf16[128,1024]{1,0:T(8,128)(2,1)} %copy-done.1) | copy-start | bytes 786436
  91.9 16.7 %collective-permute-start.9 = (bf16[1024,512]{1,0:T(8,128)(2,1)S(1)}, bf16[1024,512]{1,0:T(8,128)(2,1)S(1)}, u32[]{:S(2)}, u32[]{:S(2)}) collective-permute-start(bf16[1024,512]{1,0:T(8,128)(2,1)S(1)} %get-tuple-element.27), channel_id=1, source_target_pairs={{0,4},{4,0},{1,5},{5,1},{2,6},{6,2},{3,7},{7,3},{8,12},{12,8},{9,1... | collective-permute-start | bytes 3145736 | tf_op jit(solution)/shard_map/ppermute | solution.py:439
  93.5 9.7 %collective-permute-start.10 = (bf16[128,1024]{1,0:T(8,128)(2,1)S(1)}, bf16[128,1024]{1,0:T(8,128)(2,1)S(1)}, u32[]{:S(2)}, u32[]{:S(2)}) collective-permute-start(bf16[128,1024]{1,0:T(8,128)(2,1)S(1)} %get-tuple-element.29), channel_id=1, source_target_pairs={{8,3},{9,2},{10,1},{11,0},{16,8},{17,9},{18,10},{19,11},{24,19},{2... | collective-permute-start | bytes 786440 | tf_op jit(solution)/shard_map/ppermute | solution.py:459
  94.8 19.5 %collective-permute-start.11 = (bf16[128,1024]{1,0:T(8,128)(2,1)S(1)}, bf16[128,1024]{1,0:T(8,128)(2,1)S(1)}, u32[]{:S(2)}, u32[]{:S(2)}) collective-permute-start(bf16[128,1024]{1,0:T(8,128)(2,1)S(1)} %get-tuple-element.30), channel_id=1, source_target_pairs={{8,2},{9,3},{10,0},{11,1},{16,10},{17,11},{18,8},{19,9},{24,18},{2... | collective-permute-start | bytes 786440 | tf_op jit(solution)/shard_map/ppermute | solution.py:447
  96.1 15.2 %collective-permute-start.13 = (bf16[128,1024]{1,0:T(8,128)(2,1)S(1)}, bf16[128,1024]{1,0:T(8,128)(2,1)S(1)}, u32[]{:S(2)}, u32[]{:S(2)}) collective-permute-start(bf16[128,1024]{1,0:T(8,128)(2,1)S(1)} %get-tuple-element.31), channel_id=1, source_target_pairs={{8,1},{9,0},{10,3},{11,2},{16,9},{17,8},{18,11},{19,10},{24,17},{2... | collective-permute-start | bytes 786440 | tf_op jit(solution)/shard_map/ppermute | solution.py:447
  97.4 13.9 %collective-permute-start.14 = (bf16[128,1024]{1,0:T(8,128)(2,1)S(1)}, bf16[128,1024]{1,0:T(8,128)(2,1)S(1)}, u32[]{:S(2)}, u32[]{:S(2)}) collective-permute-start(bf16[128,1024]{1,0:T(8,128)(2,1)S(1)} %get-tuple-element.32), channel_id=1, source_target_pairs={{8,0},{9,1},{10,2},{11,3},{16,8},{17,9},{18,10},{19,11},{24,16},{2... | collective-permute-start | bytes 786440 | tf_op jit(solution)/shard_map/ppermute | solution.py:447
  103.2 11.1 %collective-permute-start.12 = (bf16[128,1024]{1,0:T(8,128)(2,1)S(1)}, bf16[128,1024]{1,0:T(8,128)(2,1)S(1)}, u32[]{:S(2)}, u32[]{:S(2)}) collective-permute-start(bf16[128,1024]{1,0:T(8,128)(2,1)S(1)} %collective-permute-done.10.refs_0_), channel_id=1, source_target_pairs={{8,11},{9,10},{10,9},{11,8},{12,15},{13,14},{14,13},{15,12}} | collective-permute-start | bytes 786440 | tf_op jit(solution)/shard_map/ppermute | solution.py:460
